TPU v7x, 32 devices: a whole 2x2x4 slice. The times are simulated.
32 devices in a mesh: video: 2 (over x), seq: 8 (over z, y), head: 2 (over core).
Axes of the slice: x: 2, y: 2, z: 4, core: 2. Of those that a mesh axis runs over, the one named last changes fastest.
Arguments:
- query: bfloat16 [6144, 1536], P(('video', 'seq'), 'head'), parts along dimension 0, may hold values from -5 to 5
- key: bfloat16 [6144, 1536], P(('video', 'seq'), 'head'), parts along dimension 0, may hold values from -5 to 5
- value: bfloat16 [6144, 1536], P(('video', 'seq'), 'head'), parts along dimension 0, may hold values from -6 to 6
- stream: bfloat16 [6144, 3072], P(('video', 'seq'), 'head'), parts along dimension 0, may hold values from -12 to 12
- shift_mod: float32 [6144], P('video'), parts along dimension 0, may hold values from -3 to 3
- scale_mod: float32 [6144], P('video'), parts along dimension 0, may hold values from -3 to 3
- out_weight: bfloat16 [1536, 3072], P('seq', 'head'), may hold values from -0.5 to 0.5
Outputs:
- normed: bfloat16 [6144, 3072], P(('video', 'seq'), 'head'), parts along dimension 0
- stream_out: bfloat16 [6144, 3072], P(('video', 'seq'), 'head'), parts along dimension 0
There are 2 independent parts, one for each index of `video`. A program takes and returns all parts, laid end to end along the dimension named above; an argument that names none is the same for every part. Nothing has to cross between parts.
All inputs are finite; a program needn't handle non-finite values.
Results may differ from a plain program's by a relative error of at most 0.0051.
Values may be sent and summed in bfloat16 or wider, within the bound.
No kernel may reach another device: no remote copies, remote signals or barrier semaphores. Data moves between devices by JAX's collectives and lax.ppermute only.
A program may use at most 128 MiB of HBM per device.

v0:
```python
import functools
import math

import jax
import jax.numpy as jnp
from jax import lax
from jax.experimental import pallas as pl
from jax.experimental.pallas import tpu as pltpu
from jax.sharding import PartitionSpec as P


D = 3072
HD = 128
TILE = 128
HT = 4
EPS = 1e-06
EXP2_SCALE = math.log2(math.e) / math.sqrt(HD)
AWAY = -1e30


def shifted(value, axis, steps):
    count = lax.axis_size(axis)
    leading, last = (max(0, -steps), min(count, count - steps))
    return lax.ppermute(value, axis, [(source, source + steps) for source in range(leading, last)])


def attend_tile(query_tile, keys_all, values_all, visible):
    tile_rows, features = query_tile.shape
    heads_here = features // HD

    def one_head(head):
        head_query = lax.dynamic_slice_in_dim(query_tile, head * HD, HD, 1)
        head_key = lax.dynamic_slice_in_dim(keys_all, head * HD, HD, 1)
        head_value = lax.dynamic_slice_in_dim(values_all, head * HD, HD, 1)
        scores = jnp.einsum(
            "nd,md->nm", head_query, head_key, preferred_element_type=jnp.float32
        ) / math.sqrt(HD)
        scores = jnp.where(visible[None, :], scores, -jnp.inf)
        top = jnp.max(scores, axis=1, keepdims=True)
        expo = jnp.exp(scores - top)
        total = jnp.sum(expo, axis=1, keepdims=True)
        probs = expo.astype(jnp.bfloat16)
        weighted = jnp.dot(probs, head_value, preferred_element_type=jnp.float32)
        return (weighted / total).astype(jnp.bfloat16)

    per_head = lax.map(one_head, jnp.arange(heads_here, dtype=jnp.int32))
    return jnp.transpose(per_head, (1, 0, 2)).reshape(tile_rows, features)


def on_device_any(query, key, value, stream, shift_mod, scale_mod, out_weight):
    slab_rows = query.shape[0]
    width_tiles = slab_rows // TILE
    layers = lax.axis_size("seq") // HT
    position = lax.axis_index("seq")
    time_tile = position // HT
    height_tile = position % HT
    key_value = jnp.stack([key, value])
    vertical = {0: key_value}
    for offset in (HT, -HT):
        vertical[-offset // HT] = shifted(key_value, "seq", offset)
    column = jnp.stack([vertical[-1], vertical[0], vertical[1]])
    sideways = {0: column}
    for offset in (1, -1):
        sideways[-offset] = shifted(column, "seq", offset)
    neighbours = []
    for across in (-1, 0, 1):
        for upward in (-1, 0, 1):
            inside = (time_tile + across >= 0) & (time_tile + across < layers)
            inside = inside & (height_tile + upward >= 0) & (height_tile + upward < HT)
            neighbours.append((sideways[upward][across + 1], inside))
    results = []
    for tile_pos in range(width_tiles):
        lowest = max(tile_pos - 1, 0)
        highest = min(tile_pos + 1, width_tiles - 1)
        begin = lowest * TILE
        count = (highest - lowest + 1) * TILE
        keys_here = jnp.concatenate(
            [paired[0][begin : begin + count] for paired, inside in neighbours], 0
        )
        values_here = jnp.concatenate(
            [paired[1][begin : begin + count] for paired, inside in neighbours], 0
        )
        flags = jnp.concatenate(
            [jnp.broadcast_to(inside, (count,)) for paired, inside in neighbours]
        )
        query_tile = query[tile_pos * TILE : (tile_pos + 1) * TILE]
        results.append(attend_tile(query_tile, keys_here, values_here, flags))
    attended = jnp.concatenate(results, 0)
    width_cols = D // lax.axis_size("head")
    first_col = lax.axis_index("head") * width_cols
    weight_cols = lax.all_gather(out_weight, "seq", axis=0, tiled=True)
    weight_rows = lax.all_to_all(weight_cols, "head", split_axis=0, concat_axis=1, tiled=True)
    partial_value = jnp.dot(attended, weight_rows, preferred_element_type=jnp.float32)
    share = lax.psum_scatter(partial_value, "head", scatter_dimension=1, tiled=True)
    mixed = stream.astype(jnp.float32) + share
    totals, squares = lax.psum((jnp.sum(mixed, axis=1), jnp.sum(mixed * mixed, axis=1)), "head")
    mean = (totals / D)[:, None]
    var = (squares / D)[:, None] - mean * mean
    scale_part = lax.dynamic_slice_in_dim(scale_mod, first_col, width_cols, 0)
    shift_part = lax.dynamic_slice_in_dim(shift_mod, first_col, width_cols, 0)
    normed = ((mixed - mean) * lax.rsqrt(var + EPS) * (1.0 + scale_part) + shift_part).astype(
        jnp.bfloat16
    )
    return (normed, mixed.astype(jnp.bfloat16))


def attention_kernel(info, query, own, y_own, z_own, e_kv, y_oth, k_far, v_far, out):
    rows = query.shape[0]
    tiles = rows // TILE
    away = jnp.where(info[1] == 1, jnp.float32(0), jnp.float32(AWAY))
    parts = [(ref.at[0], ref.at[1], False) for ref in (own, y_own, e_kv, y_oth)]
    parts += [(z_own.at[0], z_own.at[1], True), (k_far, v_far, True)]
    for tile in range(tiles):
        begin = max(tile - 1, 0) * TILE
        end = (min(tile + 1, tiles - 1) + 1) * TILE
        q = query[tile * TILE : (tile + 1) * TILE, :]
        scores = []
        tops = []
        for keys, values, far in parts:
            s = lax.dot_general(
                q,
                keys[begin:end, :],
                (((1,), (1,)), ((), ())),
                preferred_element_type=jnp.float32,
            )
            scores.append(s)
            top = jnp.max(s, axis=1, keepdims=True)
            tops.append(top + away if far else top)
        top = functools.reduce(jnp.maximum, tops)
        total = jnp.zeros((TILE, 1), jnp.float32)
        acc = jnp.zeros((TILE, HD), jnp.float32)
        for s, (keys, values, far) in zip(scores, parts):
            p = jnp.exp2((s - (top - away if far else top)) * EXP2_SCALE)
            total = total + jnp.sum(p, axis=1, keepdims=True)
            acc = acc + jnp.dot(
                p.astype(jnp.bfloat16), values[begin:end, :], preferred_element_type=jnp.float32
            )
        out[tile * TILE : (tile + 1) * TILE, :] = (acc / total).astype(jnp.bfloat16)


def attention(info, query, own, parts):
    rows = query.shape[0]
    cols = parts[0].shape[2]
    heads = cols // HD
    if own:
        q_map = lambda j, info: (0, info[0] * heads + j)
    else:
        q_map = lambda j, info: (0, j)
    pair_spec = pl.BlockSpec((2, rows, HD), lambda j, info: (0, 0, j))
    one_spec = pl.BlockSpec((rows, HD), lambda j, info: (0, j))
    pairs = rows * 7 * TILE * 2 * heads
    return pl.pallas_call(
        attention_kernel,
        grid_spec=pltpu.PrefetchScalarGridSpec(
            num_scalar_prefetch=1,
            grid=(heads,),
            in_specs=[pl.BlockSpec((rows, HD), q_map)] + [pair_spec] * 5 + [one_spec] * 2,
            out_specs=pl.BlockSpec((rows, HD), lambda j, info: (0, j)),
        ),
        out_shape=jax.ShapeDtypeStruct((rows, cols), jnp.bfloat16),
        compiler_params=pltpu.CompilerParams(vmem_limit_bytes=12 << 20),
        cost_estimate=pl.CostEstimate(
            flops=pairs * HD * 4, transcendentals=pairs, bytes_accessed=rows * cols * 28
        ),
        name="attend",
    )(info, query, *parts)


def project_kernel(
    info, a_own, a_ret, x_own, x_ret, stream_hbm, *rest, places, count
):
    pieces = rest[:count]
    mixed, stream_out, stats, weight, left, stream, sems = rest[count:]
    core, par, pos, vid = info[0], info[1], info[2], info[3]
    copies = []
    for piece, (flip, half, size) in zip(pieces, places):
        other = pos ^ flip
        if half is None:
            row = other * size
        else:
            row = other * (2 * size) + (vid if half == 0 else 1 - vid) * size
        copy = pltpu.make_async_copy(
            piece, weight.at[pl.ds(pl.multiple_of(row, 32), size)], sems.at[len(copies)]
        )
        copy.start()
        copies.append(copy)
    copy = pltpu.make_async_copy(stream_hbm, stream, sems.at[len(copies)])
    copy.start()
    copies.append(copy)
    cols = a_own.shape[1]
    for ref, block in (
        (a_own, core * 2 + par),
        (a_ret, core * 2 + 1 - par),
        (x_own, (1 - core) * 2 + par),
        (x_ret, (1 - core) * 2 + 1 - par),
    ):
        left[:, pl.ds(pl.multiple_of(block * cols, HD), cols)] = ref[...]
    for copy in copies:
        copy.wait()
    rows, width = stream.shape
    step = 512
    total = jnp.zeros((rows, 1), jnp.float32)
    for first in range(0, width, step):
        got = jnp.dot(
            left[...], weight[:, first : first + step], preferred_element_type=jnp.float32
        ) + stream[:, first : first + step].astype(jnp.float32)
        mixed[:, first : first + step] = got
        stream_out[:, first : first + step] = got.astype(jnp.bfloat16)
        total = total + jnp.sum(got, axis=1, keepdims=True)
    mean = total * (1.0 / width)
    square = jnp.zeros((rows, 1), jnp.float32)
    for first in range(0, width, step):
        off = mixed[:, first : first + step] - mean
        square = square + jnp.sum(off * off, axis=1, keepdims=True)
    lane = lax.broadcasted_iota(jnp.int32, stats.shape, 1)
    stats[...] = jnp.where(lane == 0, mean, square)


def project(info, blocks, stream, pieces, places):
    rows, width = stream.shape
    depth = 4 * blocks[0].shape[1]
    copies = len(places)
    vmem = pl.BlockSpec(memory_space=pltpu.VMEM)
    return pl.pallas_call(
        functools.partial(project_kernel, places=places, count=len(pieces)),
        in_specs=[pl.BlockSpec(memory_space=pltpu.SMEM)]
        + [vmem] * 4
        + [pl.BlockSpec(memory_space=pltpu.HBM)] * (1 + len(pieces)),
        out_specs=[vmem] * 3,
        out_shape=[
            jax.ShapeDtypeStruct((rows, width), jnp.float32),
            jax.ShapeDtypeStruct((rows, width), jnp.bfloat16),
            jax.ShapeDtypeStruct((rows, HD), jnp.float32),
        ],
        scratch_shapes=[
            pltpu.VMEM((depth, width), jnp.bfloat16),
            pltpu.VMEM((rows, depth), jnp.bfloat16),
            pltpu.VMEM((rows, width), jnp.bfloat16),
            pltpu.SemaphoreType.DMA((copies + 1,)),
        ],
        compiler_params=pltpu.CompilerParams(vmem_limit_bytes=20 << 20),
        cost_estimate=pl.CostEstimate(
            flops=2 * rows * depth * width,
            transcendentals=0,
            bytes_accessed=depth * width * 2 + rows * width * 8,
        ),
        name="project",
    )(info, *blocks, stream, *pieces)


def norm_kernel(info, mixed, mine, other, scale, shift, out, *, half):
    m0, m1 = mine[:, 0:1], other[:, 0:1]
    q0, q1 = mine[:, 1:2], other[:, 1:2]
    mean = 0.5 * (m0 + m1)
    gap = m0 - m1
    var = (q0 + q1 + gap * gap * (0.5 * half)) * (0.5 / half)
    rate = lax.rsqrt(var + EPS)
    out[...] = ((mixed[...] - mean) * rate * (1.0 + scale[...]) + shift[...]).astype(jnp.bfloat16)


def normalize(info, mixed, mine, other, scale_mod, shift_mod):
    rows, width = mixed.shape
    step = TILE
    row_block = pl.BlockSpec((step, width), lambda i, info: (i, 0))
    stat_block = pl.BlockSpec((step, HD), lambda i, info: (i, 0))
    mod_block = pl.BlockSpec((1, width), lambda i, info: (0, info[0]))
    return pl.pallas_call(
        functools.partial(norm_kernel, half=float(width)),
        grid_spec=pltpu.PrefetchScalarGridSpec(
            num_scalar_prefetch=1,
            grid=(rows // step,),
            in_specs=[row_block, stat_block, stat_block, mod_block, mod_block],
            out_specs=row_block,
        ),
        out_shape=jax.ShapeDtypeStruct((rows, width), jnp.bfloat16),
        compiler_params=pltpu.CompilerParams(vmem_limit_bytes=12 << 20),
        cost_estimate=pl.CostEstimate(
            flops=6 * rows * width, transcendentals=rows, bytes_accessed=rows * width * 6
        ),
        name="normalize",
    )(info, mixed, mine, other, scale_mod[None, :], shift_mod[None, :])


def after(value, *done):
    return lax.optimization_barrier((value,) + done)[0]


def on_device_pair(query, key, value, stream, shift_mod, scale_mod, out_weight):
    count = lax.axis_size("seq")
    position = lax.axis_index("seq")
    core = lax.axis_index("head")
    vid = lax.axis_index("video")
    par = position // HT
    height = position % HT
    relayed = jnp.where((height == 1) | (height == 2), 1, 0)
    half_cols = query.shape[1] // 2

    def flip(x, mask):
        return lax.ppermute(x, "seq", [(i, i ^ mask) for i in range(count)])

    def swap(x, axis):
        return lax.ppermute(x, axis, [(0, 1), (1, 0)])

    def some(x, mask, sources):
        pairs = [(i, i ^ mask) for i in range(count) if i % HT in sources]
        return lax.ppermute(x, "seq", pairs)

    def heads(x, which):
        return lax.dynamic_slice_in_dim(x, which * half_cols, half_cols, 1)

    give = jnp.stack([heads(key, 1 - par), heads(value, 1 - par)])
    give_q = heads(query, 1 - par)
    own = jnp.stack([heads(key, par), heads(value, par)])
    rows_half = out_weight.shape[0] // 2
    w_own = lax.dynamic_slice_in_dim(out_weight, vid * rows_half, rows_half, 0)

    e_kv = flip(give, HT)
    y_own = flip(own, 1)
    w_z1 = flip(w_own, 2)
    z_own = some(y_own, 2, (0, 3))
    w_ya = flip(after(w_own, y_own), 1)
    w_yb = flip(after(w_z1, y_own), 1)
    w_xa = swap(w_z1, "video")
    w_t = flip(after(w_own, e_kv), HT)
    y_oth = flip(e_kv, 1)
    v_z = some(e_kv[1], 2, (1, 2))
    w_xb = swap(w_ya, "video")
    w_xc = swap(w_yb, "video")
    e_q = flip(after(give_q, w_t), HT)
    k_far = some(y_oth[0], 2, (0, 3))
    v_far = some(v_z, 1, (0, 3))
    w_yc = flip(w_t, 1)
    w_z2 = flip(w_t, 2)
    w_xd = swap(w_t, "video")
    w_yd = flip(w_z2, 1)
    w_xe = swap(w_z2, "video")
    w_xf = swap(w_yc, "video")
    w_xg = swap(w_yd, "video")

    info = jnp.stack([par, relayed]).astype(jnp.int32)
    parts = (own, y_own, z_own, e_kv, y_oth, k_far, v_far)
    out_other = attention(info, e_q, False, parts)
    a_ret = flip(out_other, HT)
    a_own = attention(info, query, True, parts)
    x_own = swap(a_own, "head")
    x_ret = swap(a_ret, "head")

    n = rows_half
    here = (w_z1, w_ya, w_yb, w_t, w_z2, w_yc, w_yd)
    across = (w_xa, w_xb, w_xc, w_xd, w_xe, w_xf, w_xg)
    flips = (2, 1, 3, 4, 6, 5, 7)
    pieces = (out_weight,) + here + across
    places = ((0, None, 2 * n),)
    places += tuple((mask, half, n) for half in (0, 1) for mask in flips)
    where = jnp.stack([core, par, position, vid]).astype(jnp.int32)
    mixed, stream_out, stats = project(
        where, (a_own, a_ret, x_own, x_ret), stream, pieces, places
    )
    other = swap(stats, "head")
    normed = normalize(where, mixed, stats, other, scale_mod, shift_mod)
    return (normed, stream_out)


PAIR = {"video": 2, "seq": 2 * HT, "head": 2}


def on_device(query, *rest):
    sizes = {axis: lax.axis_size(axis) for axis in PAIR}
    if sizes == PAIR:
        return on_device_pair(query, *rest)
    return on_device_any(query, *rest)


def solution(mesh):
    return jax.shard_map(
        on_device,
        mesh=mesh,
        in_specs=(
            P(("video", "seq"), "head"),
            P(("video", "seq"), "head"),
            P(("video", "seq"), "head"),
            P(("video", "seq"), "head"),
            P("video"),
            P("video"),
            P("seq", "head"),
        ),
        out_specs=(P(("video", "seq"), "head"), P(("video", "seq"), "head")),
        check_vma=False,
    )
```

profile of v0, /device:TPU:0, one launch (start us, length us, event | category | flops | bytes accessed | tf_op | source)
XLA Modules:
  0.0 131.2 jit_solution(513435185123405489)
XLA Ops:
  0.7 1.4 %dynamic-slice_bitcast_fusion = (bf16[1,384,384]{2,1,0:T(8,128)(2,1)S(1)}, bf16[1,384,384]{2,1,0:T(8,128)(2,1)S(1)}, bf16[1,384,384]{2,1,0:T(8,128)(2,1)S(1)}, bf16[1,384,384]{2,1,0:T(8,128)(2,1)S(1)}) fusion(bf16[384,768]{1,0:T(8,128)(2,1)} %param.9, s32[]{:T(128)S(6)} %select_n.31, s32[]{:T(128)S(6)} %select_n.30, bf16[384,768]{1,0:T(8,128)(2,1)} %param.8), kind=kLoop, calls=%fused_computation.4 | loop fusion | bytes 2359304 | tf_op jit(solution)/shard_map/stack | solution.py:311
  2.9 4.1 %collective-permute-start.2 = (bf16[2,384,384]{2,1,0:T(8,128)(2,1)}, bf16[2,384,384]{2,1,0:T(8,128)(2,1)S(1)}, u32[]{:S(2)}, u32[]{:S(2)}) collective-permute-start(bf16[2,384,384]{2,1,0:T(8,128)(2,1)} %pad_maximum_fusion.1), channel_id=1, source_target_pairs={{0,8},{2,10},{4,12},{6,14},{8,0},{10,2},{12,4},{14,6},{1,9},{3,11}... | collective-permute-start | bytes 1769480 | tf_op jit(solution)/shard_map/ppermute | solution.py:299
  7.1 1.6 %collective-permute-start = (bf16[2,384,384]{2,1,0:T(8,128)(2,1)S(1)}, bf16[2,384,384]{2,1,0:T(8,128)(2,1)S(1)}, u32[]{:S(2)}, u32[]{:S(2)}) collective-permute-start(bf16[2,384,384]{2,1,0:T(8,128)(2,1)S(1)} %pad_maximum_fusion.own), channel_id=1, source_target_pairs={{0,2},{2,0},{4,6},{6,4},{8,10},{10,8},{12,14},{14,12},{1,3},{3,1},... | collective-permute-start | bytes 1769480 | tf_op jit(solution)/shard_map/ppermute | solution.py:299
  8.6 24.5 %collective-permute-done.2.e_kv = bf16[2,384,384]{2,1,0:T(8,128)(2,1)S(1)} collective-permute-done((bf16[2,384,384]{2,1,0:T(8,128)(2,1)}, bf16[2,384,384]{2,1,0:T(8,128)(2,1)S(1)}, u32[]{:S(2)}, u32[]{:S(2)}) %collective-permute-start.2) | collective-permute-done | bytes 589856 | tf_op jit(solution)/shard_map/ppermute | solution.py:299
  33.2 1.6 %collective-permute-start.3 = (bf16[2,384,384]{2,1,0:T(8,128)(2,1)S(1)}, bf16[2,384,384]{2,1,0:T(8,128)(2,1)S(1)}, u32[]{:S(2)}, u32[]{:S(2)}) collective-permute-start(bf16[2,384,384]{2,1,0:T(8,128)(2,1)S(1)} %collective-permute-done.2.e_kv), channel_id=1, source_target_pairs={{0,2},{2,0},{4,6},{6,4},{8,10},{10,8},{12,14},{14,12},{1,3},{3,1},... | collective-permute-start | bytes 1769480 | tf_op jit(solution)/shard_map/ppermute | solution.py:299
  35.6 3.3 %collective-permute-start.7 = (bf16[96,1536]{1,0:T(8,128)(2,1)S(1)}, bf16[96,1536]{1,0:T(8,128)(2,1)}, u32[]{:S(2)}, u32[]{:S(2)}) collective-permute-start(bf16[96,1536]{1,0:T(8,128)(2,1)S(1)} %constant_dynamic-slice_fusion), channel_id=1, source_target_pairs={{0,8},{2,10},{4,12},{6,14},{8,0},{10,2},{12,4},{14,6},{1,9},{3,11}... | collective-permute-start | bytes 884744 | tf_op jit(solution)/shard_map/ppermute | solution.py:299
  38.9 1.3 collective-permute-start.5
  40.2 4.6 %collective-permute-start.1 = (bf16[2,384,384]{2,1,0:T(8,128)(2,1)S(1)}, bf16[2,384,384]{2,1,0:T(8,128)(2,1)S(1)}, u32[]{:S(2)}, u32[]{:S(2)}) collective-permute-start(bf16[2,384,384]{2,1,0:T(8,128)(2,1)S(1)} %collective-permute-done.y_own), channel_id=1, source_target_pairs={{0,4},{6,2},{8,12},{14,10},{1,5},{7,3},{9,13},{15,11},{16,20},{22,... | collective-permute-start | bytes 1769480 | tf_op jit(solution)/shard_map/ppermute | solution.py:306
  44.8 6.1 %collective-permute-done.12.rest_1_ = bf16[96,1536]{1,0:T(8,128)(2,1)} collective-permute-done((bf16[96,1536]{1,0:T(8,128)(2,1)S(1)}, bf16[96,1536]{1,0:T(8,128)(2,1)}, u32[]{:S(2)}, u32[]{:S(2)}) %collective-permute-start.12) | collective-permute-done | bytes 294944 | tf_op jit(solution)/shard_map/ppermute | solution.py:299
  52.1 1.6 %collective-permute-start.14 = (bf16[96,1536]{1,0:T(8,128)(2,1)}, bf16[96,1536]{1,0:T(8,128)(2,1)S(1)}, u32[]{:S(2)}, u32[]{:S(2)}) collective-permute-start(bf16[96,1536]{1,0:T(8,128)(2,1)} %collective-permute-done.12.rest_1_), channel_id=1, source_target_pairs={{0,2},{2,0},{4,6},{6,4},{8,10},{10,8},{12,14},{14,12},{1,3},{3,1},... | collective-permute-start | bytes 884744 | tf_op jit(solution)/shard_map/ppermute | solution.py:299
  53.7 1.4 %collective-permute-done.5 = bf16[384,384]{1,0:T(8,128)(2,1)S(1)} collective-permute-done((bf16[384,384]{1,0:T(8,128)(2,1)S(1)}, bf16[384,384]{1,0:T(8,128)(2,1)S(1)}, u32[]{:S(2)}, u32[]{:S(2)}) %collective-permute-start.5) | collective-permute-done | bytes 294944 | tf_op jit(solution)/shard_map/ppermute | solution.py:306
  55.1 3.6 %collective-permute-start.8 = (bf16[384,384]{1,0:T(8,128)(2,1)}, bf16[384,384]{1,0:T(8,128)(2,1)}, u32[]{:S(2)}, u32[]{:S(2)}) collective-permute-start(bf16[384,384]{1,0:T(8,128)(2,1)} %constant_dynamic-slice_fusion.1), channel_id=1, source_target_pairs={{0,8},{2,10},{4,12},{6,14},{8,0},{10,2},{12,4},{14,6},{1,9},{3,11}... | collective-permute-start | bytes 884744 | tf_op jit(solution)/shard_map/ppermute | solution.py:299
  58.7 1.4 %collective-permute-start.6 = (bf16[384,384]{1,0:T(8,128)(2,1)S(1)}, bf16[384,384]{1,0:T(8,128)(2,1)S(1)}, u32[]{:S(2)}, u32[]{:S(2)}) collective-permute-start(bf16[384,384]{1,0:T(8,128)(2,1)S(1)} %collective-permute-done.5), channel_id=1, source_target_pairs={{0,2},{6,4},{8,10},{14,12},{1,3},{7,5},{9,11},{15,13},{16,18},{22,... | collective-permute-start | bytes 884744 | tf_op jit(solution)/shard_map/ppermute | solution.py:306
  60.9 2.0 %collective-permute-start.4 = (bf16[384,384]{1,0:T(8,128)(2,1)}, bf16[384,384]{1,0:T(8,128)(2,1)}, u32[]{:S(2)}, u32[]{:S(2)}) collective-permute-start(bf16[384,384]{1,0:T(8,128)(2,1)} %slice_bitcast_fusion.1), channel_id=1, source_target_pairs={{0,4},{6,2},{8,12},{14,10},{1,5},{7,3},{9,13},{15,11},{16,20},{22,... | collective-permute-start | bytes 884744 | tf_op jit(solution)/shard_map/ppermute | solution.py:306
  62.9 1.5 %collective-permute-start.18 = (bf16[96,1536]{1,0:T(8,128)(2,1)}, bf16[96,1536]{1,0:T(8,128)(2,1)}, u32[]{:S(2)}, u32[]{:S(2)}) collective-permute-start(bf16[96,1536]{1,0:T(8,128)(2,1)} %collective-permute-done.12.rest_1_), channel_id=1, source_target_pairs={{0,16},{16,0},{1,17},{17,1},{2,18},{18,2},{3,19},{19,3},{4,20},{20... | collective-permute-start | bytes 884744 | tf_op jit(solution)/shard_map/ppermute | solution.py:302
  64.4 2.2 %collective-permute-start.15 = (bf16[96,1536]{1,0:T(8,128)(2,1)}, bf16[96,1536]{1,0:T(8,128)(2,1)}, u32[]{:S(2)}, u32[]{:S(2)}) collective-permute-start(bf16[96,1536]{1,0:T(8,128)(2,1)} %collective-permute-done.7.rest_4_), channel_id=1, source_target_pairs={{0,4},{2,6},{4,0},{6,2},{8,12},{10,14},{12,8},{14,10},{1,5},{3,7},... | collective-permute-start | bytes 884744 | tf_op jit(solution)/shard_map/ppermute | solution.py:299
  68.5 2.3 %collective-permute-done.8.query = bf16[384,384]{1,0:T(8,128)(2,1)} collective-permute-done((bf16[384,384]{1,0:T(8,128)(2,1)}, bf16[384,384]{1,0:T(8,128)(2,1)}, u32[]{:S(2)}, u32[]{:S(2)}) %collective-permute-start.8) | collective-permute-done | bytes 294944 | tf_op jit(solution)/shard_map/ppermute | solution.py:299
  70.8 2.0 %collective-permute-start.16 = (bf16[96,1536]{1,0:T(8,128)(2,1)}, bf16[96,1536]{1,0:T(8,128)(2,1)}, u32[]{:S(2)}, u32[]{:S(2)}) collective-permute-start(bf16[96,1536]{1,0:T(8,128)(2,1)} %collective-permute-done.7.rest_4_), channel_id=1, source_target_pairs={{0,2},{2,0},{4,6},{6,4},{8,10},{10,8},{12,14},{14,12},{1,3},{3,1},... | collective-permute-start | bytes 884744 | tf_op jit(solution)/shard_map/ppermute | solution.py:299
  72.8 2.0 %collective-permute-done.4.k_far = bf16[384,384]{1,0:T(8,128)(2,1)} collective-permute-done((bf16[384,384]{1,0:T(8,128)(2,1)}, bf16[384,384]{1,0:T(8,128)(2,1)}, u32[]{:S(2)}, u32[]{:S(2)}) %collective-permute-start.4) | collective-permute-done | bytes 294944 | tf_op jit(solution)/shard_map/ppermute | solution.py:306
  74.8 1.5 %collective-permute-start.20 = (bf16[96,1536]{1,0:T(8,128)(2,1)}, bf16[96,1536]{1,0:T(8,128)(2,1)S(1)}, u32[]{:S(2)}, u32[]{:S(2)}) collective-permute-start(bf16[96,1536]{1,0:T(8,128)(2,1)} %copy-done.6), channel_id=1, source_target_pairs={{0,16},{16,0},{1,17},{17,1},{2,18},{18,2},{3,19},{19,3},{4,20},{20... | collective-permute-start | bytes 884744 | tf_op jit(solution)/shard_map/ppermute | solution.py:302
  77.2 6.7 %attend.3 = bf16[384,384]{1,0:T(8,128)(2,1)S(1)} custom-call(s32[2]{0:T(128)S(1)} %pad_add_fusion.1.info, bf16[384,384]{1,0:T(8,128)(2,1)} %collective-permute-done.8.query, bf16[2,384,384]{2,1,0:T(8,128)(2,1)S(1)} %pad_maximum_fusion.own, bf16[2,384,384]{2,1,0:T(8,128)(2,1)S(1)} %collective-permute-done.y_own, ...), custom_call_target="tpu_custom_call" | custom-call | flops 1056964608 | bytes 4128768 | tf_op jit(solution)/shard_map/attend/pallas_call | solution.py:152
  84.6 2.1 %collective-permute-start.17 = (bf16[96,1536]{1,0:T(8,128)(2,1)}, bf16[96,1536]{1,0:T(8,128)(2,1)}, u32[]{:S(2)}, u32[]{:S(2)}) collective-permute-start(bf16[96,1536]{1,0:T(8,128)(2,1)} %collective-permute-done.15.rest_5_), channel_id=1, source_target_pairs={{0,2},{2,0},{4,6},{6,4},{8,10},{10,8},{12,14},{14,12},{1,3},{3,1},... | collective-permute-start | bytes 884744 | tf_op jit(solution)/shard_map/ppermute | solution.py:299
  86.7 2.1 %collective-permute-start.9 = (bf16[384,384]{1,0:T(8,128)(2,1)S(1)}, bf16[384,384]{1,0:T(8,128)(2,1)}, u32[]{:S(2)}, u32[]{:S(2)}) collective-permute-start(bf16[384,384]{1,0:T(8,128)(2,1)S(1)} %attend.3), channel_id=1, source_target_pairs={{0,8},{2,10},{4,12},{6,14},{8,0},{10,2},{12,4},{14,6},{1,9},{3,11}... | collective-permute-start | bytes 884744 | tf_op jit(solution)/shard_map/ppermute | solution.py:299
  88.8 7.4 %attend.2.a_own = bf16[384,384]{1,0:T(8,128)(2,1)} custom-call(s32[2]{0:T(128)S(1)} %pad_add_fusion.1.info, bf16[384,768]{1,0:T(8,128)(2,1)S(1)} %copy-done, bf16[2,384,384]{2,1,0:T(8,128)(2,1)S(1)} %pad_maximum_fusion.own, bf16[2,384,384]{2,1,0:T(8,128)(2,1)S(1)} %collective-permute-done.y_own, bf16[2,384,384]{2,1,0:T(8,128)(2,1)S(1)} %collective-permute-done.1.z_own, ...), custom_call_target="tpu_custom_call" | custom-call | flops 1056964608 | bytes 4128768 | tf_op jit(solution)/shard_map/attend/pallas_call | solution.py:152
  96.9 1.5 %collective-permute-start.22 = (bf16[96,1536]{1,0:T(8,128)(2,1)}, bf16[96,1536]{1,0:T(8,128)(2,1)S(1)}, u32[]{:S(2)}, u32[]{:S(2)}) collective-permute-start(bf16[96,1536]{1,0:T(8,128)(2,1)} %collective-permute-done.15.rest_5_), channel_id=1, source_target_pairs={{0,16},{16,0},{1,17},{17,1},{2,18},{18,2},{3,19},{19,3},{4,20},{20... | collective-permute-start | bytes 884744 | tf_op jit(solution)/shard_map/ppermute | solution.py:302
  99.7 1.5 %collective-permute-start.24 = (bf16[96,1536]{1,0:T(8,128)(2,1)}, bf16[96,1536]{1,0:T(8,128)(2,1)S(1)}, u32[]{:S(2)}, u32[]{:S(2)}) collective-permute-start(bf16[96,1536]{1,0:T(8,128)(2,1)} %collective-permute-done.17.rest_7_), channel_id=1, source_target_pairs={{0,16},{16,0},{1,17},{17,1},{2,18},{18,2},{3,19},{19,3},{4,20},{20... | collective-permute-start | bytes 884744 | tf_op jit(solution)/shard_map/ppermute | solution.py:302
  101.5 11.1 %collective-permute-done.23.rest_13_ = bf16[96,1536]{1,0:T(8,128)(2,1)S(1)} collective-permute-done((bf16[96,1536]{1,0:T(8,128)(2,1)}, bf16[96,1536]{1,0:T(8,128)(2,1)S(1)}, u32[]{:S(2)}, u32[]{:S(2)}) %collective-permute-start.23) | collective-permute-done | bytes 294944 | tf_op jit(solution)/shard_map/ppermute | solution.py:302
  112.6 3.2 %collective-permute-done.24.rest_14_ = bf16[96,1536]{1,0:T(8,128)(2,1)S(1)} collective-permute-done((bf16[96,1536]{1,0:T(8,128)(2,1)}, bf16[96,1536]{1,0:T(8,128)(2,1)S(1)}, u32[]{:S(2)}, u32[]{:S(2)}) %collective-permute-start.24) | collective-permute-done | bytes 294944 | tf_op jit(solution)/shard_map/ppermute | solution.py:302
  116.9 1.3 copy-done.5
  121.0 6.0 %project.1 = (f32[384,1536]{1,0:T(8,128)S(1)}, bf16[384,1536]{1,0:T(8,128)(2,1)}, f32[384,128]{1,0:T(8,128)S(1)}) custom-call(s32[4]{0:T(128)S(1)} %pad_add_fusion.info, bf16[384,384]{1,0:T(8,128)(2,1)} %attend.2.a_own, bf16[384,384]{1,0:T(8,128)(2,1)} %collective-permute-done.9.a_ret, bf16[384,384]{1,0:T(8,128)(2,1)S(1)} %collective-permute-done.10.x_own, ...), custom_call_target="tpu_custom_call" | custom-call | flops 1811939328 | bytes 9437184 | tf_op jit(solution)/shard_map/project/pallas_call | solution.py:224
  127.1 1.4 %collective-permute-done.25.other = f32[384,128]{1,0:T(8,128)S(1)} collective-permute-done((f32[384,128]{1,0:T(8,128)S(1)}, f32[384,128]{1,0:T(8,128)S(1)}, u32[]{:S(2)}, u32[]{:S(2)}) %collective-permute-start.25) | collective-permute-done | bytes 196640 | tf_op jit(solution)/shard_map/ppermute | solution.py:302
  128.6 2.6 %normalize.1 = bf16[384,1536]{1,0:T(8,128)(2,1)} custom-call(s32[4]{0:T(128)S(1)} %pad_add_fusion.info, f32[384,1536]{1,0:T(8,128)S(1)} %get-tuple-element.13.mixed, f32[384,128]{1,0:T(8,128)S(1)} %get-tuple-element.14.mine, f32[384,128]{1,0:T(8,128)S(1)} %collective-permute-done.25.other, f32[1,3072]{1,0:T(1,128)S(1)} %bitcast.19, f32[1,3072]{1,0:T(1,128)S(1)} %bitcast.20), custom_call_target="tpu_custom_call" | custom-call | flops 3538944 | bytes 3538944 | tf_op jit(solution)/shard_map/normalize/pallas_call | solution.py:267
  (61 shorter events, 13.5 us)
Async XLA Ops:
  2.0 32.7 %copy-start.1 = (bf16[192,1536]{1,0:T(8,128)(2,1)S(1)}, bf16[192,1536]{1,0:T(8,128)(2,1)}, u32[]{:S(2)}) copy-start(bf16[192,1536]{1,0:T(8,128)(2,1)} %rest_0_.1) | copy-start | bytes 1769476
  2.9 30.2 %collective-permute-start.2 = (bf16[2,384,384]{2,1,0:T(8,128)(2,1)}, bf16[2,384,384]{2,1,0:T(8,128)(2,1)S(1)}, u32[]{:S(2)}, u32[]{:S(2)}) collective-permute-start(bf16[2,384,384]{2,1,0:T(8,128)(2,1)} %pad_maximum_fusion.1), channel_id=1, source_target_pairs={{0,8},{2,10},{4,12},{6,14},{8,0},{10,2},{12,4},{14,6},{1,9},{3,11}... | collective-permute-start | bytes 1769480 | tf_op jit(solution)/shard_map/ppermute | solution.py:299
  7.0 44.4 %copy-start = (bf16[384,768]{1,0:T(8,128)(2,1)S(1)}, bf16[384,768]{1,0:T(8,128)(2,1)}, u32[]{:S(2)}) copy-start(bf16[384,768]{1,0:T(8,128)(2,1)} %query.1) | copy-start | bytes 1769476
  7.1 33.2 %collective-permute-start = (bf16[2,384,384]{2,1,0:T(8,128)(2,1)S(1)}, bf16[2,384,384]{2,1,0:T(8,128)(2,1)S(1)}, u32[]{:S(2)}, u32[]{:S(2)}) collective-permute-start(bf16[2,384,384]{2,1,0:T(8,128)(2,1)S(1)} %pad_maximum_fusion.own), channel_id=1, source_target_pairs={{0,2},{2,0},{4,6},{6,4},{8,10},{10,8},{12,14},{14,12},{1,3},{3,1},... | collective-permute-start | bytes 1769480 | tf_op jit(solution)/shard_map/ppermute | solution.py:299
  33.2 25.5 %collective-permute-start.3 = (bf16[2,384,384]{2,1,0:T(8,128)(2,1)S(1)}, bf16[2,384,384]{2,1,0:T(8,128)(2,1)S(1)}, u32[]{:S(2)}, u32[]{:S(2)}) collective-permute-start(bf16[2,384,384]{2,1,0:T(8,128)(2,1)S(1)} %collective-permute-done.2.e_kv), channel_id=1, source_target_pairs={{0,2},{2,0},{4,6},{6,4},{8,10},{10,8},{12,14},{14,12},{1,3},{3,1},... | collective-permute-start | bytes 1769480 | tf_op jit(solution)/shard_map/ppermute | solution.py:299
  34.8 16.2 %collective-permute-start.12 = (bf16[96,1536]{1,0:T(8,128)(2,1)S(1)}, bf16[96,1536]{1,0:T(8,128)(2,1)}, u32[]{:S(2)}, u32[]{:S(2)}) collective-permute-start(bf16[96,1536]{1,0:T(8,128)(2,1)S(1)} %constant_dynamic-slice_fusion), channel_id=1, source_target_pairs={{0,4},{2,6},{4,0},{6,2},{8,12},{10,14},{12,8},{14,10},{1,5},{3,7},... | collective-permute-start | bytes 884744 | tf_op jit(solution)/shard_map/ppermute | solution.py:299
  35.6 16.5 %collective-permute-start.7 = (bf16[96,1536]{1,0:T(8,128)(2,1)S(1)}, bf16[96,1536]{1,0:T(8,128)(2,1)}, u32[]{:S(2)}, u32[]{:S(2)}) collective-permute-start(bf16[96,1536]{1,0:T(8,128)(2,1)S(1)} %constant_dynamic-slice_fusion), channel_id=1, source_target_pairs={{0,8},{2,10},{4,12},{6,14},{8,0},{10,2},{12,4},{14,6},{1,9},{3,11}... | collective-permute-start | bytes 884744 | tf_op jit(solution)/shard_map/ppermute | solution.py:299
  38.9 16.2 %collective-permute-start.5 = (bf16[384,384]{1,0:T(8,128)(2,1)S(1)}, bf16[384,384]{1,0:T(8,128)(2,1)S(1)}, u32[]{:S(2)}, u32[]{:S(2)}) collective-permute-start(bf16[384,384]{1,0:T(8,128)(2,1)S(1)} %slice_bitcast_fusion), channel_id=1, source_target_pairs={{2,6},{4,0},{10,14},{12,8},{3,7},{5,1},{11,15},{13,9},{18,22},{20,... | collective-permute-start | bytes 884744 | tf_op jit(solution)/shard_map/ppermute | solution.py:306
  40.2 24.2 %collective-permute-start.1 = (bf16[2,384,384]{2,1,0:T(8,128)(2,1)S(1)}, bf16[2,384,384]{2,1,0:T(8,128)(2,1)S(1)}, u32[]{:S(2)}, u32[]{:S(2)}) collective-permute-start(bf16[2,384,384]{2,1,0:T(8,128)(2,1)S(1)} %collective-permute-done.y_own), channel_id=1, source_target_pairs={{0,4},{6,2},{8,12},{14,10},{1,5},{7,3},{9,13},{15,11},{16,20},{22,... | collective-permute-start | bytes 1769480 | tf_op jit(solution)/shard_map/ppermute | solution.py:306
  51.0 9.9 %collective-permute-start.13 = (bf16[96,1536]{1,0:T(8,128)(2,1)S(1)}, bf16[96,1536]{1,0:T(8,128)(2,1)}, u32[]{:S(2)}, u32[]{:S(2)}) collective-permute-start(bf16[96,1536]{1,0:T(8,128)(2,1)S(1)} %constant_dynamic-slice_fusion), channel_id=1, source_target_pairs={{0,2},{2,0},{4,6},{6,4},{8,10},{10,8},{12,14},{14,12},{1,3},{3,1},... | collective-permute-start | bytes 884744 | tf_op jit(solution)/shard_map/ppermute | solution.py:299
  52.1 10.8 %collective-permute-start.14 = (bf16[96,1536]{1,0:T(8,128)(2,1)}, bf16[96,1536]{1,0:T(8,128)(2,1)S(1)}, u32[]{:S(2)}, u32[]{:S(2)}) collective-permute-start(bf16[96,1536]{1,0:T(8,128)(2,1)} %collective-permute-done.12.rest_1_), channel_id=1, source_target_pairs={{0,2},{2,0},{4,6},{6,4},{8,10},{10,8},{12,14},{14,12},{1,3},{3,1},... | collective-permute-start | bytes 884744 | tf_op jit(solution)/shard_map/ppermute | solution.py:299
  55.1 15.6 %collective-permute-start.8 = (bf16[384,384]{1,0:T(8,128)(2,1)}, bf16[384,384]{1,0:T(8,128)(2,1)}, u32[]{:S(2)}, u32[]{:S(2)}) collective-permute-start(bf16[384,384]{1,0:T(8,128)(2,1)} %constant_dynamic-slice_fusion.1), channel_id=1, source_target_pairs={{0,8},{2,10},{4,12},{6,14},{8,0},{10,2},{12,4},{14,6},{1,9},{3,11}... | collective-permute-start | bytes 884744 | tf_op jit(solution)/shard_map/ppermute | solution.py:299
  58.7 7.9 %collective-permute-start.6 = (bf16[384,384]{1,0:T(8,128)(2,1)S(1)}, bf16[384,384]{1,0:T(8,128)(2,1)S(1)}, u32[]{:S(2)}, u32[]{:S(2)}) collective-permute-start(bf16[384,384]{1,0:T(8,128)(2,1)S(1)} %collective-permute-done.5), channel_id=1, source_target_pairs={{0,2},{6,4},{8,10},{14,12},{1,3},{7,5},{9,11},{15,13},{16,18},{22,... | collective-permute-start | bytes 884744 | tf_op jit(solution)/shard_map/ppermute | solution.py:306
  60.9 13.9 %collective-permute-start.4 = (bf16[384,384]{1,0:T(8,128)(2,1)}, bf16[384,384]{1,0:T(8,128)(2,1)}, u32[]{:S(2)}, u32[]{:S(2)}) collective-permute-start(bf16[384,384]{1,0:T(8,128)(2,1)} %slice_bitcast_fusion.1), channel_id=1, source_target_pairs={{0,4},{6,2},{8,12},{14,10},{1,5},{7,3},{9,13},{15,11},{16,20},{22,... | collective-permute-start | bytes 884744 | tf_op jit(solution)/shard_map/ppermute | solution.py:306
  62.9 3.7 %copy-start.6 = (bf16[96,1536]{1,0:T(8,128)(2,1)}, bf16[96,1536]{1,0:T(8,128)(2,1)S(1)}, u32[]{:S(2)}) copy-start(bf16[96,1536]{1,0:T(8,128)(2,1)S(1)} %collective-permute-done.14.rest_3_) | copy-start | bytes 884740
  62.9 21.1 %collective-permute-start.18 = (bf16[96,1536]{1,0:T(8,128)(2,1)}, bf16[96,1536]{1,0:T(8,128)(2,1)}, u32[]{:S(2)}, u32[]{:S(2)}) collective-permute-start(bf16[96,1536]{1,0:T(8,128)(2,1)} %collective-permute-done.12.rest_1_), channel_id=1, source_target_pairs={{0,16},{16,0},{1,17},{17,1},{2,18},{18,2},{3,19},{19,3},{4,20},{20... | collective-permute-start | bytes 884744 | tf_op jit(solution)/shard_map/ppermute | solution.py:302
  64.4 20.2 %collective-permute-start.15 = (bf16[96,1536]{1,0:T(8,128)(2,1)}, bf16[96,1536]{1,0:T(8,128)(2,1)}, u32[]{:S(2)}, u32[]{:S(2)}) collective-permute-start(bf16[96,1536]{1,0:T(8,128)(2,1)} %collective-permute-done.7.rest_4_), channel_id=1, source_target_pairs={{0,4},{2,6},{4,0},{6,2},{8,12},{10,14},{12,8},{14,10},{1,5},{3,7},... | collective-permute-start | bytes 884744 | tf_op jit(solution)/shard_map/ppermute | solution.py:299
  67.3 19.3 %collective-permute-start.19 = (bf16[96,1536]{1,0:T(8,128)(2,1)}, bf16[96,1536]{1,0:T(8,128)(2,1)}, u32[]{:S(2)}, u32[]{:S(2)}) collective-permute-start(bf16[96,1536]{1,0:T(8,128)(2,1)} %collective-permute-done.13.rest_2_), channel_id=1, source_target_pairs={{0,16},{16,0},{1,17},{17,1},{2,18},{18,2},{3,19},{19,3},{4,20},{20... | collective-permute-start | bytes 884744 | tf_op jit(solution)/shard_map/ppermute | solution.py:302
  70.8 27.7 %collective-permute-start.16 = (bf16[96,1536]{1,0:T(8,128)(2,1)}, bf16[96,1536]{1,0:T(8,128)(2,1)}, u32[]{:S(2)}, u32[]{:S(2)}) collective-permute-start(bf16[96,1536]{1,0:T(8,128)(2,1)} %collective-permute-done.7.rest_4_), channel_id=1, source_target_pairs={{0,2},{2,0},{4,6},{6,4},{8,10},{10,8},{12,14},{14,12},{1,3},{3,1},... | collective-permute-start | bytes 884744 | tf_op jit(solution)/shard_map/ppermute | solution.py:299
  74.8 21.4 %collective-permute-start.20 = (bf16[96,1536]{1,0:T(8,128)(2,1)}, bf16[96,1536]{1,0:T(8,128)(2,1)S(1)}, u32[]{:S(2)}, u32[]{:S(2)}) collective-permute-start(bf16[96,1536]{1,0:T(8,128)(2,1)} %copy-done.6), channel_id=1, source_target_pairs={{0,16},{16,0},{1,17},{17,1},{2,18},{18,2},{3,19},{19,3},{4,20},{20... | collective-permute-start | bytes 884744 | tf_op jit(solution)/shard_map/ppermute | solution.py:302
  84.0 15.0 %collective-permute-start.21 = (bf16[96,1536]{1,0:T(8,128)(2,1)}, bf16[96,1536]{1,0:T(8,128)(2,1)S(1)}, u32[]{:S(2)}, u32[]{:S(2)}) collective-permute-start(bf16[96,1536]{1,0:T(8,128)(2,1)} %collective-permute-done.7.rest_4_), channel_id=1, source_target_pairs={{0,16},{16,0},{1,17},{17,1},{2,18},{18,2},{3,19},{19,3},{4,20},{20... | collective-permute-start | bytes 884744 | tf_op jit(solution)/shard_map/ppermute | solution.py:302
  84.6 15.1 %collective-permute-start.17 = (bf16[96,1536]{1,0:T(8,128)(2,1)}, bf16[96,1536]{1,0:T(8,128)(2,1)}, u32[]{:S(2)}, u32[]{:S(2)}) collective-permute-start(bf16[96,1536]{1,0:T(8,128)(2,1)} %collective-permute-done.15.rest_5_), channel_id=1, source_target_pairs={{0,2},{2,0},{4,6},{6,4},{8,10},{10,8},{12,14},{14,12},{1,3},{3,1},... | collective-permute-start | bytes 884744 | tf_op jit(solution)/shard_map/ppermute | solution.py:299
  86.7 14.5 %collective-permute-start.9 = (bf16[384,384]{1,0:T(8,128)(2,1)S(1)}, bf16[384,384]{1,0:T(8,128)(2,1)}, u32[]{:S(2)}, u32[]{:S(2)}) collective-permute-start(bf16[384,384]{1,0:T(8,128)(2,1)S(1)} %attend.3), channel_id=1, source_target_pairs={{0,8},{2,10},{4,12},{6,14},{8,0},{10,2},{12,4},{14,6},{1,9},{3,11}... | collective-permute-start | bytes 884744 | tf_op jit(solution)/shard_map/ppermute | solution.py:299
  96.9 15.7 %collective-permute-start.22 = (bf16[96,1536]{1,0:T(8,128)(2,1)}, bf16[96,1536]{1,0:T(8,128)(2,1)S(1)}, u32[]{:S(2)}, u32[]{:S(2)}) collective-permute-start(bf16[96,1536]{1,0:T(8,128)(2,1)} %collective-permute-done.15.rest_5_), channel_id=1, source_target_pairs={{0,16},{16,0},{1,17},{17,1},{2,18},{18,2},{3,19},{19,3},{4,20},{20... | collective-permute-start | bytes 884744 | tf_op jit(solution)/shard_map/ppermute | solution.py:302
  98.4 14.2 %collective-permute-start.23 = (bf16[96,1536]{1,0:T(8,128)(2,1)}, bf16[96,1536]{1,0:T(8,128)(2,1)S(1)}, u32[]{:S(2)}, u32[]{:S(2)}) collective-permute-start(bf16[96,1536]{1,0:T(8,128)(2,1)} %collective-permute-done.16.rest_6_), channel_id=1, source_target_pairs={{0,16},{16,0},{1,17},{17,1},{2,18},{18,2},{3,19},{19,3},{4,20},{20... | collective-permute-start | bytes 884744 | tf_op jit(solution)/shard_map/ppermute | solution.py:302
  99.7 16.1 %collective-permute-start.10 = (bf16[384,384]{1,0:T(8,128)(2,1)}, bf16[384,384]{1,0:T(8,128)(2,1)S(1)}, u32[]{:S(2)}, u32[]{:S(2)}) collective-permute-start(bf16[384,384]{1,0:T(8,128)(2,1)} %attend.2.a_own), channel_id=1, source_target_pairs={{0,1},{1,0},{2,3},{3,2},{4,5},{5,4},{6,7},{7,6},{8,9},{9,8},{10,11... | collective-permute-start | bytes 884744 | tf_op jit(solution)/shard_map/ppermute | solution.py:302
  99.7 16.1 %collective-permute-start.24 = (bf16[96,1536]{1,0:T(8,128)(2,1)}, bf16[96,1536]{1,0:T(8,128)(2,1)S(1)}, u32[]{:S(2)}, u32[]{:S(2)}) collective-permute-start(bf16[96,1536]{1,0:T(8,128)(2,1)} %collective-permute-done.17.rest_7_), channel_id=1, source_target_pairs={{0,16},{16,0},{1,17},{17,1},{2,18},{18,2},{3,19},{19,3},{4,20},{20... | collective-permute-start | bytes 884744 | tf_op jit(solution)/shard_map/ppermute | solution.py:302
  101.2 14.6 %collective-permute-start.11 = (bf16[384,384]{1,0:T(8,128)(2,1)}, bf16[384,384]{1,0:T(8,128)(2,1)S(1)}, u32[]{:S(2)}, u32[]{:S(2)}) collective-permute-start(bf16[384,384]{1,0:T(8,128)(2,1)} %collective-permute-done.9.a_ret), channel_id=1, source_target_pairs={{0,1},{1,0},{2,3},{3,2},{4,5},{5,4},{6,7},{7,6},{8,9},{9,8},{10,11... | collective-permute-start | bytes 884744 | tf_op jit(solution)/shard_map/ppermute | solution.py:302
  116.9 1.3 copy-start.5
  121.0 7.5 %copy-start.12 = (f32[3072]{0:T(1024)S(1)}, f32[3072]{0:T(1024)}, u32[]{:S(2)}) copy-start(f32[3072]{0:T(1024)} %param.12) | copy-start | bytes 36868
  121.0 7.5 %copy-start.13 = (f32[3072]{0:T(1024)S(1)}, f32[3072]{0:T(1024)}, u32[]{:S(2)}) copy-start(f32[3072]{0:T(1024)} %param.11) | copy-start | bytes 36868
  127.1 1.5 %collective-permute-start.25 = (f32[384,128]{1,0:T(8,128)S(1)}, f32[384,128]{1,0:T(8,128)S(1)}, u32[]{:S(2)}, u32[]{:S(2)}) collective-permute-start(f32[384,128]{1,0:T(8,128)S(1)} %get-tuple-element.14.mine), channel_id=1, source_target_pairs={{0,1},{1,0},{2,3},{3,2},{4,5},{5,4},{6,7},{7,6},{8,9},{9,8},{10,11... | collective-permute-start | bytes 589832 | tf_op jit(solution)/shard_map/ppermute | solution.py:302
  (8 other events, 7.1 us)
where the time goes:
time: 132 us; the launch traced here: 131 us
  waiting for transfers between devices  52.1 us (39%)
  starting transfers between devices  43.2 us (33%)
  Pallas kernels  22.8 us (17%)
  local copies, waits for them, and re-layouts  11.2 us (8%)
    ppermute x12, waiting for transfers between devices, flip(): return lax.ppermute(x, 'seq', [(i, i ^ mask) for i in range(count)])  32.9 us
    ppermute x12, starting transfers between devices, flip(): return lax.ppermute(x, 'seq', [(i, i ^ mask) for i in range(count)])  25.4 us
    ppermute x10, waiting for transfers between devices, swap(): return lax.ppermute(x, axis, [(0, 1), (1, 0)])  15.7 us
    pallas_call x2, Pallas kernels, attention(): pl.pallas_call(attention_kernel, grid_spec=pltpu.PrefetchScalarGridSpec(n...  14.2 us
    ppermute x4, starting transfers between devices, some(): return lax.ppermute(x, 'seq', pairs)  9.33 us
    ppermute x10, starting transfers between devices, swap(): return lax.ppermute(x, axis, [(0, 1), (1, 0)])  8.47 us
    unnamed x28, local copies, waits for them, and re-layouts  8.34 us
    pallas_call x1, Pallas kernels, project(): pl.pallas_call(functools.partial(project_kernel, places=places, count=len...  6.01 us
  transfers between devices with their start and end apart: 26, of which 8 were waited for; matrix products, arithmetic and copies ran while one was open for 1% of the time, Pallas kernels for 11%

commit v1 on v0

--- a/solution.py
+++ b/solution.py
@@ -1,4 +1,5 @@
 import functools
+import itertools
 import math
 
 import jax
@@ -16,6 +17,7 @@
 EPS = 1e-06
 EXP2_SCALE = math.log2(math.e) / math.sqrt(HD)
 AWAY = -1e30
+GROUP = 3
 
 
 def shifted(value, axis, steps):
@@ -104,89 +106,126 @@
     return (normed, mixed.astype(jnp.bfloat16))
 
 
-def attention_kernel(info, query, own, y_own, z_own, e_kv, y_oth, k_far, v_far, out):
+def lane_blocks(x, op):
+    return functools.reduce(op, [x[:, c : c + HD] for c in range(0, x.shape[1], HD)])
+
+
+def attention_kernel(info, query, *refs, kinds, own, resume, final):
+    refs = list(refs)
+    parts = []
+    for stacked, far in kinds:
+        if stacked:
+            ref = refs.pop(0)
+            parts.append((ref.at[0], ref.at[1], far))
+        else:
+            parts.append((refs.pop(0), refs.pop(0), far))
+    before = [refs.pop(0) for _ in range(3)] if resume else None
     rows = query.shape[0]
     tiles = rows // TILE
+    heads = refs[0].shape[1] // HD
     away = jnp.where(info[1] == 1, jnp.float32(0), jnp.float32(AWAY))
-    parts = [(ref.at[0], ref.at[1], False) for ref in (own, y_own, e_kv, y_oth)]
-    parts += [(z_own.at[0], z_own.at[1], True), (k_far, v_far, True)]
-    for tile in range(tiles):
+    units = list(itertools.product(range(heads), range(tiles)))
+
+    def place(head, tile):
         begin = max(tile - 1, 0) * TILE
         end = (min(tile + 1, tiles - 1) + 1) * TILE
-        q = query[tile * TILE : (tile + 1) * TILE, :]
-        scores = []
-        tops = []
-        for keys, values, far in parts:
-            s = lax.dot_general(
+        here = slice(tile * TILE, (tile + 1) * TILE)
+        return here, slice(begin, end), slice(head * HD, (head + 1) * HD)
+
+    def score(head, tile):
+        here, seen, feats = place(head, tile)
+        if own:
+            q = query[here, pl.ds(pl.multiple_of((info[0] * heads + head) * HD, HD), HD)]
+        else:
+            q = query[here, feats]
+        return [
+            lax.dot_general(
                 q,
-                keys[begin:end, :],
+                keys[seen, feats],
                 (((1,), (1,)), ((), ())),
                 preferred_element_type=jnp.float32,
             )
-            scores.append(s)
-            top = jnp.max(s, axis=1, keepdims=True)
-            tops.append(top + away if far else top)
-        top = functools.reduce(jnp.maximum, tops)
-        total = jnp.zeros((TILE, 1), jnp.float32)
+            for keys, _, _ in parts
+        ]
+
+    def highest(scores):
+        tops = [
+            lane_blocks(s, jnp.maximum) + (away if far else 0.0)
+            for s, (_, _, far) in zip(scores, parts)
+        ]
+        return jnp.max(functools.reduce(jnp.maximum, tops), axis=1, keepdims=True)
+
+    def gather(head, tile, scores, top):
+        here, seen, feats = place(head, tile)
         acc = jnp.zeros((TILE, HD), jnp.float32)
-        for s, (keys, values, far) in zip(scores, parts):
+        total = jnp.zeros((TILE, HD), jnp.float32)
+        if resume:
+            old = before[2][here, feats][:, 0:1]
+            top = jnp.maximum(top, old)
+            keep = jnp.exp2((old - top) * EXP2_SCALE)
+            acc = before[0][here, feats] * keep
+        for s, (_, values, far) in zip(scores, parts):
             p = jnp.exp2((s - (top - away if far else top)) * EXP2_SCALE)
-            total = total + jnp.sum(p, axis=1, keepdims=True)
+            total = total + lane_blocks(p, jnp.add)
             acc = acc + jnp.dot(
-                p.astype(jnp.bfloat16), values[begin:end, :], preferred_element_type=jnp.float32
+                p.astype(jnp.bfloat16), values[seen, feats], preferred_element_type=jnp.float32
             )
-        out[tile * TILE : (tile + 1) * TILE, :] = (acc / total).astype(jnp.bfloat16)
-
-
-def attention(info, query, own, parts):
+        total = jnp.sum(total, axis=1, keepdims=True)
+        if resume:
+            total = total + before[1][here, feats][:, 0:1] * keep
+        return acc, total, top
+
+    def write(head, tile, acc, total, top):
+        here, _, feats = place(head, tile)
+        if final:
+            refs[0][here, feats] = (acc / total).astype(jnp.bfloat16)
+        else:
+            refs[0][here, feats] = acc
+            refs[1][here, feats] = jnp.broadcast_to(total, (TILE, HD))
+            refs[2][here, feats] = jnp.broadcast_to(top, (TILE, HD))
+
+    for first in range(0, len(units), GROUP):
+        group = units[first : first + GROUP]
+        scores = [score(*unit) for unit in group]
+        tops = [highest(s) for s in scores]
+        done = [gather(*unit, s, top) for unit, s, top in zip(group, scores, tops)]
+        for unit, result in zip(group, done):
+            write(*unit, *result)
+
+
+def attention(info, query, own, parts, before=(), final=True):
     rows = query.shape[0]
-    cols = parts[0].shape[2]
+    cols = parts[0][0][0].shape[-1]
     heads = cols // HD
-    if own:
-        q_map = lambda j, info: (0, info[0] * heads + j)
+    vmem = pl.BlockSpec(memory_space=pltpu.VMEM)
+    operands = [x for given, far in parts for x in given] + list(before)
+    kinds = tuple((len(given) == 1, far) for given, far in parts)
+    pairs = rows * 7 * TILE * len(parts) * heads // 3
+    if final:
+        out_shape = jax.ShapeDtypeStruct((rows, cols), jnp.bfloat16)
+        out_specs = vmem
     else:
-        q_map = lambda j, info: (0, j)
-    pair_spec = pl.BlockSpec((2, rows, HD), lambda j, info: (0, 0, j))
-    one_spec = pl.BlockSpec((rows, HD), lambda j, info: (0, j))
-    pairs = rows * 7 * TILE * 2 * heads
+        out_shape = [jax.ShapeDtypeStruct((rows, cols), jnp.float32)] * 3
+        out_specs = [vmem] * 3
     return pl.pallas_call(
-        attention_kernel,
-        grid_spec=pltpu.PrefetchScalarGridSpec(
-            num_scalar_prefetch=1,
-            grid=(heads,),
-            in_specs=[pl.BlockSpec((rows, HD), q_map)] + [pair_spec] * 5 + [one_spec] * 2,
-            out_specs=pl.BlockSpec((rows, HD), lambda j, info: (0, j)),
+        functools.partial(
+            attention_kernel, kinds=kinds, own=own, resume=bool(before), final=final
         ),
-        out_shape=jax.ShapeDtypeStruct((rows, cols), jnp.bfloat16),
+        in_specs=[pl.BlockSpec(memory_space=pltpu.SMEM)] + [vmem] * (1 + len(operands)),
+        out_specs=out_specs,
+        out_shape=out_shape,
         compiler_params=pltpu.CompilerParams(vmem_limit_bytes=12 << 20),
         cost_estimate=pl.CostEstimate(
-            flops=pairs * HD * 4, transcendentals=pairs, bytes_accessed=rows * cols * 28
+            flops=pairs * HD * 4, transcendentals=pairs, bytes_accessed=rows * cols * 4 * len(parts)
         ),
         name="attend",
-    )(info, query, *parts)
-
-
-def project_kernel(
-    info, a_own, a_ret, x_own, x_ret, stream_hbm, *rest, places, count
-):
-    pieces = rest[:count]
-    mixed, stream_out, stats, weight, left, stream, sems = rest[count:]
+    )(info, query, *operands)
+
+
+def project_kernel(info, a_own, a_ret, x_own, x_ret, stream, *rest, places):
+    pieces = rest[: len(places)]
+    mixed, stream_out, stats, weight, left = rest[len(places) :]
     core, par, pos, vid = info[0], info[1], info[2], info[3]
-    copies = []
-    for piece, (flip, half, size) in zip(pieces, places):
-        other = pos ^ flip
-        if half is None:
-            row = other * size
-        else:
-            row = other * (2 * size) + (vid if half == 0 else 1 - vid) * size
-        copy = pltpu.make_async_copy(
-            piece, weight.at[pl.ds(pl.multiple_of(row, 32), size)], sems.at[len(copies)]
-        )
-        copy.start()
-        copies.append(copy)
-    copy = pltpu.make_async_copy(stream_hbm, stream, sems.at[len(copies)])
-    copy.start()
-    copies.append(copy)
     cols = a_own.shape[1]
     for ref, block in (
         (a_own, core * 2 + par),
@@ -195,23 +234,28 @@
         (x_ret, (1 - core) * 2 + 1 - par),
     ):
         left[:, pl.ds(pl.multiple_of(block * cols, HD), cols)] = ref[...]
-    for copy in copies:
-        copy.wait()
+    for piece, (flip, half, size) in zip(pieces, places):
+        row = (pos ^ flip) * size
+        if half is not None:
+            row = row * 2 + (vid if half == 0 else 1 - vid) * size
+        weight[pl.ds(pl.multiple_of(row, 32), size), :] = piece[...]
     rows, width = stream.shape
-    step = 512
-    total = jnp.zeros((rows, 1), jnp.float32)
+    step = width // 3
+    total = jnp.zeros((rows, HD), jnp.float32)
     for first in range(0, width, step):
+        block = slice(first, first + step)
         got = jnp.dot(
-            left[...], weight[:, first : first + step], preferred_element_type=jnp.float32
-        ) + stream[:, first : first + step].astype(jnp.float32)
-        mixed[:, first : first + step] = got
-        stream_out[:, first : first + step] = got.astype(jnp.bfloat16)
-        total = total + jnp.sum(got, axis=1, keepdims=True)
-    mean = total * (1.0 / width)
-    square = jnp.zeros((rows, 1), jnp.float32)
-    for first in range(0, width, step):
-        off = mixed[:, first : first + step] - mean
-        square = square + jnp.sum(off * off, axis=1, keepdims=True)
+            left[...], weight[:, block], preferred_element_type=jnp.float32
+        ) + stream[:, block].astype(jnp.float32)
+        mixed[:, block] = got
+        stream_out[:, block] = got.astype(jnp.bfloat16)
+        total = total + lane_blocks(got, jnp.add)
+    mean = jnp.sum(total, axis=1, keepdims=True) * (1.0 / width)
+    square = jnp.zeros((rows, HD), jnp.float32)
+    for first in range(0, width, HD):
+        off = mixed[:, first : first + HD] - mean
+        square = square + off * off
+    square = jnp.sum(square, axis=1, keepdims=True)
     lane = lax.broadcasted_iota(jnp.int32, stats.shape, 1)
     stats[...] = jnp.where(lane == 0, mean, square)
 
@@ -219,13 +263,10 @@
 def project(info, blocks, stream, pieces, places):
     rows, width = stream.shape
     depth = 4 * blocks[0].shape[1]
-    copies = len(places)
     vmem = pl.BlockSpec(memory_space=pltpu.VMEM)
     return pl.pallas_call(
-        functools.partial(project_kernel, places=places, count=len(pieces)),
-        in_specs=[pl.BlockSpec(memory_space=pltpu.SMEM)]
-        + [vmem] * 4
-        + [pl.BlockSpec(memory_space=pltpu.HBM)] * (1 + len(pieces)),
+        functools.partial(project_kernel, places=places),
+        in_specs=[pl.BlockSpec(memory_space=pltpu.SMEM)] + [vmem] * (5 + len(pieces)),
         out_specs=[vmem] * 3,
         out_shape=[
             jax.ShapeDtypeStruct((rows, width), jnp.float32),
@@ -235,10 +276,8 @@
         scratch_shapes=[
             pltpu.VMEM((depth, width), jnp.bfloat16),
             pltpu.VMEM((rows, depth), jnp.bfloat16),
-            pltpu.VMEM((rows, width), jnp.bfloat16),
-            pltpu.SemaphoreType.DMA((copies + 1,)),
         ],
-        compiler_params=pltpu.CompilerParams(vmem_limit_bytes=20 << 20),
+        compiler_params=pltpu.CompilerParams(vmem_limit_bytes=24 << 20),
         cost_estimate=pl.CostEstimate(
             flops=2 * rows * depth * width,
             transcendentals=0,
@@ -248,31 +287,44 @@
     )(info, *blocks, stream, *pieces)
 
 
-def norm_kernel(info, mixed, mine, other, scale, shift, out, *, half):
+def norm_kernel(info, mixed, mine, other, scale, shift, out, held, sems):
+    rows, width = mixed.shape
+    step = rows // sems.shape[0]
     m0, m1 = mine[:, 0:1], other[:, 0:1]
     q0, q1 = mine[:, 1:2], other[:, 1:2]
     mean = 0.5 * (m0 + m1)
     gap = m0 - m1
-    var = (q0 + q1 + gap * gap * (0.5 * half)) * (0.5 / half)
+    var = (q0 + q1 + gap * gap * (0.5 * width)) * (0.5 / width)
     rate = lax.rsqrt(var + EPS)
-    out[...] = ((mixed[...] - mean) * rate * (1.0 + scale[...]) + shift[...]).astype(jnp.bfloat16)
+    columns = pl.ds(pl.multiple_of(info[0] * width, HD), width)
+    gain = 1.0 + scale[:, columns]
+    bias = shift[:, columns]
+    copies = []
+    for first in range(0, rows, step):
+        here = slice(first, first + step)
+        held[here, :] = ((mixed[here, :] - mean[here]) * rate[here] * gain + bias).astype(
+            jnp.bfloat16
+        )
+        copies.append(
+            pltpu.make_async_copy(held.at[here, :], out.at[here, :], sems.at[len(copies)])
+        )
+        copies[-1].start()
+    for copy in copies:
+        copy.wait()
 
 
 def normalize(info, mixed, mine, other, scale_mod, shift_mod):
     rows, width = mixed.shape
-    step = TILE
-    row_block = pl.BlockSpec((step, width), lambda i, info: (i, 0))
-    stat_block = pl.BlockSpec((step, HD), lambda i, info: (i, 0))
-    mod_block = pl.BlockSpec((1, width), lambda i, info: (0, info[0]))
+    vmem = pl.BlockSpec(memory_space=pltpu.VMEM)
     return pl.pallas_call(
-        functools.partial(norm_kernel, half=float(width)),
-        grid_spec=pltpu.PrefetchScalarGridSpec(
-            num_scalar_prefetch=1,
-            grid=(rows // step,),
-            in_specs=[row_block, stat_block, stat_block, mod_block, mod_block],
-            out_specs=row_block,
-        ),
+        norm_kernel,
+        in_specs=[pl.BlockSpec(memory_space=pltpu.SMEM)] + [vmem] * 5,
+        out_specs=pl.BlockSpec(memory_space=pltpu.HBM),
         out_shape=jax.ShapeDtypeStruct((rows, width), jnp.bfloat16),
+        scratch_shapes=[
+            pltpu.VMEM((rows, width), jnp.bfloat16),
+            pltpu.SemaphoreType.DMA((rows // TILE,)),
+        ],
         compiler_params=pltpu.CompilerParams(vmem_limit_bytes=12 << 20),
         cost_estimate=pl.CostEstimate(
             flops=6 * rows * width, transcendentals=rows, bytes_accessed=rows * width * 6
@@ -308,37 +360,51 @@
     def heads(x, which):
         return lax.dynamic_slice_in_dim(x, which * half_cols, half_cols, 1)
 
-    give = jnp.stack([heads(key, 1 - par), heads(value, 1 - par)])
+    give_k = heads(key, 1 - par)
+    own_k = heads(key, par)
+    own_v = heads(value, par)
+    give_v = heads(value, 1 - par)
     give_q = heads(query, 1 - par)
-    own = jnp.stack([heads(key, par), heads(value, par)])
     rows_half = out_weight.shape[0] // 2
     w_own = lax.dynamic_slice_in_dim(out_weight, vid * rows_half, rows_half, 0)
 
-    e_kv = flip(give, HT)
-    y_own = flip(own, 1)
+    e_k = flip(give_k, HT)
+    y_ok = flip(own_k, 1)
     w_z1 = flip(w_own, 2)
-    z_own = some(y_own, 2, (0, 3))
-    w_ya = flip(after(w_own, y_own), 1)
-    w_yb = flip(after(w_z1, y_own), 1)
+    e_v = flip(give_v, HT)
+    y_ov = flip(own_v, 1)
+    ov_z = some(own_v, 2, (1, 2))
+    ok_far = some(y_ok, 2, (0, 3))
+    w_ya = flip(after(w_own, y_ov), 1)
+    ov_far = some(ov_z, 1, (0, 3))
+    y_k = flip(e_k, 1)
     w_xa = swap(w_z1, "video")
-    w_t = flip(after(w_own, e_kv), HT)
-    y_oth = flip(e_kv, 1)
-    v_z = some(e_kv[1], 2, (1, 2))
+    w_t = flip(after(w_own, e_v), HT)
+    y_v = flip(e_v, 1)
+    v_z = some(e_v, 2, (1, 2))
+    k_far = some(y_k, 2, (0, 3))
+    v_far = some(v_z, 1, (0, 3))
     w_xb = swap(w_ya, "video")
+    w_yb = flip(after(w_z1, y_v), 1)
     w_xc = swap(w_yb, "video")
+    w_z2 = flip(w_t, 2)
     e_q = flip(after(give_q, w_t), HT)
-    k_far = some(y_oth[0], 2, (0, 3))
-    v_far = some(v_z, 1, (0, 3))
+    w_xd = swap(w_t, "video")
     w_yc = flip(w_t, 1)
-    w_z2 = flip(w_t, 2)
-    w_xd = swap(w_t, "video")
     w_yd = flip(w_z2, 1)
-    w_xe = swap(w_z2, "video")
+    w_xe = flip(w_xd, 2)
     w_xf = swap(w_yc, "video")
-    w_xg = swap(w_yd, "video")
+    w_xg = flip(w_xe, 1)
 
     info = jnp.stack([par, relayed]).astype(jnp.int32)
-    parts = (own, y_own, z_own, e_kv, y_oth, k_far, v_far)
+    parts = (
+        ((own_k, own_v), False),
+        ((y_ok, y_ov), False),
+        ((ok_far, ov_far), True),
+        ((e_k, e_v), False),
+        ((y_k, y_v), False),
+        ((k_far, v_far), True),
+    )
     out_other = attention(info, e_q, False, parts)
     a_ret = flip(out_other, HT)
     a_own = attention(info, query, True, parts)

time: 132 us -> 122 us (0.924)
  waiting for transfers between devices: 52.1 us -> 42.1 us
  Pallas kernels: 22.8 us -> 14.8 us
  local copies, waits for them, and re-layouts: 11.2 us -> 16.1 us
  starting transfers between devices: 43.2 us -> 47.9 us
    ppermute x10 -> x8, waiting for transfers between devices: 15.7 us -> 1.46 us  [swap(): return lax.ppermute(x, axis, [(0, 1), (1, 0)])]
    ppermute x12 -> x17, starting transfers between devices: 25.4 us -> 33.6 us  [flip(): return lax.ppermute(x, 'seq', [(i, i ^ mask) for i in range(count)])]
    pallas_call x4, Pallas kernels: 22.8 us -> 14.8 us  [the longest x2 7.65 us: attention(): pl.pallas_call(functools.partial(attention_kernel, kinds=kinds, own=own,...]
    unnamed x28 -> x46, local copies, waits for them, and re-layouts: 8.34 us -> 14 us
    ppermute x12 -> x17, waiting for transfers between devices: 32.9 us -> 37.6 us  [flip(): return lax.ppermute(x, 'seq', [(i, i ^ mask) for i in range(count)])]
    ppermute x10 -> x8, starting transfers between devices: 8.47 us -> 5.16 us  [swap(): return lax.ppermute(x, axis, [(0, 1), (1, 0)])]
    another operation x1 -> x0, local copies, waits for them, and re-layouts: 1.36 us -> none  [on_device_pair(): give = jnp.stack([heads(key, 1 - par), heads(value, 1 - par)])]
    ppermute x4 -> x6, waiting for transfers between devices: 3.42 us -> 3 us  [some(): return lax.ppermute(x, 'seq', pairs)]
  transfers between devices with their start and end apart: 26 -> 31, of which waited for: 8 -> 10; matrix products, arithmetic and copies ran while one was open for 1% -> 1% of each run, Pallas kernels for 11% -> 6%
where the time goes in v1:
time: 122 us
  starting transfers between devices  47.9 us (39%)
  waiting for transfers between devices  42.1 us (35%)
  local copies, waits for them, and re-layouts  16.1 us (13%)
  Pallas kernels  14.8 us (12%)
    ppermute x17, waiting for transfers between devices, flip(): return lax.ppermute(x, 'seq', [(i, i ^ mask) for i in range(count)])  37.6 us
    ppermute x17, starting transfers between devices, flip(): return lax.ppermute(x, 'seq', [(i, i ^ mask) for i in range(count)])  33.6 us
    unnamed x46, local copies, waits for them, and re-layouts  14 us
    ppermute x6, starting transfers between devices, some(): return lax.ppermute(x, 'seq', pairs)  9.14 us
    pallas_call x2, Pallas kernels, attention(): pl.pallas_call(functools.partial(attention_kernel, kinds=kinds, own=own,...  7.65 us
    pallas_call x1, Pallas kernels, project(): pl.pallas_call(functools.partial(project_kernel, places=places), in_specs...  5.22 us
    ppermute x8, starting transfers between devices, swap(): return lax.ppermute(x, axis, [(0, 1), (1, 0)])  5.16 us
    ppermute x6, waiting for transfers between devices, some(): return lax.ppermute(x, 'seq', pairs)  3 us
  transfers between devices with their start and end apart: 31, of which 10 were waited for; matrix products, arithmetic and copies ran while one was open for 1% of the time, Pallas kernels for 6%

profile of v1, /device:TPU:0, one launch (start us, length us, event | category | flops | bytes accessed | tf_op | source)
XLA Modules:
  0.0 121.9 jit_solution(17626229261032610013)
XLA Ops:
  1.9 4.1 %collective-permute-start.6 = (bf16[384,384]{1,0:T(8,128)(2,1)S(1)}, bf16[384,384]{1,0:T(8,128)(2,1)S(1)}, u32[]{:S(2)}, u32[]{:S(2)}) collective-permute-start(bf16[384,384]{1,0:T(8,128)(2,1)S(1)} %get-tuple-element.16), channel_id=1, source_target_pairs={{0,8},{2,10},{4,12},{6,14},{8,0},{10,2},{12,4},{14,6},{1,9},{3,11}... | collective-permute-start | bytes 884744 | tf_op jit(solution)/shard_map/ppermute | solution.py:351
  6.8 1.6 %collective-permute-start.17 = (bf16[96,1536]{1,0:T(8,128)(2,1)}, bf16[96,1536]{1,0:T(8,128)(2,1)}, u32[]{:S(2)}, u32[]{:S(2)}) collective-permute-start(bf16[96,1536]{1,0:T(8,128)(2,1)} %constant_dynamic-slice_fusion), channel_id=1, source_target_pairs={{0,4},{2,6},{4,0},{6,2},{8,12},{10,14},{12,8},{14,10},{1,5},{3,7},... | collective-permute-start | bytes 884744 | tf_op jit(solution)/shard_map/ppermute | solution.py:351
  8.8 1.5 %collective-permute-start = (bf16[384,384]{1,0:T(8,128)(2,1)S(1)}, bf16[384,384]{1,0:T(8,128)(2,1)S(1)}, u32[]{:S(2)}, u32[]{:S(2)}) collective-permute-start(bf16[384,384]{1,0:T(8,128)(2,1)S(1)} %get-tuple-element.19.refs_0_), channel_id=1, source_target_pairs={{0,2},{2,0},{4,6},{6,4},{8,10},{10,8},{12,14},{14,12},{1,3},{3,1},... | collective-permute-start | bytes 884744 | tf_op jit(solution)/shard_map/ppermute | solution.py:351
  10.3 10.8 %collective-permute-done.6.refs_7_ = bf16[384,384]{1,0:T(8,128)(2,1)S(1)} collective-permute-done((bf16[384,384]{1,0:T(8,128)(2,1)S(1)}, bf16[384,384]{1,0:T(8,128)(2,1)S(1)}, u32[]{:S(2)}, u32[]{:S(2)}) %collective-permute-start.6) | collective-permute-done | bytes 294944 | tf_op jit(solution)/shard_map/ppermute | solution.py:351
  21.1 1.3 %collective-permute-start.3 = (bf16[384,384]{1,0:T(8,128)(2,1)S(1)}, bf16[384,384]{1,0:T(8,128)(2,1)S(1)}, u32[]{:S(2)}, u32[]{:S(2)}) collective-permute-start(bf16[384,384]{1,0:T(8,128)(2,1)S(1)} %get-tuple-element.17.refs_1_), channel_id=1, source_target_pairs={{2,6},{4,0},{10,14},{12,8},{3,7},{5,1},{11,15},{13,9},{18,22},{20,... | collective-permute-start | bytes 884744 | tf_op jit(solution)/shard_map/ppermute | solution.py:358
  22.4 5.8 %collective-permute-start.1 = (bf16[384,384]{1,0:T(8,128)(2,1)S(1)}, bf16[384,384]{1,0:T(8,128)(2,1)S(1)}, u32[]{:S(2)}, u32[]{:S(2)}) collective-permute-start(bf16[384,384]{1,0:T(8,128)(2,1)S(1)} %get-tuple-element.17.refs_1_), channel_id=1, source_target_pairs={{0,2},{2,0},{4,6},{6,4},{8,10},{10,8},{12,14},{14,12},{1,3},{3,1},... | collective-permute-start | bytes 884744 | tf_op jit(solution)/shard_map/ppermute | solution.py:351
  28.2 11.0 %collective-permute-done.5.refs_6_ = bf16[384,384]{1,0:T(8,128)(2,1)S(1)} collective-permute-done((bf16[384,384]{1,0:T(8,128)(2,1)S(1)}, bf16[384,384]{1,0:T(8,128)(2,1)S(1)}, u32[]{:S(2)}, u32[]{:S(2)}) %collective-permute-start.5) | collective-permute-done | bytes 294944 | tf_op jit(solution)/shard_map/ppermute | solution.py:351
  39.2 1.8 %collective-permute-start.7 = (bf16[384,384]{1,0:T(8,128)(2,1)S(1)}, bf16[384,384]{1,0:T(8,128)(2,1)S(1)}, u32[]{:S(2)}, u32[]{:S(2)}) collective-permute-start(bf16[384,384]{1,0:T(8,128)(2,1)S(1)} %collective-permute-done.5.refs_6_), channel_id=1, source_target_pairs={{0,2},{2,0},{4,6},{6,4},{8,10},{10,8},{12,14},{14,12},{1,3},{3,1},... | collective-permute-start | bytes 884744 | tf_op jit(solution)/shard_map/ppermute | solution.py:351
  41.0 1.6 %collective-permute-start.2 = (bf16[384,384]{1,0:T(8,128)(2,1)S(1)}, bf16[384,384]{1,0:T(8,128)(2,1)S(1)}, u32[]{:S(2)}, u32[]{:S(2)}) collective-permute-start(bf16[384,384]{1,0:T(8,128)(2,1)S(1)} %collective-permute-done.refs_2_), channel_id=1, source_target_pairs={{0,4},{6,2},{8,12},{14,10},{1,5},{7,3},{9,13},{15,11},{16,20},{22,... | collective-permute-start | bytes 884744 | tf_op jit(solution)/shard_map/ppermute | solution.py:358
  42.6 2.2 %collective-permute-done.12.rest_4_ = bf16[96,1536]{1,0:T(8,128)(2,1)} collective-permute-done((bf16[96,1536]{1,0:T(8,128)(2,1)}, bf16[96,1536]{1,0:T(8,128)(2,1)}, u32[]{:S(2)}, u32[]{:S(2)}) %collective-permute-start.12) | collective-permute-done | bytes 294944 | tf_op jit(solution)/shard_map/ppermute | solution.py:351
  44.8 1.3 %collective-permute-start.10 = (bf16[384,384]{1,0:T(8,128)(2,1)S(1)}, bf16[384,384]{1,0:T(8,128)(2,1)S(1)}, u32[]{:S(2)}, u32[]{:S(2)}) collective-permute-start(bf16[384,384]{1,0:T(8,128)(2,1)S(1)} %collective-permute-done.6.refs_7_), channel_id=1, source_target_pairs={{2,6},{4,0},{10,14},{12,8},{3,7},{5,1},{11,15},{13,9},{18,22},{20,... | collective-permute-start | bytes 884744 | tf_op jit(solution)/shard_map/ppermute | solution.py:358
  46.1 2.9 %collective-permute-start.8 = (bf16[384,384]{1,0:T(8,128)(2,1)S(1)}, bf16[384,384]{1,0:T(8,128)(2,1)S(1)}, u32[]{:S(2)}, u32[]{:S(2)}) collective-permute-start(bf16[384,384]{1,0:T(8,128)(2,1)S(1)} %collective-permute-done.6.refs_7_), channel_id=1, source_target_pairs={{0,2},{2,0},{4,6},{6,4},{8,10},{10,8},{12,14},{14,12},{1,3},{3,1},... | collective-permute-start | bytes 884744 | tf_op jit(solution)/shard_map/ppermute | solution.py:351
  49.1 1.9 %collective-permute-start.4 = (bf16[384,384]{1,0:T(8,128)(2,1)S(1)}, bf16[384,384]{1,0:T(8,128)(2,1)S(1)}, u32[]{:S(2)}, u32[]{:S(2)}) collective-permute-start(bf16[384,384]{1,0:T(8,128)(2,1)S(1)} %collective-permute-done.3), channel_id=1, source_target_pairs={{0,2},{6,4},{8,10},{14,12},{1,3},{7,5},{9,11},{15,13},{16,18},{22,... | collective-permute-start | bytes 884744 | tf_op jit(solution)/shard_map/ppermute | solution.py:358
  51.0 1.3 %collective-permute-start.9 = (bf16[384,384]{1,0:T(8,128)(2,1)S(1)}, bf16[384,384]{1,0:T(8,128)(2,1)S(1)}, u32[]{:S(2)}, u32[]{:S(2)}) collective-permute-start(bf16[384,384]{1,0:T(8,128)(2,1)S(1)} %collective-permute-done.7.refs_8_), channel_id=1, source_target_pairs={{0,4},{6,2},{8,12},{14,10},{1,5},{7,3},{9,13},{15,11},{16,20},{22,... | collective-permute-start | bytes 884744 | tf_op jit(solution)/shard_map/ppermute | solution.py:358
  52.4 3.4 %collective-permute-start.13 = (bf16[384,384]{1,0:T(8,128)(2,1)S(1)}, bf16[384,384]{1,0:T(8,128)(2,1)S(1)}, u32[]{:S(2)}, u32[]{:S(2)}) collective-permute-start(bf16[384,384]{1,0:T(8,128)(2,1)S(1)} %constant_dynamic-slice_fusion.1), channel_id=1, source_target_pairs={{0,8},{2,10},{4,12},{6,14},{8,0},{10,2},{12,4},{14,6},{1,9},{3,11}... | collective-permute-start | bytes 884744 | tf_op jit(solution)/shard_map/ppermute | solution.py:351
  55.8 1.8 %collective-permute-start.11 = (bf16[384,384]{1,0:T(8,128)(2,1)S(1)}, bf16[384,384]{1,0:T(8,128)(2,1)S(1)}, u32[]{:S(2)}, u32[]{:S(2)}) collective-permute-start(bf16[384,384]{1,0:T(8,128)(2,1)S(1)} %collective-permute-done.10), channel_id=1, source_target_pairs={{0,2},{6,4},{8,10},{14,12},{1,3},{7,5},{9,11},{15,13},{16,18},{22,... | collective-permute-start | bytes 884744 | tf_op jit(solution)/shard_map/ppermute | solution.py:358
  58.3 1.5 %collective-permute-start.23 = (bf16[96,1536]{1,0:T(8,128)(2,1)}, bf16[96,1536]{1,0:T(8,128)(2,1)}, u32[]{:S(2)}, u32[]{:S(2)}) collective-permute-start(bf16[96,1536]{1,0:T(8,128)(2,1)} %collective-permute-done.17.rest_1_), channel_id=1, source_target_pairs={{0,16},{16,0},{1,17},{17,1},{2,18},{18,2},{3,19},{19,3},{4,20},{20... | collective-permute-start | bytes 884744 | tf_op jit(solution)/shard_map/ppermute | solution.py:354
  59.8 3.0 %collective-permute-done.4.refs_5_ = bf16[384,384]{1,0:T(8,128)(2,1)S(1)} collective-permute-done((bf16[384,384]{1,0:T(8,128)(2,1)S(1)}, bf16[384,384]{1,0:T(8,128)(2,1)S(1)}, u32[]{:S(2)}, u32[]{:S(2)}) %collective-permute-start.4) | collective-permute-done | bytes 294944 | tf_op jit(solution)/shard_map/ppermute | solution.py:358
  63.5 2.5 %collective-permute-start.18 = (bf16[96,1536]{1,0:T(8,128)(2,1)}, bf16[96,1536]{1,0:T(8,128)(2,1)}, u32[]{:S(2)}, u32[]{:S(2)}) collective-permute-start(bf16[96,1536]{1,0:T(8,128)(2,1)} %constant_dynamic-slice_fusion), channel_id=1, source_target_pairs={{0,2},{2,0},{4,6},{6,4},{8,10},{10,8},{12,14},{14,12},{1,3},{3,1},... | collective-permute-start | bytes 884744 | tf_op jit(solution)/shard_map/ppermute | solution.py:351
  66.7 1.5 %collective-permute-start.26 = (bf16[96,1536]{1,0:T(8,128)(2,1)}, bf16[96,1536]{1,0:T(8,128)(2,1)}, u32[]{:S(2)}, u32[]{:S(2)}) collective-permute-start(bf16[96,1536]{1,0:T(8,128)(2,1)} %collective-permute-done.12.rest_4_), channel_id=1, source_target_pairs={{0,16},{16,0},{1,17},{17,1},{2,18},{18,2},{3,19},{19,3},{4,20},{20... | collective-permute-start | bytes 884744 | tf_op jit(solution)/shard_map/ppermute | solution.py:354
  77.0 3.8 %attend.3 = bf16[384,384]{1,0:T(8,128)(2,1)S(1)} custom-call(s32[2]{0:T(128)S(1)} %pad_add_fusion.1.info, bf16[384,384]{1,0:T(8,128)(2,1)S(1)} %copy-done.19, bf16[384,384]{1,0:T(8,128)(2,1)S(1)} %get-tuple-element.19.refs_0_, bf16[384,384]{1,0:T(8,128)(2,1)S(1)} %get-tuple-element.17.refs_1_, bf16[384,384]{1,0:T(8,128)(2,1)S(1)} %collective-permute-done.refs_2_, ...), custom_call_target="tpu_custom_call" | custom-call | flops 1056964608 | bytes 3538944 | tf_op jit(solution)/shard_map/attend/pallas_call | solution.py:210
  81.1 1.5 %collective-permute-start.24 = (bf16[96,1536]{1,0:T(8,128)(2,1)}, bf16[96,1536]{1,0:T(8,128)(2,1)S(1)}, u32[]{:S(2)}, u32[]{:S(2)}) collective-permute-start(bf16[96,1536]{1,0:T(8,128)(2,1)} %collective-permute-done.18.rest_2_), channel_id=1, source_target_pairs={{0,16},{16,0},{1,17},{17,1},{2,18},{18,2},{3,19},{19,3},{4,20},{20... | collective-permute-start | bytes 884744 | tf_op jit(solution)/shard_map/ppermute | solution.py:354
  82.6 2.0 %collective-permute-start.27 = (bf16[96,1536]{1,0:T(8,128)(2,1)}, bf16[96,1536]{1,0:T(8,128)(2,1)}, u32[]{:S(2)}, u32[]{:S(2)}) collective-permute-start(bf16[96,1536]{1,0:T(8,128)(2,1)} %collective-permute-done.26.rest_11_), channel_id=1, source_target_pairs={{0,4},{2,6},{4,0},{6,2},{8,12},{10,14},{12,8},{14,10},{1,5},{3,7},... | collective-permute-start | bytes 884744 | tf_op jit(solution)/shard_map/ppermute | solution.py:351
  85.2 3.4 %collective-permute-start.14 = (bf16[384,384]{1,0:T(8,128)(2,1)S(1)}, bf16[384,384]{1,0:T(8,128)(2,1)}, u32[]{:S(2)}, u32[]{:S(2)}) collective-permute-start(bf16[384,384]{1,0:T(8,128)(2,1)S(1)} %attend.3), channel_id=1, source_target_pairs={{0,8},{2,10},{4,12},{6,14},{8,0},{10,2},{12,4},{14,6},{1,9},{3,11}... | collective-permute-start | bytes 884744 | tf_op jit(solution)/shard_map/ppermute | solution.py:351
  89.5 3.8 %attend.2.a_own = bf16[384,384]{1,0:T(8,128)(2,1)S(1)} custom-call(s32[2]{0:T(128)S(1)} %pad_add_fusion.1.info, bf16[384,768]{1,0:T(8,128)(2,1)S(1)} %copy-done, bf16[384,384]{1,0:T(8,128)(2,1)S(1)} %get-tuple-element.19.refs_0_, bf16[384,384]{1,0:T(8,128)(2,1)S(1)} %get-tuple-element.17.refs_1_, bf16[384,384]{1,0:T(8,128)(2,1)S(1)} %collective-permute-done.refs_2_, ...), custom_call_target="tpu_custom_call" | custom-call | flops 1056964608 | bytes 3538944 | tf_op jit(solution)/shard_map/attend/pallas_call | solution.py:210
  94.4 2.0 %collective-permute-done.27.rest_12_ = bf16[96,1536]{1,0:T(8,128)(2,1)} collective-permute-done((bf16[96,1536]{1,0:T(8,128)(2,1)}, bf16[96,1536]{1,0:T(8,128)(2,1)}, u32[]{:S(2)}, u32[]{:S(2)}) %collective-permute-start.27) | collective-permute-done | bytes 294944 | tf_op jit(solution)/shard_map/ppermute | solution.py:351
  97.1 1.7 %collective-permute-start.29 = (bf16[96,1536]{1,0:T(8,128)(2,1)}, bf16[96,1536]{1,0:T(8,128)(2,1)S(1)}, u32[]{:S(2)}, u32[]{:S(2)}) collective-permute-start(bf16[96,1536]{1,0:T(8,128)(2,1)} %collective-permute-done.27.rest_12_), channel_id=1, source_target_pairs={{0,2},{2,0},{4,6},{6,4},{8,10},{10,8},{12,14},{14,12},{1,3},{3,1},... | collective-permute-start | bytes 884744 | tf_op jit(solution)/shard_map/ppermute | solution.py:351
  99.3 4.9 %collective-permute-done.22.rest_7_ = bf16[96,1536]{1,0:T(8,128)(2,1)S(1)} collective-permute-done((bf16[96,1536]{1,0:T(8,128)(2,1)}, bf16[96,1536]{1,0:T(8,128)(2,1)S(1)}, u32[]{:S(2)}, u32[]{:S(2)}) %collective-permute-start.22) | collective-permute-done | bytes 294944 | tf_op jit(solution)/shard_map/ppermute | solution.py:351
  104.3 5.8 %collective-permute-done.29.rest_14_ = bf16[96,1536]{1,0:T(8,128)(2,1)S(1)} collective-permute-done((bf16[96,1536]{1,0:T(8,128)(2,1)}, bf16[96,1536]{1,0:T(8,128)(2,1)S(1)}, u32[]{:S(2)}, u32[]{:S(2)}) %collective-permute-start.29) | collective-permute-done | bytes 294944 | tf_op jit(solution)/shard_map/ppermute | solution.py:351
  113.3 5.2 %project.1 = (f32[384,1536]{1,0:T(8,128)S(1)}, bf16[384,1536]{1,0:T(8,128)(2,1)}, f32[384,128]{1,0:T(8,128)S(1)}) custom-call(s32[4]{0:T(128)S(1)} %pad_add_fusion.info, bf16[384,384]{1,0:T(8,128)(2,1)S(1)} %attend.2.a_own, bf16[384,384]{1,0:T(8,128)(2,1)} %collective-permute-done.14.a_ret, bf16[384,384]{1,0:T(8,128)(2,1)S(1)} %collective-permute-done.15.x_own, ...), custom_call_target="tpu_custom_call" | custom-call | flops 1811939328 | bytes 9437184 | tf_op jit(solution)/shard_map/project/pallas_call | solution.py:267
  118.5 1.4 %collective-permute-done.30.other = f32[384,128]{1,0:T(8,128)S(1)} collective-permute-done((f32[384,128]{1,0:T(8,128)S(1)}, f32[384,128]{1,0:T(8,128)S(1)}, u32[]{:S(2)}, u32[]{:S(2)}) %collective-permute-start.30) | collective-permute-done | bytes 196640 | tf_op jit(solution)/shard_map/ppermute | solution.py:354
  120.0 1.9 %normalize.1 = bf16[384,1536]{1,0:T(8,128)(2,1)} custom-call(s32[4]{0:T(128)S(1)} %pad_add_fusion.info, f32[384,1536]{1,0:T(8,128)S(1)} %get-tuple-element.13.mixed, f32[384,128]{1,0:T(8,128)S(1)} %get-tuple-element.14.mine, f32[384,128]{1,0:T(8,128)S(1)} %collective-permute-done.30.other, f32[1,3072]{1,0:T(1,128)S(1)} %bitcast.7, f32[1,3072]{1,0:T(1,128)S(1)} %bitcast.8), custom_call_target="tpu_custom_call" | custom-call | flops 3538944 | bytes 3538944 | tf_op jit(solution)/shard_map/normalize/pallas_call | solution.py:319
  (86 shorter events, 20.7 us)
Async XLA Ops:
  1.9 44.2 %copy-start = (bf16[384,768]{1,0:T(8,128)(2,1)S(1)}, bf16[384,768]{1,0:T(8,128)(2,1)}, u32[]{:S(2)}) copy-start(bf16[384,768]{1,0:T(8,128)(2,1)} %query.1) | copy-start | bytes 1769476
  1.9 19.2 %collective-permute-start.6 = (bf16[384,384]{1,0:T(8,128)(2,1)S(1)}, bf16[384,384]{1,0:T(8,128)(2,1)S(1)}, u32[]{:S(2)}, u32[]{:S(2)}) collective-permute-start(bf16[384,384]{1,0:T(8,128)(2,1)S(1)} %get-tuple-element.16), channel_id=1, source_target_pairs={{0,8},{2,10},{4,12},{6,14},{8,0},{10,2},{12,4},{14,6},{1,9},{3,11}... | collective-permute-start | bytes 884744 | tf_op jit(solution)/shard_map/ppermute | solution.py:351
  6.8 15.6 %collective-permute-start.17 = (bf16[96,1536]{1,0:T(8,128)(2,1)}, bf16[96,1536]{1,0:T(8,128)(2,1)}, u32[]{:S(2)}, u32[]{:S(2)}) collective-permute-start(bf16[96,1536]{1,0:T(8,128)(2,1)} %constant_dynamic-slice_fusion), channel_id=1, source_target_pairs={{0,4},{2,6},{4,0},{6,2},{8,12},{10,14},{12,8},{14,10},{1,5},{3,7},... | collective-permute-start | bytes 884744 | tf_op jit(solution)/shard_map/ppermute | solution.py:351
  8.4 30.8 %collective-permute-start.5 = (bf16[384,384]{1,0:T(8,128)(2,1)S(1)}, bf16[384,384]{1,0:T(8,128)(2,1)S(1)}, u32[]{:S(2)}, u32[]{:S(2)}) collective-permute-start(bf16[384,384]{1,0:T(8,128)(2,1)S(1)} %get-tuple-element.18), channel_id=1, source_target_pairs={{0,8},{2,10},{4,12},{6,14},{8,0},{10,2},{12,4},{14,6},{1,9},{3,11}... | collective-permute-start | bytes 884744 | tf_op jit(solution)/shard_map/ppermute | solution.py:351
  8.8 32.2 %collective-permute-start = (bf16[384,384]{1,0:T(8,128)(2,1)S(1)}, bf16[384,384]{1,0:T(8,128)(2,1)S(1)}, u32[]{:S(2)}, u32[]{:S(2)}) collective-permute-start(bf16[384,384]{1,0:T(8,128)(2,1)S(1)} %get-tuple-element.19.refs_0_), channel_id=1, source_target_pairs={{0,2},{2,0},{4,6},{6,4},{8,10},{10,8},{12,14},{14,12},{1,3},{3,1},... | collective-permute-start | bytes 884744 | tf_op jit(solution)/shard_map/ppermute | solution.py:351
  21.1 23.7 %collective-permute-start.12 = (bf16[96,1536]{1,0:T(8,128)(2,1)}, bf16[96,1536]{1,0:T(8,128)(2,1)}, u32[]{:S(2)}, u32[]{:S(2)}) collective-permute-start(bf16[96,1536]{1,0:T(8,128)(2,1)} %constant_dynamic-slice_fusion), channel_id=1, source_target_pairs={{0,8},{2,10},{4,12},{6,14},{8,0},{10,2},{12,4},{14,6},{1,9},{3,11}... | collective-permute-start | bytes 884744 | tf_op jit(solution)/shard_map/ppermute | solution.py:351
  21.1 25.0 %collective-permute-start.3 = (bf16[384,384]{1,0:T(8,128)(2,1)S(1)}, bf16[384,384]{1,0:T(8,128)(2,1)S(1)}, u32[]{:S(2)}, u32[]{:S(2)}) collective-permute-start(bf16[384,384]{1,0:T(8,128)(2,1)S(1)} %get-tuple-element.17.refs_1_), channel_id=1, source_target_pairs={{2,6},{4,0},{10,14},{12,8},{3,7},{5,1},{11,15},{13,9},{18,22},{20,... | collective-permute-start | bytes 884744 | tf_op jit(solution)/shard_map/ppermute | solution.py:358
  22.4 26.7 %collective-permute-start.1 = (bf16[384,384]{1,0:T(8,128)(2,1)S(1)}, bf16[384,384]{1,0:T(8,128)(2,1)S(1)}, u32[]{:S(2)}, u32[]{:S(2)}) collective-permute-start(bf16[384,384]{1,0:T(8,128)(2,1)S(1)} %get-tuple-element.17.refs_1_), channel_id=1, source_target_pairs={{0,2},{2,0},{4,6},{6,4},{8,10},{10,8},{12,14},{14,12},{1,3},{3,1},... | collective-permute-start | bytes 884744 | tf_op jit(solution)/shard_map/ppermute | solution.py:351
  39.2 11.8 %collective-permute-start.7 = (bf16[384,384]{1,0:T(8,128)(2,1)S(1)}, bf16[384,384]{1,0:T(8,128)(2,1)S(1)}, u32[]{:S(2)}, u32[]{:S(2)}) collective-permute-start(bf16[384,384]{1,0:T(8,128)(2,1)S(1)} %collective-permute-done.5.refs_6_), channel_id=1, source_target_pairs={{0,2},{2,0},{4,6},{6,4},{8,10},{10,8},{12,14},{14,12},{1,3},{3,1},... | collective-permute-start | bytes 884744 | tf_op jit(solution)/shard_map/ppermute | solution.py:351
  41.0 11.3 %collective-permute-start.2 = (bf16[384,384]{1,0:T(8,128)(2,1)S(1)}, bf16[384,384]{1,0:T(8,128)(2,1)S(1)}, u32[]{:S(2)}, u32[]{:S(2)}) collective-permute-start(bf16[384,384]{1,0:T(8,128)(2,1)S(1)} %collective-permute-done.refs_2_), channel_id=1, source_target_pairs={{0,4},{6,2},{8,12},{14,10},{1,5},{7,3},{9,13},{15,11},{16,20},{22,... | collective-permute-start | bytes 884744 | tf_op jit(solution)/shard_map/ppermute | solution.py:358
  44.8 11.0 %collective-permute-start.10 = (bf16[384,384]{1,0:T(8,128)(2,1)S(1)}, bf16[384,384]{1,0:T(8,128)(2,1)S(1)}, u32[]{:S(2)}, u32[]{:S(2)}) collective-permute-start(bf16[384,384]{1,0:T(8,128)(2,1)S(1)} %collective-permute-done.6.refs_7_), channel_id=1, source_target_pairs={{2,6},{4,0},{10,14},{12,8},{3,7},{5,1},{11,15},{13,9},{18,22},{20,... | collective-permute-start | bytes 884744 | tf_op jit(solution)/shard_map/ppermute | solution.py:358
  46.1 11.5 %collective-permute-start.8 = (bf16[384,384]{1,0:T(8,128)(2,1)S(1)}, bf16[384,384]{1,0:T(8,128)(2,1)S(1)}, u32[]{:S(2)}, u32[]{:S(2)}) collective-permute-start(bf16[384,384]{1,0:T(8,128)(2,1)S(1)} %collective-permute-done.6.refs_7_), channel_id=1, source_target_pairs={{0,2},{2,0},{4,6},{6,4},{8,10},{10,8},{12,14},{14,12},{1,3},{3,1},... | collective-permute-start | bytes 884744 | tf_op jit(solution)/shard_map/ppermute | solution.py:351
  49.1 13.7 %collective-permute-start.4 = (bf16[384,384]{1,0:T(8,128)(2,1)S(1)}, bf16[384,384]{1,0:T(8,128)(2,1)S(1)}, u32[]{:S(2)}, u32[]{:S(2)}) collective-permute-start(bf16[384,384]{1,0:T(8,128)(2,1)S(1)} %collective-permute-done.3), channel_id=1, source_target_pairs={{0,2},{6,4},{8,10},{14,12},{1,3},{7,5},{9,11},{15,13},{16,18},{22,... | collective-permute-start | bytes 884744 | tf_op jit(solution)/shard_map/ppermute | solution.py:358
  51.0 15.0 %collective-permute-start.9 = (bf16[384,384]{1,0:T(8,128)(2,1)S(1)}, bf16[384,384]{1,0:T(8,128)(2,1)S(1)}, u32[]{:S(2)}, u32[]{:S(2)}) collective-permute-start(bf16[384,384]{1,0:T(8,128)(2,1)S(1)} %collective-permute-done.7.refs_8_), channel_id=1, source_target_pairs={{0,4},{6,2},{8,12},{14,10},{1,5},{7,3},{9,13},{15,11},{16,20},{22,... | collective-permute-start | bytes 884744 | tf_op jit(solution)/shard_map/ppermute | solution.py:358
  52.4 16.3 %collective-permute-start.13 = (bf16[384,384]{1,0:T(8,128)(2,1)S(1)}, bf16[384,384]{1,0:T(8,128)(2,1)S(1)}, u32[]{:S(2)}, u32[]{:S(2)}) collective-permute-start(bf16[384,384]{1,0:T(8,128)(2,1)S(1)} %constant_dynamic-slice_fusion.1), channel_id=1, source_target_pairs={{0,8},{2,10},{4,12},{6,14},{8,0},{10,2},{12,4},{14,6},{1,9},{3,11}... | collective-permute-start | bytes 884744 | tf_op jit(solution)/shard_map/ppermute | solution.py:351
  55.8 14.4 %collective-permute-start.11 = (bf16[384,384]{1,0:T(8,128)(2,1)S(1)}, bf16[384,384]{1,0:T(8,128)(2,1)S(1)}, u32[]{:S(2)}, u32[]{:S(2)}) collective-permute-start(bf16[384,384]{1,0:T(8,128)(2,1)S(1)} %collective-permute-done.10), channel_id=1, source_target_pairs={{0,2},{6,4},{8,10},{14,12},{1,3},{7,5},{9,11},{15,13},{16,18},{22,... | collective-permute-start | bytes 884744 | tf_op jit(solution)/shard_map/ppermute | solution.py:358
  58.3 22.5 %collective-permute-start.23 = (bf16[96,1536]{1,0:T(8,128)(2,1)}, bf16[96,1536]{1,0:T(8,128)(2,1)}, u32[]{:S(2)}, u32[]{:S(2)}) collective-permute-start(bf16[96,1536]{1,0:T(8,128)(2,1)} %collective-permute-done.17.rest_1_), channel_id=1, source_target_pairs={{0,16},{16,0},{1,17},{17,1},{2,18},{18,2},{3,19},{19,3},{4,20},{20... | collective-permute-start | bytes 884744 | tf_op jit(solution)/shard_map/ppermute | solution.py:354
  63.5 17.6 %collective-permute-start.18 = (bf16[96,1536]{1,0:T(8,128)(2,1)}, bf16[96,1536]{1,0:T(8,128)(2,1)}, u32[]{:S(2)}, u32[]{:S(2)}) collective-permute-start(bf16[96,1536]{1,0:T(8,128)(2,1)} %constant_dynamic-slice_fusion), channel_id=1, source_target_pairs={{0,2},{2,0},{4,6},{6,4},{8,10},{10,8},{12,14},{14,12},{1,3},{3,1},... | collective-permute-start | bytes 884744 | tf_op jit(solution)/shard_map/ppermute | solution.py:351
  66.7 15.9 %collective-permute-start.26 = (bf16[96,1536]{1,0:T(8,128)(2,1)}, bf16[96,1536]{1,0:T(8,128)(2,1)}, u32[]{:S(2)}, u32[]{:S(2)}) collective-permute-start(bf16[96,1536]{1,0:T(8,128)(2,1)} %collective-permute-done.12.rest_4_), channel_id=1, source_target_pairs={{0,16},{16,0},{1,17},{17,1},{2,18},{18,2},{3,19},{19,3},{4,20},{20... | collective-permute-start | bytes 884744 | tf_op jit(solution)/shard_map/ppermute | solution.py:354
  69.5 15.2 %collective-permute-start.21 = (bf16[96,1536]{1,0:T(8,128)(2,1)}, bf16[96,1536]{1,0:T(8,128)(2,1)}, u32[]{:S(2)}, u32[]{:S(2)}) collective-permute-start(bf16[96,1536]{1,0:T(8,128)(2,1)} %collective-permute-done.12.rest_4_), channel_id=1, source_target_pairs={{0,2},{2,0},{4,6},{6,4},{8,10},{10,8},{12,14},{14,12},{1,3},{3,1},... | collective-permute-start | bytes 884744 | tf_op jit(solution)/shard_map/ppermute | solution.py:351
  71.0 14.2 %collective-permute-start.20 = (bf16[96,1536]{1,0:T(8,128)(2,1)}, bf16[96,1536]{1,0:T(8,128)(2,1)}, u32[]{:S(2)}, u32[]{:S(2)}) collective-permute-start(bf16[96,1536]{1,0:T(8,128)(2,1)} %collective-permute-done.12.rest_4_), channel_id=1, source_target_pairs={{0,4},{2,6},{4,0},{6,2},{8,12},{10,14},{12,8},{14,10},{1,5},{3,7},... | collective-permute-start | bytes 884744 | tf_op jit(solution)/shard_map/ppermute | solution.py:351
  80.8 12.5 %collective-permute-start.19 = (bf16[96,1536]{1,0:T(8,128)(2,1)}, bf16[96,1536]{1,0:T(8,128)(2,1)}, u32[]{:S(2)}, u32[]{:S(2)}) collective-permute-start(bf16[96,1536]{1,0:T(8,128)(2,1)} %collective-permute-done.17.rest_1_), channel_id=1, source_target_pairs={{0,2},{2,0},{4,6},{6,4},{8,10},{10,8},{12,14},{14,12},{1,3},{3,1},... | collective-permute-start | bytes 884744 | tf_op jit(solution)/shard_map/ppermute | solution.py:351
  81.1 12.3 %collective-permute-start.24 = (bf16[96,1536]{1,0:T(8,128)(2,1)}, bf16[96,1536]{1,0:T(8,128)(2,1)S(1)}, u32[]{:S(2)}, u32[]{:S(2)}) collective-permute-start(bf16[96,1536]{1,0:T(8,128)(2,1)} %collective-permute-done.18.rest_2_), channel_id=1, source_target_pairs={{0,16},{16,0},{1,17},{17,1},{2,18},{18,2},{3,19},{19,3},{4,20},{20... | collective-permute-start | bytes 884744 | tf_op jit(solution)/shard_map/ppermute | solution.py:354
  82.6 13.7 %collective-permute-start.27 = (bf16[96,1536]{1,0:T(8,128)(2,1)}, bf16[96,1536]{1,0:T(8,128)(2,1)}, u32[]{:S(2)}, u32[]{:S(2)}) collective-permute-start(bf16[96,1536]{1,0:T(8,128)(2,1)} %collective-permute-done.26.rest_11_), channel_id=1, source_target_pairs={{0,4},{2,6},{4,0},{6,2},{8,12},{10,14},{12,8},{14,10},{1,5},{3,7},... | collective-permute-start | bytes 884744 | tf_op jit(solution)/shard_map/ppermute | solution.py:351
  84.6 11.8 %collective-permute-start.28 = (bf16[96,1536]{1,0:T(8,128)(2,1)}, bf16[96,1536]{1,0:T(8,128)(2,1)S(1)}, u32[]{:S(2)}, u32[]{:S(2)}) collective-permute-start(bf16[96,1536]{1,0:T(8,128)(2,1)} %collective-permute-done.21.rest_6_), channel_id=1, source_target_pairs={{0,16},{16,0},{1,17},{17,1},{2,18},{18,2},{3,19},{19,3},{4,20},{20... | collective-permute-start | bytes 884744 | tf_op jit(solution)/shard_map/ppermute | solution.py:354
  85.2 14.1 %collective-permute-start.14 = (bf16[384,384]{1,0:T(8,128)(2,1)S(1)}, bf16[384,384]{1,0:T(8,128)(2,1)}, u32[]{:S(2)}, u32[]{:S(2)}) collective-permute-start(bf16[384,384]{1,0:T(8,128)(2,1)S(1)} %attend.3), channel_id=1, source_target_pairs={{0,8},{2,10},{4,12},{6,14},{8,0},{10,2},{12,4},{14,6},{1,9},{3,11}... | collective-permute-start | bytes 884744 | tf_op jit(solution)/shard_map/ppermute | solution.py:351
  93.4 10.9 %collective-permute-start.15 = (bf16[384,384]{1,0:T(8,128)(2,1)S(1)}, bf16[384,384]{1,0:T(8,128)(2,1)S(1)}, u32[]{:S(2)}, u32[]{:S(2)}) collective-permute-start(bf16[384,384]{1,0:T(8,128)(2,1)S(1)} %attend.2.a_own), channel_id=1, source_target_pairs={{0,1},{1,0},{2,3},{3,2},{4,5},{5,4},{6,7},{7,6},{8,9},{9,8},{10,11... | collective-permute-start | bytes 884744 | tf_op jit(solution)/shard_map/ppermute | solution.py:354
  94.2 10.1 %collective-permute-start.22 = (bf16[96,1536]{1,0:T(8,128)(2,1)}, bf16[96,1536]{1,0:T(8,128)(2,1)S(1)}, u32[]{:S(2)}, u32[]{:S(2)}) collective-permute-start(bf16[96,1536]{1,0:T(8,128)(2,1)} %collective-permute-done.20.rest_5_), channel_id=1, source_target_pairs={{0,2},{2,0},{4,6},{6,4},{8,10},{10,8},{12,14},{14,12},{1,3},{3,1},... | collective-permute-start | bytes 884744 | tf_op jit(solution)/shard_map/ppermute | solution.py:351
  96.3 7.9 %collective-permute-start.25 = (bf16[96,1536]{1,0:T(8,128)(2,1)}, bf16[96,1536]{1,0:T(8,128)(2,1)S(1)}, u32[]{:S(2)}, u32[]{:S(2)}) collective-permute-start(bf16[96,1536]{1,0:T(8,128)(2,1)} %collective-permute-done.19.rest_3_), channel_id=1, source_target_pairs={{0,16},{16,0},{1,17},{17,1},{2,18},{18,2},{3,19},{19,3},{4,20},{20... | collective-permute-start | bytes 884744 | tf_op jit(solution)/shard_map/ppermute | solution.py:354
  97.1 13.0 %collective-permute-start.29 = (bf16[96,1536]{1,0:T(8,128)(2,1)}, bf16[96,1536]{1,0:T(8,128)(2,1)S(1)}, u32[]{:S(2)}, u32[]{:S(2)}) collective-permute-start(bf16[96,1536]{1,0:T(8,128)(2,1)} %collective-permute-done.27.rest_12_), channel_id=1, source_target_pairs={{0,2},{2,0},{4,6},{6,4},{8,10},{10,8},{12,14},{14,12},{1,3},{3,1},... | collective-permute-start | bytes 884744 | tf_op jit(solution)/shard_map/ppermute | solution.py:351
  99.3 10.8 %collective-permute-start.16 = (bf16[384,384]{1,0:T(8,128)(2,1)}, bf16[384,384]{1,0:T(8,128)(2,1)S(1)}, u32[]{:S(2)}, u32[]{:S(2)}) collective-permute-start(bf16[384,384]{1,0:T(8,128)(2,1)} %collective-permute-done.14.a_ret), channel_id=1, source_target_pairs={{0,1},{1,0},{2,3},{3,2},{4,5},{5,4},{6,7},{7,6},{8,9},{9,8},{10,11... | collective-permute-start | bytes 884744 | tf_op jit(solution)/shard_map/ppermute | solution.py:354
  118.5 1.4 %collective-permute-start.30 = (f32[384,128]{1,0:T(8,128)S(1)}, f32[384,128]{1,0:T(8,128)S(1)}, u32[]{:S(2)}, u32[]{:S(2)}) collective-permute-start(f32[384,128]{1,0:T(8,128)S(1)} %get-tuple-element.14.mine), channel_id=1, source_target_pairs={{0,1},{1,0},{2,3},{3,2},{4,5},{5,4},{6,7},{7,6},{8,9},{9,8},{10,11... | collective-permute-start | bytes 589832 | tf_op jit(solution)/shard_map/ppermute | solution.py:354
  (22 other events, 80.5 us)

commit v2 on v1

--- a/solution.py
+++ b/solution.py
@@ -110,21 +110,15 @@
     return functools.reduce(op, [x[:, c : c + HD] for c in range(0, x.shape[1], HD)])
 
 
-def attention_kernel(info, query, *refs, kinds, own, resume, final):
-    refs = list(refs)
-    parts = []
-    for stacked, far in kinds:
-        if stacked:
-            ref = refs.pop(0)
-            parts.append((ref.at[0], ref.at[1], far))
-        else:
-            parts.append((refs.pop(0), refs.pop(0), far))
-    before = [refs.pop(0) for _ in range(3)] if resume else None
+def attention_kernel(info, query, *refs, returned):
+    out, logs = refs[6:]
+    parts = tuple((refs[i], refs[i + 1], i == 4) for i in (0, 2, 4))
     rows = query.shape[0]
     tiles = rows // TILE
-    heads = refs[0].shape[1] // HD
+    heads = out.shape[1] // HD
     away = jnp.where(info[1] == 1, jnp.float32(0), jnp.float32(AWAY))
-    units = list(itertools.product(range(heads), range(tiles)))
+    lane = lax.broadcasted_iota(jnp.int32, (TILE, HD), 1)
+    log_of = [jnp.zeros((TILE, HD), jnp.float32) for _ in range(tiles)]
 
     def place(head, tile):
         begin = max(tile - 1, 0) * TILE
@@ -134,13 +128,9 @@
 
     def score(head, tile):
         here, seen, feats = place(head, tile)
-        if own:
-            q = query[here, pl.ds(pl.multiple_of((info[0] * heads + head) * HD, HD), HD)]
-        else:
-            q = query[here, feats]
         return [
             lax.dot_general(
-                q,
+                query[here, feats],
                 keys[seen, feats],
                 (((1,), (1,)), ((), ())),
                 preferred_element_type=jnp.float32,
@@ -156,89 +146,152 @@
         return jnp.max(functools.reduce(jnp.maximum, tops), axis=1, keepdims=True)
 
     def gather(head, tile, scores, top):
-        here, seen, feats = place(head, tile)
+        _, seen, feats = place(head, tile)
         acc = jnp.zeros((TILE, HD), jnp.float32)
         total = jnp.zeros((TILE, HD), jnp.float32)
-        if resume:
-            old = before[2][here, feats][:, 0:1]
-            top = jnp.maximum(top, old)
-            keep = jnp.exp2((old - top) * EXP2_SCALE)
-            acc = before[0][here, feats] * keep
         for s, (_, values, far) in zip(scores, parts):
             p = jnp.exp2((s - (top - away if far else top)) * EXP2_SCALE)
             total = total + lane_blocks(p, jnp.add)
             acc = acc + jnp.dot(
                 p.astype(jnp.bfloat16), values[seen, feats], preferred_element_type=jnp.float32
             )
-        total = jnp.sum(total, axis=1, keepdims=True)
-        if resume:
-            total = total + before[1][here, feats][:, 0:1] * keep
-        return acc, total, top
-
-    def write(head, tile, acc, total, top):
-        here, _, feats = place(head, tile)
-        if final:
-            refs[0][here, feats] = (acc / total).astype(jnp.bfloat16)
-        else:
-            refs[0][here, feats] = acc
-            refs[1][here, feats] = jnp.broadcast_to(total, (TILE, HD))
-            refs[2][here, feats] = jnp.broadcast_to(top, (TILE, HD))
-
-    for first in range(0, len(units), GROUP):
-        group = units[first : first + GROUP]
+        return acc, jnp.sum(total, axis=1, keepdims=True)
+
+    units = list(itertools.product(range(heads), range(tiles)))
+    for start in range(0, len(units), GROUP):
+        group = units[start : start + GROUP]
         scores = [score(*unit) for unit in group]
         tops = [highest(s) for s in scores]
         done = [gather(*unit, s, top) for unit, s, top in zip(group, scores, tops)]
-        for unit, result in zip(group, done):
-            write(*unit, *result)
-
-
-def attention(info, query, own, parts, before=(), final=True):
-    rows = query.shape[0]
-    cols = parts[0][0][0].shape[-1]
-    heads = cols // HD
+        for (head, tile), top, (acc, total) in zip(group, tops, done):
+            here, _, feats = place(head, tile)
+            out[here, feats] = (acc / total).astype(out.dtype)
+            log = top * EXP2_SCALE + jnp.log2(total)
+            log_of[tile] = jnp.where(lane == head, log, log_of[tile])
+    for tile in range(tiles):
+        here = slice(tile * TILE, (tile + 1) * TILE)
+        if returned:
+            logs[:, here] = jnp.transpose(log_of[tile])[: logs.shape[0], :]
+        else:
+            logs[here, :] = log_of[tile]
+
+
+def attention(info, query, parts, returned):
+    rows, cols = query.shape
     vmem = pl.BlockSpec(memory_space=pltpu.VMEM)
-    operands = [x for given, far in parts for x in given] + list(before)
-    kinds = tuple((len(given) == 1, far) for given, far in parts)
-    pairs = rows * 7 * TILE * len(parts) * heads // 3
-    if final:
-        out_shape = jax.ShapeDtypeStruct((rows, cols), jnp.bfloat16)
-        out_specs = vmem
+    pairs = rows * 7 * TILE * cols // HD
+    if returned:
+        kind, log_shape = jnp.bfloat16, (8, rows)
     else:
-        out_shape = [jax.ShapeDtypeStruct((rows, cols), jnp.float32)] * 3
-        out_specs = [vmem] * 3
+        kind, log_shape = jnp.float32, (rows, HD)
     return pl.pallas_call(
-        functools.partial(
-            attention_kernel, kinds=kinds, own=own, resume=bool(before), final=final
-        ),
-        in_specs=[pl.BlockSpec(memory_space=pltpu.SMEM)] + [vmem] * (1 + len(operands)),
-        out_specs=out_specs,
-        out_shape=out_shape,
+        functools.partial(attention_kernel, returned=returned),
+        in_specs=[pl.BlockSpec(memory_space=pltpu.SMEM)] + [vmem] * (1 + len(parts)),
+        out_specs=[vmem] * 2,
+        out_shape=[
+            jax.ShapeDtypeStruct((rows, cols), kind),
+            jax.ShapeDtypeStruct(log_shape, jnp.float32),
+        ],
         compiler_params=pltpu.CompilerParams(vmem_limit_bytes=12 << 20),
         cost_estimate=pl.CostEstimate(
-            flops=pairs * HD * 4, transcendentals=pairs, bytes_accessed=rows * cols * 4 * len(parts)
+            flops=pairs * HD * 4, transcendentals=pairs, bytes_accessed=rows * cols * 16
         ),
         name="attend",
-    )(info, query, *operands)
-
-
-def project_kernel(info, a_own, a_ret, x_own, x_ret, stream, *rest, places):
+    )(info, query, *parts)
+
+
+def merge_kernel(mine, my_logs, got, got_logs, out):
+    rows, cols = out.shape
+    heads = cols // HD
+    for tile in range(rows // TILE):
+        here = slice(tile * TILE, (tile + 1) * TILE)
+        fill = jnp.zeros((HD - got_logs.shape[0], TILE), jnp.float32)
+        other = jnp.transpose(jnp.concatenate([got_logs[:, here], fill], 0))
+        logs = my_logs[here, :]
+        for head in range(heads):
+            feats = slice(head * HD, (head + 1) * HD)
+            gap = other[:, head : head + 1] - logs[:, head : head + 1]
+            share = 1.0 / (1.0 + jnp.exp2(gap))
+            far = got[here, feats].astype(jnp.float32)
+            out[here, feats] = (mine[here, feats] * share + far * (1.0 - share)).astype(out.dtype)
+
+
+def merge(mine, my_logs, got, got_logs):
+    vmem = pl.BlockSpec(memory_space=pltpu.VMEM)
+    return pl.pallas_call(
+        merge_kernel,
+        in_specs=[vmem] * 4,
+        out_specs=vmem,
+        out_shape=jax.ShapeDtypeStruct(got.shape, got.dtype),
+        compiler_params=pltpu.CompilerParams(vmem_limit_bytes=6 << 20),
+        cost_estimate=pl.CostEstimate(
+            flops=got.size * 4, transcendentals=got.size // HD, bytes_accessed=got.size * 8
+        ),
+        name="merge",
+    )(mine, my_logs, got, got_logs)
+
+
+def weight_rows(info, place):
+    flip, half, size = place
+    row = (info[1] ^ flip) * size
+    if half is not None:
+        row = row * 2 + (info[2] if half == 0 else 1 - info[2]) * size
+    return pl.ds(pl.multiple_of(row, 32), size)
+
+
+def stage_kernel(info, *rest, places):
+    pieces, (weight, sems) = rest[: len(places)], rest[len(places) :]
+    copies = [
+        pltpu.make_async_copy(piece, weight.at[weight_rows(info, place)], sems.at[i])
+        for i, (piece, place) in enumerate(zip(pieces, places))
+    ]
+    for copy in copies:
+        copy.start()
+    for copy in copies:
+        copy.wait()
+
+
+def stage(info, pieces, places, depth):
+    width = pieces[0].shape[1]
+    return pl.pallas_call(
+        functools.partial(stage_kernel, places=places),
+        in_specs=[pl.BlockSpec(memory_space=pltpu.SMEM)]
+        + [pl.BlockSpec(memory_space=pl.ANY)] * len(pieces),
+        out_specs=pl.BlockSpec(memory_space=pltpu.VMEM),
+        out_shape=jax.ShapeDtypeStruct((depth, width), pieces[0].dtype),
+        scratch_shapes=[pltpu.SemaphoreType.DMA((len(pieces),))],
+        compiler_params=pltpu.CompilerParams(vmem_limit_bytes=8 << 20),
+        cost_estimate=pl.CostEstimate(
+            flops=0, transcendentals=0, bytes_accessed=depth * width * 4
+        ),
+        name="stage",
+    )(info, *pieces)
+
+
+def project_kernel(
+    info, a_low, a_high, x_low, x_high, stream, staged, *rest, places
+):
     pieces = rest[: len(places)]
-    mixed, stream_out, stats, weight, left = rest[len(places) :]
-    core, par, pos, vid = info[0], info[1], info[2], info[3]
-    cols = a_own.shape[1]
-    for ref, block in (
-        (a_own, core * 2 + par),
-        (a_ret, core * 2 + 1 - par),
-        (x_own, (1 - core) * 2 + par),
-        (x_ret, (1 - core) * 2 + 1 - par),
-    ):
-        left[:, pl.ds(pl.multiple_of(block * cols, HD), cols)] = ref[...]
-    for piece, (flip, half, size) in zip(pieces, places):
-        row = (pos ^ flip) * size
-        if half is not None:
-            row = row * 2 + (vid if half == 0 else 1 - vid) * size
-        weight[pl.ds(pl.multiple_of(row, 32), size), :] = piece[...]
+    mixed, stream_out, stats, weight, left, sems = rest[len(places) :]
+    core = info[0]
+    low, high = a_low.shape[1], a_high.shape[1]
+
+    def columns(owner, shift, size):
+        return pl.ds(pl.multiple_of(owner * (low + high) + shift, HD), size)
+
+    copies = [
+        pltpu.make_async_copy(piece, weight.at[weight_rows(info, place)], sems.at[i])
+        for i, (piece, place) in enumerate(zip(pieces, places))
+    ]
+    for ref, shift in ((x_low, 0), (x_high, low)):
+        where = columns(1 - core, shift, ref.shape[1])
+        copies.append(pltpu.make_async_copy(ref, left.at[:, where], sems.at[len(copies)]))
+    for copy in copies:
+        copy.start()
+    for ref, shift in ((a_low, 0), (a_high, low)):
+        left[:, columns(core, shift, ref.shape[1])] = ref[...]
+    for copy in copies:
+        copy.wait()
     rows, width = stream.shape
     step = width // 3
     total = jnp.zeros((rows, HD), jnp.float32)
@@ -260,31 +313,38 @@
     stats[...] = jnp.where(lane == 0, mean, square)
 
 
-def project(info, blocks, stream, pieces, places):
+def project(info, blocks, stream, staged, pieces, places):
     rows, width = stream.shape
-    depth = 4 * blocks[0].shape[1]
+    depth = staged.shape[0]
     vmem = pl.BlockSpec(memory_space=pltpu.VMEM)
+    anywhere = pl.BlockSpec(memory_space=pl.ANY)
     return pl.pallas_call(
         functools.partial(project_kernel, places=places),
-        in_specs=[pl.BlockSpec(memory_space=pltpu.SMEM)] + [vmem] * (5 + len(pieces)),
-        out_specs=[vmem] * 3,
+        in_specs=[pl.BlockSpec(memory_space=pltpu.SMEM)]
+        + [vmem] * 2
+        + [anywhere] * 2
+        + [vmem] * 2
+        + [anywhere] * len(pieces),
+        out_specs=[vmem] * 4,
         out_shape=[
             jax.ShapeDtypeStruct((rows, width), jnp.float32),
             jax.ShapeDtypeStruct((rows, width), jnp.bfloat16),
             jax.ShapeDtypeStruct((rows, HD), jnp.float32),
+            jax.ShapeDtypeStruct(staged.shape, staged.dtype),
         ],
         scratch_shapes=[
-            pltpu.VMEM((depth, width), jnp.bfloat16),
             pltpu.VMEM((rows, depth), jnp.bfloat16),
+            pltpu.SemaphoreType.DMA((len(pieces) + 2,)),
         ],
-        compiler_params=pltpu.CompilerParams(vmem_limit_bytes=24 << 20),
+        input_output_aliases={6: 3},
+        compiler_params=pltpu.CompilerParams(vmem_limit_bytes=14 << 20),
         cost_estimate=pl.CostEstimate(
             flops=2 * rows * depth * width,
             transcendentals=0,
             bytes_accessed=depth * width * 2 + rows * width * 8,
         ),
         name="project",
-    )(info, *blocks, stream, *pieces)
+    )(info, *blocks, stream, staged, *pieces)
 
 
 def norm_kernel(info, mixed, mine, other, scale, shift, out, held, sems):
@@ -333,10 +393,6 @@
     )(info, mixed, mine, other, scale_mod[None, :], shift_mod[None, :])
 
 
-def after(value, *done):
-    return lax.optimization_barrier((value,) + done)[0]
-
-
 def on_device_pair(query, key, value, stream, shift_mod, scale_mod, out_weight):
     count = lax.axis_size("seq")
     position = lax.axis_index("seq")
@@ -345,7 +401,6 @@
     par = position // HT
     height = position % HT
     relayed = jnp.where((height == 1) | (height == 2), 1, 0)
-    half_cols = query.shape[1] // 2
 
     def flip(x, mask):
         return lax.ppermute(x, "seq", [(i, i ^ mask) for i in range(count)])
@@ -357,70 +412,79 @@
         pairs = [(i, i ^ mask) for i in range(count) if i % HT in sources]
         return lax.ppermute(x, "seq", pairs)
 
-    def heads(x, which):
-        return lax.dynamic_slice_in_dim(x, which * half_cols, half_cols, 1)
-
-    give_k = heads(key, 1 - par)
-    own_k = heads(key, par)
-    own_v = heads(value, par)
-    give_v = heads(value, 1 - par)
-    give_q = heads(query, 1 - par)
     rows_half = out_weight.shape[0] // 2
     w_own = lax.dynamic_slice_in_dim(out_weight, vid * rows_half, rows_half, 0)
 
-    e_k = flip(give_k, HT)
-    y_ok = flip(own_k, 1)
+    half = query.shape[1] // HD // 2 * HD
+    q_low = query[:, :half]
+    key, value, late = lax.optimization_barrier((key, value, query, q_low))[:3]
+    k_low, v_low = (x[:, :half] for x in (key, value))
+    q_high, k_high, v_high = (x[:, half:] for x in (late, key, value))
+
+    e_low = flip(q_low, HT)
+    y_kl = flip(k_low, 1)
+    v_zl = some(v_low, 2, (1, 2))
+    y_vl = flip(v_low, 1)
+    w_t = flip(w_own, HT)
+    k_fl = some(y_kl, 2, (0, 3))
+    v_fl = some(v_zl, 1, (0, 3))
+    y_kh = flip(k_high, 1)
+    v_zh = some(v_high, 2, (1, 2))
+    e_high = flip(q_high, HT)
+    y_vh = flip(v_high, 1)
+    k_fh = some(y_kh, 2, (0, 3))
+    v_fh = some(v_zh, 1, (0, 3))
     w_z1 = flip(w_own, 2)
-    e_v = flip(give_v, HT)
-    y_ov = flip(own_v, 1)
-    ov_z = some(own_v, 2, (1, 2))
-    ok_far = some(y_ok, 2, (0, 3))
-    w_ya = flip(after(w_own, y_ov), 1)
-    ov_far = some(ov_z, 1, (0, 3))
-    y_k = flip(e_k, 1)
+    w_xd = swap(w_t, "video")
     w_xa = swap(w_z1, "video")
-    w_t = flip(after(w_own, e_v), HT)
-    y_v = flip(e_v, 1)
-    v_z = some(e_v, 2, (1, 2))
-    k_far = some(y_k, 2, (0, 3))
-    v_far = some(v_z, 1, (0, 3))
+    w_z2 = flip(w_t, 2)
+    w_ya = flip(w_own, 1)
+    w_yc = flip(w_t, 1)
+    w_z3 = flip(w_ya, 2)
+    w_yd = flip(w_z2, 1)
+    w_xe = swap(w_z2, "video")
     w_xb = swap(w_ya, "video")
-    w_yb = flip(after(w_z1, y_v), 1)
-    w_xc = swap(w_yb, "video")
-    w_z2 = flip(w_t, 2)
-    e_q = flip(after(give_q, w_t), HT)
-    w_xd = swap(w_t, "video")
-    w_yc = flip(w_t, 1)
-    w_yd = flip(w_z2, 1)
-    w_xe = flip(w_xd, 2)
-    w_xf = swap(w_yc, "video")
-    w_xg = flip(w_xe, 1)
+    w_yf = flip(w_xd, 1)
+    w_xc = swap(w_z3, "video")
+    w_xg = swap(w_yd, "video")
 
     info = jnp.stack([par, relayed]).astype(jnp.int32)
-    parts = (
-        ((own_k, own_v), False),
-        ((y_ok, y_ov), False),
-        ((ok_far, ov_far), True),
-        ((e_k, e_v), False),
-        ((y_k, y_v), False),
-        ((k_far, v_far), True),
+    parts_low = (k_low, v_low, y_kl, y_vl, k_fl, v_fl)
+    parts_high = (k_high, v_high, y_kh, y_vh, k_fh, v_fh)
+    give_low, logs_low = attention(info, e_low, parts_low, True)
+    r_low = flip(give_low, HT)
+    l_low = flip(logs_low, HT)
+    mine_low, mine_logs_low = attention(info, q_low, parts_low, False)
+    give_high, logs_high = attention(info, e_high, parts_high, True)
+    r_high = flip(give_high, HT)
+    l_high = flip(logs_high, HT)
+    mine_high, mine_logs_high = attention(info, q_high, parts_high, False)
+    a_low = merge(mine_low, mine_logs_low, r_low, l_low)
+    x_low = swap(a_low, "head")
+    a_high = merge(mine_high, mine_logs_high, r_high, l_high)
+    x_high = swap(a_high, "head")
+
+    n = rows_half
+    early = (
+        (out_weight, (0, None, 2 * n)),
+        (w_z1, (2, 0, n)),
+        (w_ya, (1, 0, n)),
+        (w_z3, (3, 0, n)),
+        (w_t, (4, 0, n)),
+        (w_z2, (6, 0, n)),
+        (w_yc, (5, 0, n)),
+        (w_yd, (7, 0, n)),
+        (w_xa, (2, 1, n)),
+        (w_xb, (1, 1, n)),
+        (w_xd, (4, 1, n)),
+        (w_xe, (6, 1, n)),
     )
-    out_other = attention(info, e_q, False, parts)
-    a_ret = flip(out_other, HT)
-    a_own = attention(info, query, True, parts)
-    x_own = swap(a_own, "head")
-    x_ret = swap(a_ret, "head")
-
-    n = rows_half
-    here = (w_z1, w_ya, w_yb, w_t, w_z2, w_yc, w_yd)
-    across = (w_xa, w_xb, w_xc, w_xd, w_xe, w_xf, w_xg)
-    flips = (2, 1, 3, 4, 6, 5, 7)
-    pieces = (out_weight,) + here + across
-    places = ((0, None, 2 * n),)
-    places += tuple((mask, half, n) for half in (0, 1) for mask in flips)
-    where = jnp.stack([core, par, position, vid]).astype(jnp.int32)
-    mixed, stream_out, stats = project(
-        where, (a_own, a_ret, x_own, x_ret), stream, pieces, places
+    last = ((w_xc, (3, 1, n)), (w_yf, (5, 1, n)), (w_xg, (7, 1, n)))
+    where = jnp.stack([core, position, vid]).astype(jnp.int32)
+    depth = 2 * n * count
+    staged = stage(where, *map(tuple, zip(*early)), depth)
+    mixed, stream_out, stats, _ = project(
+        where, (a_low, a_high, x_low, x_high), stream, staged, *map(tuple, zip(*last))
     )
     other = swap(stats, "head")
     normed = normalize(where, mixed, stats, other, scale_mod, shift_mod)
@@ -438,7 +502,7 @@
 
 
 def solution(mesh):
-    return jax.shard_map(
+    step = jax.shard_map(
         on_device,
         mesh=mesh,
         in_specs=(
@@ -453,3 +517,6 @@
         out_specs=(P(("video", "seq"), "head"), P(("video", "seq"), "head")),
         check_vma=False,
     )
+    if dict(mesh.shape) != PAIR:
+        return step
+    return step

time: 122 us -> 144 us (1.18)
  waiting for transfers between devices: 42.1 us -> 55 us
  Pallas kernels: 14.8 us -> 20.1 us
  starting transfers between devices: 47.9 us -> 52.5 us
    ppermute x8 -> x9, waiting for transfers between devices: 1.46 us -> 8.48 us  [swap(): return lax.ppermute(x, axis, [(0, 1), (1, 0)])]
    ppermute x17 -> x18, waiting for transfers between devices: 37.6 us -> 44 us  [flip(): return lax.ppermute(x, 'seq', [(i, i ^ mask) for i in range(count)])]
    pallas_call x2 -> x7, Pallas kernels: 7.65 us -> 13.4 us  [the longest x4 10 us: attention(): pl.pallas_call(functools.partial(attention_kernel, returned=returned), in...]
    ppermute x6, starting transfers between devices: 9.14 us -> 14.1 us  [some(): return lax.ppermute(x, 'seq', pairs)]
    unnamed x46 -> x50, local copies, waits for them, and re-layouts: 14 us -> 10.2 us
    slice x0 -> x4, local copies, waits for them, and re-layouts: none -> 3.22 us  [the longest x3 2.16 us: on_device_pair(): q_high, k_high, v_high = (x[:, half:] for x in (late, key, value))]
    ppermute x17 -> x18, starting transfers between devices: 33.6 us -> 31.2 us  [flip(): return lax.ppermute(x, 'seq', [(i, i ^ mask) for i in range(count)])]
    ppermute x8 -> x9, starting transfers between devices: 5.16 us -> 7.11 us  [swap(): return lax.ppermute(x, axis, [(0, 1), (1, 0)])]
  transfers between devices with their start and end apart: 31 -> 33, of which waited for: 10 -> 10; matrix products, arithmetic and copies ran while one was open for 1% -> 3% of each run, Pallas kernels for 6% -> 9%
where the time goes in v2:
time: 144 us
  waiting for transfers between devices  55 us (38%)
  starting transfers between devices  52.5 us (36%)
  Pallas kernels  20.1 us (14%)
  local copies, waits for them, and re-layouts  15.1 us (10%)
    ppermute x18, waiting for transfers between devices, flip(): return lax.ppermute(x, 'seq', [(i, i ^ mask) for i in range(count)])  44 us
    ppermute x18, starting transfers between devices, flip(): return lax.ppermute(x, 'seq', [(i, i ^ mask) for i in range(count)])  31.2 us
    ppermute x6, starting transfers between devices, some(): return lax.ppermute(x, 'seq', pairs)  14.1 us
    unnamed x50, local copies, waits for them, and re-layouts  10.2 us
    pallas_call x4, Pallas kernels, attention(): pl.pallas_call(functools.partial(attention_kernel, returned=returned), in...  10 us
    ppermute x9, waiting for transfers between devices, swap(): return lax.ppermute(x, axis, [(0, 1), (1, 0)])  8.48 us
    ppermute x9, starting transfers between devices, swap(): return lax.ppermute(x, axis, [(0, 1), (1, 0)])  7.11 us
    pallas_call x1, Pallas kernels, project(): pl.pallas_call(functools.partial(project_kernel, places=places), in_specs...  4.76 us
  transfers between devices with their start and end apart: 33, of which 10 were waited for; matrix products, arithmetic and copies ran while one was open for 3% of the time, Pallas kernels for 9%

profile of v2, /device:TPU:0, one launch (start us, length us, event | category | flops | bytes accessed | tf_op | source)
XLA Modules:
  0.0 143.8 jit_solution(14874502852603077890)
XLA Ops:
  1.7 4.1 %collective-permute-start.5 = (bf16[384,384]{1,0:T(8,128)(2,1)S(1)}, bf16[384,384]{1,0:T(8,128)(2,1)S(1)}, u32[]{:S(2)}, u32[]{:S(2)}) collective-permute-start(bf16[384,384]{1,0:T(8,128)(2,1)S(1)} %slice.18.query), channel_id=1, source_target_pairs={{0,8},{2,10},{4,12},{6,14},{8,0},{10,2},{12,4},{14,6},{1,9},{3,11}... | collective-permute-start | bytes 884744 | tf_op jit(solution)/shard_map/ppermute | solution.py:406
  7.0 1.7 %constant_dynamic-slice_fusion = bf16[96,1536]{1,0:T(8,128)(2,1)} fusion(bf16[192,1536]{1,0:T(8,128)(2,1)} %rest_0_.1, s32[]{:T(128)S(6)} %select_n.21), kind=kLoop, calls=%fused_computation.2 | loop fusion | bytes 589828 | tf_op jit(solution)/shard_map/dynamic_slice | solution.py:416
  8.6 2.9 %collective-permute-start.21 = (bf16[96,1536]{1,0:T(8,128)(2,1)}, bf16[96,1536]{1,0:T(8,128)(2,1)S(1)}, u32[]{:S(2)}, u32[]{:S(2)}) collective-permute-start(bf16[96,1536]{1,0:T(8,128)(2,1)} %constant_dynamic-slice_fusion), channel_id=1, source_target_pairs={{0,8},{2,10},{4,12},{6,14},{8,0},{10,2},{12,4},{14,6},{1,9},{3,11}... | collective-permute-start | bytes 884744 | tf_op jit(solution)/shard_map/ppermute | solution.py:406
  12.6 1.6 %collective-permute-start.8 = (bf16[384,384]{1,0:T(8,128)(2,1)S(1)}, bf16[384,384]{1,0:T(8,128)(2,1)S(1)}, u32[]{:S(2)}, u32[]{:S(2)}) collective-permute-start(bf16[384,384]{1,0:T(8,128)(2,1)S(1)} %get-tuple-element.32.refs_0_), channel_id=1, source_target_pairs={{0,2},{2,0},{4,6},{6,4},{8,10},{10,8},{12,14},{14,12},{1,3},{3,1},... | collective-permute-start | bytes 884744 | tf_op jit(solution)/shard_map/ppermute | solution.py:406
  15.6 23.4 %collective-permute-done.13.query = bf16[384,384]{1,0:T(8,128)(2,1)S(1)} collective-permute-done((bf16[384,384]{1,0:T(8,128)(2,1)S(1)}, bf16[384,384]{1,0:T(8,128)(2,1)S(1)}, u32[]{:S(2)}, u32[]{:S(2)}) %collective-permute-start.13) | collective-permute-done | bytes 294944 | tf_op jit(solution)/shard_map/ppermute | solution.py:406
  39.7 1.8 %collective-permute-start = (bf16[384,384]{1,0:T(8,128)(2,1)S(1)}, bf16[384,384]{1,0:T(8,128)(2,1)S(1)}, u32[]{:S(2)}, u32[]{:S(2)}) collective-permute-start(bf16[384,384]{1,0:T(8,128)(2,1)S(1)} %get-tuple-element.33.refs_0_), channel_id=1, source_target_pairs={{0,2},{2,0},{4,6},{6,4},{8,10},{10,8},{12,14},{14,12},{1,3},{3,1},... | collective-permute-start | bytes 884744 | tf_op jit(solution)/shard_map/ppermute | solution.py:406
  42.4 2.0 %collective-permute-done.21.rest_4_ = bf16[96,1536]{1,0:T(8,128)(2,1)S(1)} collective-permute-done((bf16[96,1536]{1,0:T(8,128)(2,1)}, bf16[96,1536]{1,0:T(8,128)(2,1)S(1)}, u32[]{:S(2)}, u32[]{:S(2)}) %collective-permute-start.21) | collective-permute-done | bytes 294944 | tf_op jit(solution)/shard_map/ppermute | solution.py:406
  45.7 5.3 %collective-permute-start.10 = (bf16[384,384]{1,0:T(8,128)(2,1)S(1)}, bf16[384,384]{1,0:T(8,128)(2,1)S(1)}, u32[]{:S(2)}, u32[]{:S(2)}) collective-permute-start(bf16[384,384]{1,0:T(8,128)(2,1)S(1)} %collective-permute-done.8.refs_2_), channel_id=1, source_target_pairs={{0,4},{6,2},{8,12},{14,10},{1,5},{7,3},{9,13},{15,11},{16,20},{22,... | collective-permute-start | bytes 884744 | tf_op jit(solution)/shard_map/ppermute | solution.py:413
  51.0 1.6 %collective-permute-start.12 = (bf16[384,384]{1,0:T(8,128)(2,1)S(1)}, bf16[384,384]{1,0:T(8,128)(2,1)S(1)}, u32[]{:S(2)}, u32[]{:S(2)}) collective-permute-start(bf16[384,384]{1,0:T(8,128)(2,1)S(1)} %collective-permute-done.11), channel_id=1, source_target_pairs={{0,2},{6,4},{8,10},{14,12},{1,3},{7,5},{9,11},{15,13},{16,18},{22,... | collective-permute-start | bytes 884744 | tf_op jit(solution)/shard_map/ppermute | solution.py:413
  53.3 3.4 %collective-permute-start.2 = (bf16[384,384]{1,0:T(8,128)(2,1)S(1)}, bf16[384,384]{1,0:T(8,128)(2,1)S(1)}, u32[]{:S(2)}, u32[]{:S(2)}) collective-permute-start(bf16[384,384]{1,0:T(8,128)(2,1)S(1)} %collective-permute-done.refs_2_), channel_id=1, source_target_pairs={{0,4},{6,2},{8,12},{14,10},{1,5},{7,3},{9,13},{15,11},{16,20},{22,... | collective-permute-start | bytes 884744 | tf_op jit(solution)/shard_map/ppermute | solution.py:413
  58.1 3.1 %collective-permute-start.19 = (bf16[96,1536]{1,0:T(8,128)(2,1)}, bf16[96,1536]{1,0:T(8,128)(2,1)}, u32[]{:S(2)}, u32[]{:S(2)}) collective-permute-start(bf16[96,1536]{1,0:T(8,128)(2,1)} %constant_dynamic-slice_fusion), channel_id=1, source_target_pairs={{0,2},{2,0},{4,6},{6,4},{8,10},{10,8},{12,14},{14,12},{1,3},{3,1},... | collective-permute-start | bytes 884744 | tf_op jit(solution)/shard_map/ppermute | solution.py:406
  63.6 2.5 %attend.7 = (bf16[384,384]{1,0:T(8,128)(2,1)S(1)}, f32[8,384]{1,0:T(8,128)S(1)}) custom-call(s32[2]{0:T(128)S(1)} %pad_add_fusion.1.info, bf16[384,384]{1,0:T(8,128)(2,1)S(1)} %copy-done.11, bf16[384,384]{1,0:T(8,128)(2,1)S(1)} %get-tuple-element.32.refs_0_, bf16[384,384]{1,0:T(8,128)(2,1)S(1)} %get-tuple-element.30.refs_1_, ...), custom_call_target="tpu_custom_call" | custom-call | flops 528482304 | bytes 2359296 | tf_op jit(solution)/shard_map/attend/pallas_call | solution.py:187
  66.3 1.5 %collective-permute-start.27 = (bf16[96,1536]{1,0:T(8,128)(2,1)}, bf16[96,1536]{1,0:T(8,128)(2,1)}, u32[]{:S(2)}, u32[]{:S(2)}) collective-permute-start(bf16[96,1536]{1,0:T(8,128)(2,1)} %copy-done.6), channel_id=1, source_target_pairs={{0,16},{16,0},{1,17},{17,1},{2,18},{18,2},{3,19},{19,3},{4,20},{20... | collective-permute-start | bytes 884744 | tf_op jit(solution)/shard_map/ppermute | solution.py:409
  67.8 2.5 %collective-permute-start.23 = (bf16[96,1536]{1,0:T(8,128)(2,1)}, bf16[96,1536]{1,0:T(8,128)(2,1)S(1)}, u32[]{:S(2)}, u32[]{:S(2)}) collective-permute-start(bf16[96,1536]{1,0:T(8,128)(2,1)} %copy-done.6), channel_id=1, source_target_pairs={{0,2},{2,0},{4,6},{6,4},{8,10},{10,8},{12,14},{14,12},{1,3},{3,1},... | collective-permute-start | bytes 884744 | tf_op jit(solution)/shard_map/ppermute | solution.py:406
  70.3 2.4 %collective-permute-done.4.refs_5_ = bf16[384,384]{1,0:T(8,128)(2,1)S(1)} collective-permute-done((bf16[384,384]{1,0:T(8,128)(2,1)}, bf16[384,384]{1,0:T(8,128)(2,1)S(1)}, u32[]{:S(2)}, u32[]{:S(2)}) %collective-permute-start.4) | collective-permute-done | bytes 294944 | tf_op jit(solution)/shard_map/ppermute | solution.py:413
  72.8 2.4 %collective-permute-start.22 = (bf16[96,1536]{1,0:T(8,128)(2,1)}, bf16[96,1536]{1,0:T(8,128)(2,1)S(1)}, u32[]{:S(2)}, u32[]{:S(2)}) collective-permute-start(bf16[96,1536]{1,0:T(8,128)(2,1)} %copy-done.6), channel_id=1, source_target_pairs={{0,4},{2,6},{4,0},{6,2},{8,12},{10,14},{12,8},{14,10},{1,5},{3,7},... | collective-permute-start | bytes 884744 | tf_op jit(solution)/shard_map/ppermute | solution.py:406
  76.1 2.5 %attend.5 = (bf16[384,384]{1,0:T(8,128)(2,1)S(1)}, f32[8,384]{1,0:T(8,128)S(1)}) custom-call(s32[2]{0:T(128)S(1)} %pad_add_fusion.1.info, bf16[384,384]{1,0:T(8,128)(2,1)S(1)} %copy-done.9, bf16[384,384]{1,0:T(8,128)(2,1)S(1)} %get-tuple-element.33.refs_0_, bf16[384,384]{1,0:T(8,128)(2,1)S(1)} %get-tuple-element.31.refs_1_, ...), custom_call_target="tpu_custom_call" | custom-call | flops 528482304 | bytes 2359296 | tf_op jit(solution)/shard_map/attend/pallas_call | solution.py:187
  79.1 3.3 %collective-permute-start.14 = (bf16[384,384]{1,0:T(8,128)(2,1)S(1)}, bf16[384,384]{1,0:T(8,128)(2,1)S(1)}, u32[]{:S(2)}, u32[]{:S(2)}) collective-permute-start(bf16[384,384]{1,0:T(8,128)(2,1)S(1)} %get-tuple-element.25), channel_id=1, source_target_pairs={{0,8},{2,10},{4,12},{6,14},{8,0},{10,2},{12,4},{14,6},{1,9},{3,11}... | collective-permute-start | bytes 884744 | tf_op jit(solution)/shard_map/ppermute | solution.py:406
  82.4 2.9 %collective-permute-start.15 = (f32[8,384]{1,0:T(8,128)S(1)}, f32[8,384]{1,0:T(8,128)S(1)}, u32[]{:S(2)}, u32[]{:S(2)}) collective-permute-start(f32[8,384]{1,0:T(8,128)S(1)} %get-tuple-element.26), channel_id=1, source_target_pairs={{0,8},{2,10},{4,12},{6,14},{8,0},{10,2},{12,4},{14,6},{1,9},{3,11}... | collective-permute-start | bytes 36872 | tf_op jit(solution)/shard_map/ppermute | solution.py:406
  86.0 2.2 %collective-permute-start.7 = (f32[8,384]{1,0:T(8,128)S(1)}, f32[8,384]{1,0:T(8,128)S(1)}, u32[]{:S(2)}, u32[]{:S(2)}) collective-permute-start(f32[8,384]{1,0:T(8,128)S(1)} %get-tuple-element.21), channel_id=1, source_target_pairs={{0,8},{2,10},{4,12},{6,14},{8,0},{10,2},{12,4},{14,6},{1,9},{3,11}... | collective-permute-start | bytes 36872 | tf_op jit(solution)/shard_map/ppermute | solution.py:406
  88.2 1.5 %collective-permute-start.26 = (bf16[96,1536]{1,0:T(8,128)(2,1)}, bf16[96,1536]{1,0:T(8,128)(2,1)S(1)}, u32[]{:S(2)}, u32[]{:S(2)}) collective-permute-start(bf16[96,1536]{1,0:T(8,128)(2,1)} %collective-permute-done.19.rest_2_), channel_id=1, source_target_pairs={{0,16},{16,0},{1,17},{17,1},{2,18},{18,2},{3,19},{19,3},{4,20},{20... | collective-permute-start | bytes 884744 | tf_op jit(solution)/shard_map/ppermute | solution.py:409
  89.7 17.4 %collective-permute-done.15.got_logs = f32[8,384]{1,0:T(8,128)S(1)} collective-permute-done((f32[8,384]{1,0:T(8,128)S(1)}, f32[8,384]{1,0:T(8,128)S(1)}, u32[]{:S(2)}, u32[]{:S(2)}) %collective-permute-start.15) | collective-permute-done | bytes 12320 | tf_op jit(solution)/shard_map/ppermute | solution.py:406
  107.7 1.5 %collective-permute-start.25 = (bf16[96,1536]{1,0:T(8,128)(2,1)}, bf16[96,1536]{1,0:T(8,128)(2,1)S(1)}, u32[]{:S(2)}, u32[]{:S(2)}) collective-permute-start(bf16[96,1536]{1,0:T(8,128)(2,1)} %collective-permute-done.18.rest_1_), channel_id=1, source_target_pairs={{0,16},{16,0},{1,17},{17,1},{2,18},{18,2},{3,19},{19,3},{4,20},{20... | collective-permute-start | bytes 884744 | tf_op jit(solution)/shard_map/ppermute | solution.py:409
  111.2 2.5 %attend.6 = (f32[384,384]{1,0:T(8,128)S(1)}, f32[384,128]{1,0:T(8,128)S(1)}) custom-call(s32[2]{0:T(128)S(1)} %pad_add_fusion.1.info, bf16[384,384]{1,0:T(8,128)(2,1)S(1)} %copy-done.4, bf16[384,384]{1,0:T(8,128)(2,1)S(1)} %get-tuple-element.32.refs_0_, bf16[384,384]{1,0:T(8,128)(2,1)S(1)} %get-tuple-element.30.refs_1_, ...), custom_call_target="tpu_custom_call" | custom-call | flops 528482304 | bytes 2359296 | tf_op jit(solution)/shard_map/attend/pallas_call | solution.py:187
  113.7 2.5 %attend.4 = (f32[384,384]{1,0:T(8,128)S(1)}, f32[384,128]{1,0:T(8,128)S(1)}) custom-call(s32[2]{0:T(128)S(1)} %pad_add_fusion.1.info, bf16[384,384]{1,0:T(8,128)(2,1)S(1)} %copy-done.2, bf16[384,384]{1,0:T(8,128)(2,1)S(1)} %get-tuple-element.33.refs_0_, bf16[384,384]{1,0:T(8,128)(2,1)S(1)} %get-tuple-element.31.refs_1_, ...), custom_call_target="tpu_custom_call" | custom-call | flops 528482304 | bytes 2359296 | tf_op jit(solution)/shard_map/attend/pallas_call | solution.py:187
  118.6 1.5 %collective-permute-start.29 = (bf16[96,1536]{1,0:T(8,128)(2,1)}, bf16[96,1536]{1,0:T(8,128)(2,1)S(1)}, u32[]{:S(2)}, u32[]{:S(2)}) collective-permute-start(bf16[96,1536]{1,0:T(8,128)(2,1)} %collective-permute-done.20.rest_3_), channel_id=1, source_target_pairs={{0,16},{16,0},{1,17},{17,1},{2,18},{18,2},{3,19},{19,3},{4,20},{20... | collective-permute-start | bytes 884744 | tf_op jit(solution)/shard_map/ppermute | solution.py:409
  121.4 2.8 %collective-permute-done.28.rest_11_ = bf16[96,1536]{1,0:T(8,128)(2,1)S(1)} collective-permute-done((bf16[96,1536]{1,0:T(8,128)(2,1)S(1)}, bf16[96,1536]{1,0:T(8,128)(2,1)S(1)}, u32[]{:S(2)}, u32[]{:S(2)}) %collective-permute-start.28) | collective-permute-done | bytes 294944 | tf_op jit(solution)/shard_map/ppermute | solution.py:409
  128.8 2.4 %stage.1.staged = bf16[1536,1536]{1,0:T(8,128)(2,1)S(1)} custom-call(s32[3]{0:T(128)S(1)} %pad_add_fusion.info, bf16[192,1536]{1,0:T(8,128)(2,1)S(1)} %copy-done, bf16[96,1536]{1,0:T(8,128)(2,1)} %collective-permute-done.18.rest_1_, bf16[96,1536]{1,0:T(8,128)(2,1)} %collective-permute-done.19.rest_2_, bf16[96,1536]{1,0:T(8,128)(2,1)} %collective-permute-done.20.rest_3_, ...), custom_call_target="tpu_custom_call" | custom-call | bytes 9437184 | tf_op jit(solution)/shard_map/stage/pallas_call | solution.py:256
  131.2 4.3 %collective-permute-done.31.rest_2_ = bf16[96,1536]{1,0:T(8,128)(2,1)S(1)} collective-permute-done((bf16[96,1536]{1,0:T(8,128)(2,1)}, bf16[96,1536]{1,0:T(8,128)(2,1)S(1)}, u32[]{:S(2)}, u32[]{:S(2)}) %collective-permute-start.31) | collective-permute-done | bytes 294944 | tf_op jit(solution)/shard_map/ppermute | solution.py:409
  135.5 4.8 %project.1 = (f32[384,1536]{1,0:T(8,128)S(1)}, bf16[384,1536]{1,0:T(8,128)(2,1)}, f32[384,128]{1,0:T(8,128)S(1)}, bf16[1536,1536]{1,0:T(8,128)(2,1)S(1)}) custom-call(s32[3]{0:T(128)S(1)} %pad_add_fusion.info, bf16[384,384]{1,0:T(8,128)(2,1)S(1)} %merge.2.a_low, bf16[384,384]{1,0:T(8,128)(2,1)S(1)} %merge.3.a_high, ...), custom_call_target="tpu_custom_call", output_to_operand_aliasing={{3}: (6, {})} | custom-call | flops 1811939328 | bytes 9437184 | tf_op jit(solution)/shard_map/project/pallas_call | solution.py:321
  140.3 1.4 collective-permute-done.32.other
  141.8 1.9 %normalize.1 = bf16[384,1536]{1,0:T(8,128)(2,1)} custom-call(s32[3]{0:T(128)S(1)} %pad_add_fusion.info, f32[384,1536]{1,0:T(8,128)S(1)} %get-tuple-element.27.mixed, f32[384,128]{1,0:T(8,128)S(1)} %get-tuple-element.28.mine, f32[384,128]{1,0:T(8,128)S(1)} %collective-permute-done.32.other, f32[1,3072]{1,0:T(1,128)S(1)} %bitcast.7, f32[1,3072]{1,0:T(1,128)S(1)} %bitcast.8), custom_call_target="tpu_custom_call" | custom-call | flops 3538944 | bytes 3538944 | tf_op jit(solution)/shard_map/normalize/pallas_call | solution.py:379
  (100 shorter events, 25.3 us)
Async XLA Ops:
  1.7 39.8 %collective-permute-start.5 = (bf16[384,384]{1,0:T(8,128)(2,1)S(1)}, bf16[384,384]{1,0:T(8,128)(2,1)S(1)}, u32[]{:S(2)}, u32[]{:S(2)}) collective-permute-start(bf16[384,384]{1,0:T(8,128)(2,1)S(1)} %slice.18.query), channel_id=1, source_target_pairs={{0,8},{2,10},{4,12},{6,14},{8,0},{10,2},{12,4},{14,6},{1,9},{3,11}... | collective-permute-start | bytes 884744 | tf_op jit(solution)/shard_map/ppermute | solution.py:406
  6.8 32.1 %collective-permute-start.13 = (bf16[384,384]{1,0:T(8,128)(2,1)S(1)}, bf16[384,384]{1,0:T(8,128)(2,1)S(1)}, u32[]{:S(2)}, u32[]{:S(2)}) collective-permute-start(bf16[384,384]{1,0:T(8,128)(2,1)S(1)} %slice.21.query), channel_id=1, source_target_pairs={{0,8},{2,10},{4,12},{6,14},{8,0},{10,2},{12,4},{14,6},{1,9},{3,11}... | collective-permute-start | bytes 884744 | tf_op jit(solution)/shard_map/ppermute | solution.py:406
  8.6 35.8 %collective-permute-start.21 = (bf16[96,1536]{1,0:T(8,128)(2,1)}, bf16[96,1536]{1,0:T(8,128)(2,1)S(1)}, u32[]{:S(2)}, u32[]{:S(2)}) collective-permute-start(bf16[96,1536]{1,0:T(8,128)(2,1)} %constant_dynamic-slice_fusion), channel_id=1, source_target_pairs={{0,8},{2,10},{4,12},{6,14},{8,0},{10,2},{12,4},{14,6},{1,9},{3,11}... | collective-permute-start | bytes 884744 | tf_op jit(solution)/shard_map/ppermute | solution.py:406
  12.6 33.1 %collective-permute-start.8 = (bf16[384,384]{1,0:T(8,128)(2,1)S(1)}, bf16[384,384]{1,0:T(8,128)(2,1)S(1)}, u32[]{:S(2)}, u32[]{:S(2)}) collective-permute-start(bf16[384,384]{1,0:T(8,128)(2,1)S(1)} %get-tuple-element.32.refs_0_), channel_id=1, source_target_pairs={{0,2},{2,0},{4,6},{6,4},{8,10},{10,8},{12,14},{14,12},{1,3},{3,1},... | collective-permute-start | bytes 884744 | tf_op jit(solution)/shard_map/ppermute | solution.py:406
  14.3 36.7 %collective-permute-start.11 = (bf16[384,384]{1,0:T(8,128)(2,1)S(1)}, bf16[384,384]{1,0:T(8,128)(2,1)S(1)}, u32[]{:S(2)}, u32[]{:S(2)}) collective-permute-start(bf16[384,384]{1,0:T(8,128)(2,1)S(1)} %get-tuple-element.30.refs_1_), channel_id=1, source_target_pairs={{2,6},{4,0},{10,14},{12,8},{3,7},{5,1},{11,15},{13,9},{18,22},{20,... | collective-permute-start | bytes 884744 | tf_op jit(solution)/shard_map/ppermute | solution.py:413
  39.7 13.0 %collective-permute-start = (bf16[384,384]{1,0:T(8,128)(2,1)S(1)}, bf16[384,384]{1,0:T(8,128)(2,1)S(1)}, u32[]{:S(2)}, u32[]{:S(2)}) collective-permute-start(bf16[384,384]{1,0:T(8,128)(2,1)S(1)} %get-tuple-element.33.refs_0_), channel_id=1, source_target_pairs={{0,2},{2,0},{4,6},{6,4},{8,10},{10,8},{12,14},{14,12},{1,3},{3,1},... | collective-permute-start | bytes 884744 | tf_op jit(solution)/shard_map/ppermute | solution.py:406
  42.2 11.1 %collective-permute-start.9 = (bf16[384,384]{1,0:T(8,128)(2,1)S(1)}, bf16[384,384]{1,0:T(8,128)(2,1)S(1)}, u32[]{:S(2)}, u32[]{:S(2)}) collective-permute-start(bf16[384,384]{1,0:T(8,128)(2,1)S(1)} %get-tuple-element.30.refs_1_), channel_id=1, source_target_pairs={{0,2},{2,0},{4,6},{6,4},{8,10},{10,8},{12,14},{14,12},{1,3},{3,1},... | collective-permute-start | bytes 884744 | tf_op jit(solution)/shard_map/ppermute | solution.py:406
  44.4 12.3 %collective-permute-start.3 = (bf16[384,384]{1,0:T(8,128)(2,1)S(1)}, bf16[384,384]{1,0:T(8,128)(2,1)}, u32[]{:S(2)}, u32[]{:S(2)}) collective-permute-start(bf16[384,384]{1,0:T(8,128)(2,1)S(1)} %get-tuple-element.31.refs_1_), channel_id=1, source_target_pairs={{2,6},{4,0},{10,14},{12,8},{3,7},{5,1},{11,15},{13,9},{18,22},{20,... | collective-permute-start | bytes 884744 | tf_op jit(solution)/shard_map/ppermute | solution.py:413
  45.7 12.3 %collective-permute-start.10 = (bf16[384,384]{1,0:T(8,128)(2,1)S(1)}, bf16[384,384]{1,0:T(8,128)(2,1)S(1)}, u32[]{:S(2)}, u32[]{:S(2)}) collective-permute-start(bf16[384,384]{1,0:T(8,128)(2,1)S(1)} %collective-permute-done.8.refs_2_), channel_id=1, source_target_pairs={{0,4},{6,2},{8,12},{14,10},{1,5},{7,3},{9,13},{15,11},{16,20},{22,... | collective-permute-start | bytes 884744 | tf_op jit(solution)/shard_map/ppermute | solution.py:413
  51.0 10.2 %collective-permute-start.12 = (bf16[384,384]{1,0:T(8,128)(2,1)S(1)}, bf16[384,384]{1,0:T(8,128)(2,1)S(1)}, u32[]{:S(2)}, u32[]{:S(2)}) collective-permute-start(bf16[384,384]{1,0:T(8,128)(2,1)S(1)} %collective-permute-done.11), channel_id=1, source_target_pairs={{0,2},{6,4},{8,10},{14,12},{1,3},{7,5},{9,11},{15,13},{16,18},{22,... | collective-permute-start | bytes 884744 | tf_op jit(solution)/shard_map/ppermute | solution.py:413
  52.7 13.7 %collective-permute-start.1 = (bf16[384,384]{1,0:T(8,128)(2,1)S(1)}, bf16[384,384]{1,0:T(8,128)(2,1)S(1)}, u32[]{:S(2)}, u32[]{:S(2)}) collective-permute-start(bf16[384,384]{1,0:T(8,128)(2,1)S(1)} %get-tuple-element.31.refs_1_), channel_id=1, source_target_pairs={{0,2},{2,0},{4,6},{6,4},{8,10},{10,8},{12,14},{14,12},{1,3},{3,1},... | collective-permute-start | bytes 884744 | tf_op jit(solution)/shard_map/ppermute | solution.py:406
  53.3 14.5 %collective-permute-start.2 = (bf16[384,384]{1,0:T(8,128)(2,1)S(1)}, bf16[384,384]{1,0:T(8,128)(2,1)S(1)}, u32[]{:S(2)}, u32[]{:S(2)}) collective-permute-start(bf16[384,384]{1,0:T(8,128)(2,1)S(1)} %collective-permute-done.refs_2_), channel_id=1, source_target_pairs={{0,4},{6,2},{8,12},{14,10},{1,5},{7,3},{9,13},{15,11},{16,20},{22,... | collective-permute-start | bytes 884744 | tf_op jit(solution)/shard_map/ppermute | solution.py:413
  56.7 16.0 %collective-permute-start.4 = (bf16[384,384]{1,0:T(8,128)(2,1)}, bf16[384,384]{1,0:T(8,128)(2,1)S(1)}, u32[]{:S(2)}, u32[]{:S(2)}) collective-permute-start(bf16[384,384]{1,0:T(8,128)(2,1)} %collective-permute-done.3), channel_id=1, source_target_pairs={{0,2},{6,4},{8,10},{14,12},{1,3},{7,5},{9,11},{15,13},{16,18},{22,... | collective-permute-start | bytes 884744 | tf_op jit(solution)/shard_map/ppermute | solution.py:413
  58.1 21.0 %collective-permute-start.19 = (bf16[96,1536]{1,0:T(8,128)(2,1)}, bf16[96,1536]{1,0:T(8,128)(2,1)}, u32[]{:S(2)}, u32[]{:S(2)}) collective-permute-start(bf16[96,1536]{1,0:T(8,128)(2,1)} %constant_dynamic-slice_fusion), channel_id=1, source_target_pairs={{0,2},{2,0},{4,6},{6,4},{8,10},{10,8},{12,14},{14,12},{1,3},{3,1},... | collective-permute-start | bytes 884744 | tf_op jit(solution)/shard_map/ppermute | solution.py:406
  61.2 21.2 %collective-permute-start.18 = (bf16[96,1536]{1,0:T(8,128)(2,1)}, bf16[96,1536]{1,0:T(8,128)(2,1)}, u32[]{:S(2)}, u32[]{:S(2)}) collective-permute-start(bf16[96,1536]{1,0:T(8,128)(2,1)} %constant_dynamic-slice_fusion), channel_id=1, source_target_pairs={{0,4},{2,6},{4,0},{6,2},{8,12},{10,14},{12,8},{14,10},{1,5},{3,7},... | collective-permute-start | bytes 884744 | tf_op jit(solution)/shard_map/ppermute | solution.py:406
  66.3 16.0 %collective-permute-start.27 = (bf16[96,1536]{1,0:T(8,128)(2,1)}, bf16[96,1536]{1,0:T(8,128)(2,1)}, u32[]{:S(2)}, u32[]{:S(2)}) collective-permute-start(bf16[96,1536]{1,0:T(8,128)(2,1)} %copy-done.6), channel_id=1, source_target_pairs={{0,16},{16,0},{1,17},{17,1},{2,18},{18,2},{3,19},{19,3},{4,20},{20... | collective-permute-start | bytes 884744 | tf_op jit(solution)/shard_map/ppermute | solution.py:409
  67.8 17.5 %collective-permute-start.23 = (bf16[96,1536]{1,0:T(8,128)(2,1)}, bf16[96,1536]{1,0:T(8,128)(2,1)S(1)}, u32[]{:S(2)}, u32[]{:S(2)}) collective-permute-start(bf16[96,1536]{1,0:T(8,128)(2,1)} %copy-done.6), channel_id=1, source_target_pairs={{0,2},{2,0},{4,6},{6,4},{8,10},{10,8},{12,14},{14,12},{1,3},{3,1},... | collective-permute-start | bytes 884744 | tf_op jit(solution)/shard_map/ppermute | solution.py:406
  72.8 15.4 %collective-permute-start.22 = (bf16[96,1536]{1,0:T(8,128)(2,1)}, bf16[96,1536]{1,0:T(8,128)(2,1)S(1)}, u32[]{:S(2)}, u32[]{:S(2)}) collective-permute-start(bf16[96,1536]{1,0:T(8,128)(2,1)} %copy-done.6), channel_id=1, source_target_pairs={{0,4},{2,6},{4,0},{6,2},{8,12},{10,14},{12,8},{14,10},{1,5},{3,7},... | collective-permute-start | bytes 884744 | tf_op jit(solution)/shard_map/ppermute | solution.py:406
  79.1 30.2 %collective-permute-start.14 = (bf16[384,384]{1,0:T(8,128)(2,1)S(1)}, bf16[384,384]{1,0:T(8,128)(2,1)S(1)}, u32[]{:S(2)}, u32[]{:S(2)}) collective-permute-start(bf16[384,384]{1,0:T(8,128)(2,1)S(1)} %get-tuple-element.25), channel_id=1, source_target_pairs={{0,8},{2,10},{4,12},{6,14},{8,0},{10,2},{12,4},{14,6},{1,9},{3,11}... | collective-permute-start | bytes 884744 | tf_op jit(solution)/shard_map/ppermute | solution.py:406
  82.4 28.3 %collective-permute-start.6 = (bf16[384,384]{1,0:T(8,128)(2,1)S(1)}, bf16[384,384]{1,0:T(8,128)(2,1)S(1)}, u32[]{:S(2)}, u32[]{:S(2)}) collective-permute-start(bf16[384,384]{1,0:T(8,128)(2,1)S(1)} %get-tuple-element.20), channel_id=1, source_target_pairs={{0,8},{2,10},{4,12},{6,14},{8,0},{10,2},{12,4},{14,6},{1,9},{3,11}... | collective-permute-start | bytes 884744 | tf_op jit(solution)/shard_map/ppermute | solution.py:406
  82.4 24.7 %collective-permute-start.15 = (f32[8,384]{1,0:T(8,128)S(1)}, f32[8,384]{1,0:T(8,128)S(1)}, u32[]{:S(2)}, u32[]{:S(2)}) collective-permute-start(f32[8,384]{1,0:T(8,128)S(1)} %get-tuple-element.26), channel_id=1, source_target_pairs={{0,8},{2,10},{4,12},{6,14},{8,0},{10,2},{12,4},{14,6},{1,9},{3,11}... | collective-permute-start | bytes 36872 | tf_op jit(solution)/shard_map/ppermute | solution.py:406
  86.0 21.7 %collective-permute-start.7 = (f32[8,384]{1,0:T(8,128)S(1)}, f32[8,384]{1,0:T(8,128)S(1)}, u32[]{:S(2)}, u32[]{:S(2)}) collective-permute-start(f32[8,384]{1,0:T(8,128)S(1)} %get-tuple-element.21), channel_id=1, source_target_pairs={{0,8},{2,10},{4,12},{6,14},{8,0},{10,2},{12,4},{14,6},{1,9},{3,11}... | collective-permute-start | bytes 36872 | tf_op jit(solution)/shard_map/ppermute | solution.py:406
  88.2 29.1 %collective-permute-start.26 = (bf16[96,1536]{1,0:T(8,128)(2,1)}, bf16[96,1536]{1,0:T(8,128)(2,1)S(1)}, u32[]{:S(2)}, u32[]{:S(2)}) collective-permute-start(bf16[96,1536]{1,0:T(8,128)(2,1)} %collective-permute-done.19.rest_2_), channel_id=1, source_target_pairs={{0,16},{16,0},{1,17},{17,1},{2,18},{18,2},{3,19},{19,3},{4,20},{20... | collective-permute-start | bytes 884744 | tf_op jit(solution)/shard_map/ppermute | solution.py:409
  107.1 11.6 %collective-permute-start.20 = (bf16[96,1536]{1,0:T(8,128)(2,1)}, bf16[96,1536]{1,0:T(8,128)(2,1)}, u32[]{:S(2)}, u32[]{:S(2)}) collective-permute-start(bf16[96,1536]{1,0:T(8,128)(2,1)} %collective-permute-done.19.rest_2_), channel_id=1, source_target_pairs={{0,4},{2,6},{4,0},{6,2},{8,12},{10,14},{12,8},{14,10},{1,5},{3,7},... | collective-permute-start | bytes 884744 | tf_op jit(solution)/shard_map/ppermute | solution.py:406
  107.7 12.4 %collective-permute-start.25 = (bf16[96,1536]{1,0:T(8,128)(2,1)}, bf16[96,1536]{1,0:T(8,128)(2,1)S(1)}, u32[]{:S(2)}, u32[]{:S(2)}) collective-permute-start(bf16[96,1536]{1,0:T(8,128)(2,1)} %collective-permute-done.18.rest_1_), channel_id=1, source_target_pairs={{0,16},{16,0},{1,17},{17,1},{2,18},{18,2},{3,19},{19,3},{4,20},{20... | collective-permute-start | bytes 884744 | tf_op jit(solution)/shard_map/ppermute | solution.py:409
  109.2 11.6 %collective-permute-start.24 = (bf16[96,1536]{1,0:T(8,128)(2,1)S(1)}, bf16[96,1536]{1,0:T(8,128)(2,1)}, u32[]{:S(2)}, u32[]{:S(2)}) collective-permute-start(bf16[96,1536]{1,0:T(8,128)(2,1)S(1)} %collective-permute-done.22.rest_5_), channel_id=1, source_target_pairs={{0,2},{2,0},{4,6},{6,4},{8,10},{10,8},{12,14},{14,12},{1,3},{3,1},... | collective-permute-start | bytes 884744 | tf_op jit(solution)/shard_map/ppermute | solution.py:406
  110.7 13.5 %collective-permute-start.28 = (bf16[96,1536]{1,0:T(8,128)(2,1)S(1)}, bf16[96,1536]{1,0:T(8,128)(2,1)S(1)}, u32[]{:S(2)}, u32[]{:S(2)}) collective-permute-start(bf16[96,1536]{1,0:T(8,128)(2,1)S(1)} %collective-permute-done.22.rest_5_), channel_id=1, source_target_pairs={{0,16},{16,0},{1,17},{17,1},{2,18},{18,2},{3,19},{19,3},{4,20},{20... | collective-permute-start | bytes 884744 | tf_op jit(solution)/shard_map/ppermute | solution.py:409
  118.0 13.2 %collective-permute-start.30 = (bf16[96,1536]{1,0:T(8,128)(2,1)}, bf16[96,1536]{1,0:T(8,128)(2,1)S(1)}, u32[]{:S(2)}, u32[]{:S(2)}) collective-permute-start(bf16[96,1536]{1,0:T(8,128)(2,1)} %collective-permute-done.27.rest_10_), channel_id=1, source_target_pairs={{0,2},{2,0},{4,6},{6,4},{8,10},{10,8},{12,14},{14,12},{1,3},{3,1},... | collective-permute-start | bytes 884744 | tf_op jit(solution)/shard_map/ppermute | solution.py:406
  118.6 12.6 %collective-permute-start.29 = (bf16[96,1536]{1,0:T(8,128)(2,1)}, bf16[96,1536]{1,0:T(8,128)(2,1)S(1)}, u32[]{:S(2)}, u32[]{:S(2)}) collective-permute-start(bf16[96,1536]{1,0:T(8,128)(2,1)} %collective-permute-done.20.rest_3_), channel_id=1, source_target_pairs={{0,16},{16,0},{1,17},{17,1},{2,18},{18,2},{3,19},{19,3},{4,20},{20... | collective-permute-start | bytes 884744 | tf_op jit(solution)/shard_map/ppermute | solution.py:409
  120.8 14.6 %collective-permute-start.17 = (bf16[384,384]{1,0:T(8,128)(2,1)S(1)}, bf16[384,384]{1,0:T(8,128)(2,1)S(1)}, u32[]{:S(2)}, u32[]{:S(2)}) collective-permute-start(bf16[384,384]{1,0:T(8,128)(2,1)S(1)} %merge.3.a_high), channel_id=1, source_target_pairs={{0,1},{1,0},{2,3},{3,2},{4,5},{5,4},{6,7},{7,6},{8,9},{9,8},{10,11... | collective-permute-start | bytes 884744 | tf_op jit(solution)/shard_map/ppermute | solution.py:409
  120.9 14.6 %collective-permute-start.31 = (bf16[96,1536]{1,0:T(8,128)(2,1)}, bf16[96,1536]{1,0:T(8,128)(2,1)S(1)}, u32[]{:S(2)}, u32[]{:S(2)}) collective-permute-start(bf16[96,1536]{1,0:T(8,128)(2,1)} %collective-permute-done.24.rest_7_), channel_id=1, source_target_pairs={{0,16},{16,0},{1,17},{17,1},{2,18},{18,2},{3,19},{19,3},{4,20},{20... | collective-permute-start | bytes 884744 | tf_op jit(solution)/shard_map/ppermute | solution.py:409
  124.9 10.6 %collective-permute-start.16 = (bf16[384,384]{1,0:T(8,128)(2,1)S(1)}, bf16[384,384]{1,0:T(8,128)(2,1)}, u32[]{:S(2)}, u32[]{:S(2)}) collective-permute-start(bf16[384,384]{1,0:T(8,128)(2,1)S(1)} %merge.2.a_low), channel_id=1, source_target_pairs={{0,1},{1,0},{2,3},{3,2},{4,5},{5,4},{6,7},{7,6},{8,9},{9,8},{10,11... | collective-permute-start | bytes 884744 | tf_op jit(solution)/shard_map/ppermute | solution.py:409
  (26 other events, 300.3 us)

commit v3 on v2

--- a/solution.py
+++ b/solution.py
@@ -444,8 +444,8 @@
     w_yd = flip(w_z2, 1)
     w_xe = swap(w_z2, "video")
     w_xb = swap(w_ya, "video")
-    w_yf = flip(w_xd, 1)
-    w_xc = swap(w_z3, "video")
+    w_xf = swap(w_yc, "video")
+    w_yx = flip(w_xa, 1)
     w_xg = swap(w_yd, "video")
 
     info = jnp.stack([par, relayed]).astype(jnp.int32)
@@ -478,8 +478,9 @@
         (w_xb, (1, 1, n)),
         (w_xd, (4, 1, n)),
         (w_xe, (6, 1, n)),
+        (w_xf, (5, 1, n)),
     )
-    last = ((w_xc, (3, 1, n)), (w_yf, (5, 1, n)), (w_xg, (7, 1, n)))
+    last = ((w_yx, (3, 1, n)), (w_xg, (7, 1, n)))
     where = jnp.stack([core, position, vid]).astype(jnp.int32)
     depth = 2 * n * count
     staged = stage(where, *map(tuple, zip(*early)), depth)

time: 144 us -> 144 us (level)
  no operation moved by 1% of the time
where the time goes in v3:
time: 144 us; the launch traced here: 143 us
  waiting for transfers between devices  54.9 us (38%)
  starting transfers between devices  51.8 us (36%)
  Pallas kernels  20 us (14%)
  local copies, waits for them, and re-layouts  15.1 us (10%)
    ppermute x18, waiting for transfers between devices, flip(): return lax.ppermute(x, 'seq', [(i, i ^ mask) for i in range(count)])  44.8 us
    ppermute x18, starting transfers between devices, flip(): return lax.ppermute(x, 'seq', [(i, i ^ mask) for i in range(count)])  30.4 us
    ppermute x6, starting transfers between devices, some(): return lax.ppermute(x, 'seq', pairs)  14.1 us
    unnamed x50, local copies, waits for them, and re-layouts  10.2 us
    pallas_call x4, Pallas kernels, attention(): pl.pallas_call(functools.partial(attention_kernel, returned=returned), in...  10 us
    ppermute x9, waiting for transfers between devices, swap(): return lax.ppermute(x, axis, [(0, 1), (1, 0)])  7.66 us
    ppermute x9, starting transfers between devices, swap(): return lax.ppermute(x, axis, [(0, 1), (1, 0)])  7.19 us
    pallas_call x1, Pallas kernels, project(): pl.pallas_call(functools.partial(project_kernel, places=places), in_specs...  4.68 us
  transfers between devices with their start and end apart: 33, of which 10 were waited for; matrix products, arithmetic and copies ran while one was open for 3% of the time, Pallas kernels for 9%

profile of v3, /device:TPU:0, one launch (start us, length us, event | category | flops | bytes accessed | tf_op | source)
XLA Modules:
  0.0 143.0 jit_solution(8639346219618454066)
XLA Ops:
  1.7 4.1 %collective-permute-start.5 = (bf16[384,384]{1,0:T(8,128)(2,1)S(1)}, bf16[384,384]{1,0:T(8,128)(2,1)S(1)}, u32[]{:S(2)}, u32[]{:S(2)}) collective-permute-start(bf16[384,384]{1,0:T(8,128)(2,1)S(1)} %slice.18.query), channel_id=1, source_target_pairs={{0,8},{2,10},{4,12},{6,14},{8,0},{10,2},{12,4},{14,6},{1,9},{3,11}... | collective-permute-start | bytes 884744 | tf_op jit(solution)/shard_map/ppermute | solution.py:406
  7.0 1.7 %constant_dynamic-slice_fusion = bf16[96,1536]{1,0:T(8,128)(2,1)} fusion(bf16[192,1536]{1,0:T(8,128)(2,1)} %rest_0_.1, s32[]{:T(128)S(6)} %select_n.21), kind=kLoop, calls=%fused_computation.2 | loop fusion | bytes 589828 | tf_op jit(solution)/shard_map/dynamic_slice | solution.py:416
  8.6 2.9 %collective-permute-start.21 = (bf16[96,1536]{1,0:T(8,128)(2,1)}, bf16[96,1536]{1,0:T(8,128)(2,1)S(1)}, u32[]{:S(2)}, u32[]{:S(2)}) collective-permute-start(bf16[96,1536]{1,0:T(8,128)(2,1)} %constant_dynamic-slice_fusion), channel_id=1, source_target_pairs={{0,8},{2,10},{4,12},{6,14},{8,0},{10,2},{12,4},{14,6},{1,9},{3,11}... | collective-permute-start | bytes 884744 | tf_op jit(solution)/shard_map/ppermute | solution.py:406
  12.6 1.6 %collective-permute-start.8 = (bf16[384,384]{1,0:T(8,128)(2,1)S(1)}, bf16[384,384]{1,0:T(8,128)(2,1)S(1)}, u32[]{:S(2)}, u32[]{:S(2)}) collective-permute-start(bf16[384,384]{1,0:T(8,128)(2,1)S(1)} %get-tuple-element.32.refs_0_), channel_id=1, source_target_pairs={{0,2},{2,0},{4,6},{6,4},{8,10},{10,8},{12,14},{14,12},{1,3},{3,1},... | collective-permute-start | bytes 884744 | tf_op jit(solution)/shard_map/ppermute | solution.py:406
  15.6 23.4 %collective-permute-done.13.query = bf16[384,384]{1,0:T(8,128)(2,1)S(1)} collective-permute-done((bf16[384,384]{1,0:T(8,128)(2,1)S(1)}, bf16[384,384]{1,0:T(8,128)(2,1)S(1)}, u32[]{:S(2)}, u32[]{:S(2)}) %collective-permute-start.13) | collective-permute-done | bytes 294944 | tf_op jit(solution)/shard_map/ppermute | solution.py:406
  39.7 1.8 %collective-permute-start = (bf16[384,384]{1,0:T(8,128)(2,1)S(1)}, bf16[384,384]{1,0:T(8,128)(2,1)S(1)}, u32[]{:S(2)}, u32[]{:S(2)}) collective-permute-start(bf16[384,384]{1,0:T(8,128)(2,1)S(1)} %get-tuple-element.33.refs_0_), channel_id=1, source_target_pairs={{0,2},{2,0},{4,6},{6,4},{8,10},{10,8},{12,14},{14,12},{1,3},{3,1},... | collective-permute-start | bytes 884744 | tf_op jit(solution)/shard_map/ppermute | solution.py:406
  42.4 2.0 %collective-permute-done.21.rest_4_ = bf16[96,1536]{1,0:T(8,128)(2,1)S(1)} collective-permute-done((bf16[96,1536]{1,0:T(8,128)(2,1)}, bf16[96,1536]{1,0:T(8,128)(2,1)S(1)}, u32[]{:S(2)}, u32[]{:S(2)}) %collective-permute-start.21) | collective-permute-done | bytes 294944 | tf_op jit(solution)/shard_map/ppermute | solution.py:406
  45.7 5.3 %collective-permute-start.10 = (bf16[384,384]{1,0:T(8,128)(2,1)S(1)}, bf16[384,384]{1,0:T(8,128)(2,1)S(1)}, u32[]{:S(2)}, u32[]{:S(2)}) collective-permute-start(bf16[384,384]{1,0:T(8,128)(2,1)S(1)} %collective-permute-done.8.refs_2_), channel_id=1, source_target_pairs={{0,4},{6,2},{8,12},{14,10},{1,5},{7,3},{9,13},{15,11},{16,20},{22,... | collective-permute-start | bytes 884744 | tf_op jit(solution)/shard_map/ppermute | solution.py:413
  51.0 1.6 %collective-permute-start.12 = (bf16[384,384]{1,0:T(8,128)(2,1)S(1)}, bf16[384,384]{1,0:T(8,128)(2,1)S(1)}, u32[]{:S(2)}, u32[]{:S(2)}) collective-permute-start(bf16[384,384]{1,0:T(8,128)(2,1)S(1)} %collective-permute-done.11), channel_id=1, source_target_pairs={{0,2},{6,4},{8,10},{14,12},{1,3},{7,5},{9,11},{15,13},{16,18},{22,... | collective-permute-start | bytes 884744 | tf_op jit(solution)/shard_map/ppermute | solution.py:413
  53.3 3.4 %collective-permute-start.2 = (bf16[384,384]{1,0:T(8,128)(2,1)S(1)}, bf16[384,384]{1,0:T(8,128)(2,1)S(1)}, u32[]{:S(2)}, u32[]{:S(2)}) collective-permute-start(bf16[384,384]{1,0:T(8,128)(2,1)S(1)} %collective-permute-done.refs_2_), channel_id=1, source_target_pairs={{0,4},{6,2},{8,12},{14,10},{1,5},{7,3},{9,13},{15,11},{16,20},{22,... | collective-permute-start | bytes 884744 | tf_op jit(solution)/shard_map/ppermute | solution.py:413
  58.1 3.1 %collective-permute-start.19 = (bf16[96,1536]{1,0:T(8,128)(2,1)}, bf16[96,1536]{1,0:T(8,128)(2,1)}, u32[]{:S(2)}, u32[]{:S(2)}) collective-permute-start(bf16[96,1536]{1,0:T(8,128)(2,1)} %constant_dynamic-slice_fusion), channel_id=1, source_target_pairs={{0,2},{2,0},{4,6},{6,4},{8,10},{10,8},{12,14},{14,12},{1,3},{3,1},... | collective-permute-start | bytes 884744 | tf_op jit(solution)/shard_map/ppermute | solution.py:406
  63.6 2.5 %attend.7 = (bf16[384,384]{1,0:T(8,128)(2,1)S(1)}, f32[8,384]{1,0:T(8,128)S(1)}) custom-call(s32[2]{0:T(128)S(1)} %pad_add_fusion.1.info, bf16[384,384]{1,0:T(8,128)(2,1)S(1)} %copy-done.13, bf16[384,384]{1,0:T(8,128)(2,1)S(1)} %get-tuple-element.32.refs_0_, bf16[384,384]{1,0:T(8,128)(2,1)S(1)} %get-tuple-element.30.refs_1_, ...), custom_call_target="tpu_custom_call" | custom-call | flops 528482304 | bytes 2359296 | tf_op jit(solution)/shard_map/attend/pallas_call | solution.py:187
  66.3 1.5 %collective-permute-start.27 = (bf16[96,1536]{1,0:T(8,128)(2,1)}, bf16[96,1536]{1,0:T(8,128)(2,1)S(1)}, u32[]{:S(2)}, u32[]{:S(2)}) collective-permute-start(bf16[96,1536]{1,0:T(8,128)(2,1)} %copy-done.6), channel_id=1, source_target_pairs={{0,16},{16,0},{1,17},{17,1},{2,18},{18,2},{3,19},{19,3},{4,20},{20... | collective-permute-start | bytes 884744 | tf_op jit(solution)/shard_map/ppermute | solution.py:409
  67.8 2.5 %collective-permute-start.23 = (bf16[96,1536]{1,0:T(8,128)(2,1)}, bf16[96,1536]{1,0:T(8,128)(2,1)S(1)}, u32[]{:S(2)}, u32[]{:S(2)}) collective-permute-start(bf16[96,1536]{1,0:T(8,128)(2,1)} %copy-done.6), channel_id=1, source_target_pairs={{0,2},{2,0},{4,6},{6,4},{8,10},{10,8},{12,14},{14,12},{1,3},{3,1},... | collective-permute-start | bytes 884744 | tf_op jit(solution)/shard_map/ppermute | solution.py:406
  70.3 2.4 %collective-permute-done.4.refs_5_ = bf16[384,384]{1,0:T(8,128)(2,1)S(1)} collective-permute-done((bf16[384,384]{1,0:T(8,128)(2,1)}, bf16[384,384]{1,0:T(8,128)(2,1)S(1)}, u32[]{:S(2)}, u32[]{:S(2)}) %collective-permute-start.4) | collective-permute-done | bytes 294944 | tf_op jit(solution)/shard_map/ppermute | solution.py:413
  72.8 2.4 %collective-permute-start.22 = (bf16[96,1536]{1,0:T(8,128)(2,1)}, bf16[96,1536]{1,0:T(8,128)(2,1)}, u32[]{:S(2)}, u32[]{:S(2)}) collective-permute-start(bf16[96,1536]{1,0:T(8,128)(2,1)} %copy-done.6), channel_id=1, source_target_pairs={{0,4},{2,6},{4,0},{6,2},{8,12},{10,14},{12,8},{14,10},{1,5},{3,7},... | collective-permute-start | bytes 884744 | tf_op jit(solution)/shard_map/ppermute | solution.py:406
  76.1 2.5 %attend.5 = (bf16[384,384]{1,0:T(8,128)(2,1)S(1)}, f32[8,384]{1,0:T(8,128)S(1)}) custom-call(s32[2]{0:T(128)S(1)} %pad_add_fusion.1.info, bf16[384,384]{1,0:T(8,128)(2,1)S(1)} %copy-done.9, bf16[384,384]{1,0:T(8,128)(2,1)S(1)} %get-tuple-element.33.refs_0_, bf16[384,384]{1,0:T(8,128)(2,1)S(1)} %get-tuple-element.31.refs_1_, ...), custom_call_target="tpu_custom_call" | custom-call | flops 528482304 | bytes 2359296 | tf_op jit(solution)/shard_map/attend/pallas_call | solution.py:187
  79.1 3.3 %collective-permute-start.14 = (bf16[384,384]{1,0:T(8,128)(2,1)S(1)}, bf16[384,384]{1,0:T(8,128)(2,1)S(1)}, u32[]{:S(2)}, u32[]{:S(2)}) collective-permute-start(bf16[384,384]{1,0:T(8,128)(2,1)S(1)} %get-tuple-element.25), channel_id=1, source_target_pairs={{0,8},{2,10},{4,12},{6,14},{8,0},{10,2},{12,4},{14,6},{1,9},{3,11}... | collective-permute-start | bytes 884744 | tf_op jit(solution)/shard_map/ppermute | solution.py:406
  83.1 2.9 %collective-permute-start.15 = (f32[8,384]{1,0:T(8,128)S(1)}, f32[8,384]{1,0:T(8,128)S(1)}, u32[]{:S(2)}, u32[]{:S(2)}) collective-permute-start(f32[8,384]{1,0:T(8,128)S(1)} %get-tuple-element.26), channel_id=1, source_target_pairs={{0,8},{2,10},{4,12},{6,14},{8,0},{10,2},{12,4},{14,6},{1,9},{3,11}... | collective-permute-start | bytes 36872 | tf_op jit(solution)/shard_map/ppermute | solution.py:406
  86.0 1.4 collective-permute-start.7
  87.5 1.5 %collective-permute-start.26 = (bf16[96,1536]{1,0:T(8,128)(2,1)}, bf16[96,1536]{1,0:T(8,128)(2,1)S(1)}, u32[]{:S(2)}, u32[]{:S(2)}) collective-permute-start(bf16[96,1536]{1,0:T(8,128)(2,1)} %collective-permute-done.19.rest_2_), channel_id=1, source_target_pairs={{0,16},{16,0},{1,17},{17,1},{2,18},{18,2},{3,19},{19,3},{4,20},{20... | collective-permute-start | bytes 884744 | tf_op jit(solution)/shard_map/ppermute | solution.py:409
  88.9 18.1 %collective-permute-done.15.got_logs = f32[8,384]{1,0:T(8,128)S(1)} collective-permute-done((f32[8,384]{1,0:T(8,128)S(1)}, f32[8,384]{1,0:T(8,128)S(1)}, u32[]{:S(2)}, u32[]{:S(2)}) %collective-permute-start.15) | collective-permute-done | bytes 12320 | tf_op jit(solution)/shard_map/ppermute | solution.py:406
  107.1 1.5 %collective-permute-start.25 = (bf16[96,1536]{1,0:T(8,128)(2,1)}, bf16[96,1536]{1,0:T(8,128)(2,1)}, u32[]{:S(2)}, u32[]{:S(2)}) collective-permute-start(bf16[96,1536]{1,0:T(8,128)(2,1)} %collective-permute-done.18.rest_1_), channel_id=1, source_target_pairs={{0,16},{16,0},{1,17},{17,1},{2,18},{18,2},{3,19},{19,3},{4,20},{20... | collective-permute-start | bytes 884744 | tf_op jit(solution)/shard_map/ppermute | solution.py:409
  109.2 1.4 collective-permute-start.24
  111.2 2.5 %attend.6 = (f32[384,384]{1,0:T(8,128)S(1)}, f32[384,128]{1,0:T(8,128)S(1)}) custom-call(s32[2]{0:T(128)S(1)} %pad_add_fusion.1.info, bf16[384,384]{1,0:T(8,128)(2,1)S(1)} %copy-done.4, bf16[384,384]{1,0:T(8,128)(2,1)S(1)} %get-tuple-element.32.refs_0_, bf16[384,384]{1,0:T(8,128)(2,1)S(1)} %get-tuple-element.30.refs_1_, ...), custom_call_target="tpu_custom_call" | custom-call | flops 528482304 | bytes 2359296 | tf_op jit(solution)/shard_map/attend/pallas_call | solution.py:187
  113.7 2.5 %attend.4 = (f32[384,384]{1,0:T(8,128)S(1)}, f32[384,128]{1,0:T(8,128)S(1)}) custom-call(s32[2]{0:T(128)S(1)} %pad_add_fusion.1.info, bf16[384,384]{1,0:T(8,128)(2,1)S(1)} %copy-done.2, bf16[384,384]{1,0:T(8,128)(2,1)S(1)} %get-tuple-element.33.refs_0_, bf16[384,384]{1,0:T(8,128)(2,1)S(1)} %get-tuple-element.31.refs_1_, ...), custom_call_target="tpu_custom_call" | custom-call | flops 528482304 | bytes 2359296 | tf_op jit(solution)/shard_map/attend/pallas_call | solution.py:187
  118.0 1.5 %collective-permute-start.28 = (bf16[96,1536]{1,0:T(8,128)(2,1)}, bf16[96,1536]{1,0:T(8,128)(2,1)S(1)}, u32[]{:S(2)}, u32[]{:S(2)}) collective-permute-start(bf16[96,1536]{1,0:T(8,128)(2,1)} %collective-permute-done.22.rest_5_), channel_id=1, source_target_pairs={{0,16},{16,0},{1,17},{17,1},{2,18},{18,2},{3,19},{19,3},{4,20},{20... | collective-permute-start | bytes 884744 | tf_op jit(solution)/shard_map/ppermute | solution.py:409
  122.9 5.5 %collective-permute-done.28.rest_11_ = bf16[96,1536]{1,0:T(8,128)(2,1)S(1)} collective-permute-done((bf16[96,1536]{1,0:T(8,128)(2,1)}, bf16[96,1536]{1,0:T(8,128)(2,1)S(1)}, u32[]{:S(2)}, u32[]{:S(2)}) %collective-permute-start.28) | collective-permute-done | bytes 294944 | tf_op jit(solution)/shard_map/ppermute | solution.py:409
  132.3 2.3 %stage.1.staged = bf16[1536,1536]{1,0:T(8,128)(2,1)S(1)} custom-call(s32[3]{0:T(128)S(1)} %pad_add_fusion.info, bf16[192,1536]{1,0:T(8,128)(2,1)S(1)} %copy-done, bf16[96,1536]{1,0:T(8,128)(2,1)} %collective-permute-done.18.rest_1_, bf16[96,1536]{1,0:T(8,128)(2,1)} %collective-permute-done.19.rest_2_, bf16[96,1536]{1,0:T(8,128)(2,1)S(1)} %copy-done.19, ...), custom_call_target="tpu_custom_call" | custom-call | bytes 9437184 | tf_op jit(solution)/shard_map/stage/pallas_call | solution.py:256
  134.7 4.7 %project.1 = (f32[384,1536]{1,0:T(8,128)S(1)}, bf16[384,1536]{1,0:T(8,128)(2,1)}, f32[384,128]{1,0:T(8,128)S(1)}, bf16[1536,1536]{1,0:T(8,128)(2,1)S(1)}) custom-call(s32[3]{0:T(128)S(1)} %pad_add_fusion.info, bf16[384,384]{1,0:T(8,128)(2,1)S(1)} %merge.2.a_low, bf16[384,384]{1,0:T(8,128)(2,1)S(1)} %merge.3.a_high, ...), custom_call_target="tpu_custom_call", output_to_operand_aliasing={{3}: (6, {})} | custom-call | flops 1811939328 | bytes 9437184 | tf_op jit(solution)/shard_map/project/pallas_call | solution.py:321
  139.5 1.4 collective-permute-done.32.other
  140.9 1.9 %normalize.1 = bf16[384,1536]{1,0:T(8,128)(2,1)} custom-call(s32[3]{0:T(128)S(1)} %pad_add_fusion.info, f32[384,1536]{1,0:T(8,128)S(1)} %get-tuple-element.27.mixed, f32[384,128]{1,0:T(8,128)S(1)} %get-tuple-element.28.mine, f32[384,128]{1,0:T(8,128)S(1)} %collective-permute-done.32.other, f32[1,3072]{1,0:T(1,128)S(1)} %bitcast.7, f32[1,3072]{1,0:T(1,128)S(1)} %bitcast.8), custom_call_target="tpu_custom_call" | custom-call | flops 3538944 | bytes 3538944 | tf_op jit(solution)/shard_map/normalize/pallas_call | solution.py:379
  (100 shorter events, 24.7 us)
Async XLA Ops:
  1.7 39.8 %collective-permute-start.5 = (bf16[384,384]{1,0:T(8,128)(2,1)S(1)}, bf16[384,384]{1,0:T(8,128)(2,1)S(1)}, u32[]{:S(2)}, u32[]{:S(2)}) collective-permute-start(bf16[384,384]{1,0:T(8,128)(2,1)S(1)} %slice.18.query), channel_id=1, source_target_pairs={{0,8},{2,10},{4,12},{6,14},{8,0},{10,2},{12,4},{14,6},{1,9},{3,11}... | collective-permute-start | bytes 884744 | tf_op jit(solution)/shard_map/ppermute | solution.py:406
  6.8 32.1 %collective-permute-start.13 = (bf16[384,384]{1,0:T(8,128)(2,1)S(1)}, bf16[384,384]{1,0:T(8,128)(2,1)S(1)}, u32[]{:S(2)}, u32[]{:S(2)}) collective-permute-start(bf16[384,384]{1,0:T(8,128)(2,1)S(1)} %slice.21.query), channel_id=1, source_target_pairs={{0,8},{2,10},{4,12},{6,14},{8,0},{10,2},{12,4},{14,6},{1,9},{3,11}... | collective-permute-start | bytes 884744 | tf_op jit(solution)/shard_map/ppermute | solution.py:406
  8.6 35.8 %collective-permute-start.21 = (bf16[96,1536]{1,0:T(8,128)(2,1)}, bf16[96,1536]{1,0:T(8,128)(2,1)S(1)}, u32[]{:S(2)}, u32[]{:S(2)}) collective-permute-start(bf16[96,1536]{1,0:T(8,128)(2,1)} %constant_dynamic-slice_fusion), channel_id=1, source_target_pairs={{0,8},{2,10},{4,12},{6,14},{8,0},{10,2},{12,4},{14,6},{1,9},{3,11}... | collective-permute-start | bytes 884744 | tf_op jit(solution)/shard_map/ppermute | solution.py:406
  12.6 33.1 %collective-permute-start.8 = (bf16[384,384]{1,0:T(8,128)(2,1)S(1)}, bf16[384,384]{1,0:T(8,128)(2,1)S(1)}, u32[]{:S(2)}, u32[]{:S(2)}) collective-permute-start(bf16[384,384]{1,0:T(8,128)(2,1)S(1)} %get-tuple-element.32.refs_0_), channel_id=1, source_target_pairs={{0,2},{2,0},{4,6},{6,4},{8,10},{10,8},{12,14},{14,12},{1,3},{3,1},... | collective-permute-start | bytes 884744 | tf_op jit(solution)/shard_map/ppermute | solution.py:406
  14.3 36.7 %collective-permute-start.11 = (bf16[384,384]{1,0:T(8,128)(2,1)S(1)}, bf16[384,384]{1,0:T(8,128)(2,1)S(1)}, u32[]{:S(2)}, u32[]{:S(2)}) collective-permute-start(bf16[384,384]{1,0:T(8,128)(2,1)S(1)} %get-tuple-element.30.refs_1_), channel_id=1, source_target_pairs={{2,6},{4,0},{10,14},{12,8},{3,7},{5,1},{11,15},{13,9},{18,22},{20,... | collective-permute-start | bytes 884744 | tf_op jit(solution)/shard_map/ppermute | solution.py:413
  39.7 13.0 %collective-permute-start = (bf16[384,384]{1,0:T(8,128)(2,1)S(1)}, bf16[384,384]{1,0:T(8,128)(2,1)S(1)}, u32[]{:S(2)}, u32[]{:S(2)}) collective-permute-start(bf16[384,384]{1,0:T(8,128)(2,1)S(1)} %get-tuple-element.33.refs_0_), channel_id=1, source_target_pairs={{0,2},{2,0},{4,6},{6,4},{8,10},{10,8},{12,14},{14,12},{1,3},{3,1},... | collective-permute-start | bytes 884744 | tf_op jit(solution)/shard_map/ppermute | solution.py:406
  42.2 11.1 %collective-permute-start.9 = (bf16[384,384]{1,0:T(8,128)(2,1)S(1)}, bf16[384,384]{1,0:T(8,128)(2,1)S(1)}, u32[]{:S(2)}, u32[]{:S(2)}) collective-permute-start(bf16[384,384]{1,0:T(8,128)(2,1)S(1)} %get-tuple-element.30.refs_1_), channel_id=1, source_target_pairs={{0,2},{2,0},{4,6},{6,4},{8,10},{10,8},{12,14},{14,12},{1,3},{3,1},... | collective-permute-start | bytes 884744 | tf_op jit(solution)/shard_map/ppermute | solution.py:406
  44.4 12.3 %collective-permute-start.3 = (bf16[384,384]{1,0:T(8,128)(2,1)S(1)}, bf16[384,384]{1,0:T(8,128)(2,1)}, u32[]{:S(2)}, u32[]{:S(2)}) collective-permute-start(bf16[384,384]{1,0:T(8,128)(2,1)S(1)} %get-tuple-element.31.refs_1_), channel_id=1, source_target_pairs={{2,6},{4,0},{10,14},{12,8},{3,7},{5,1},{11,15},{13,9},{18,22},{20,... | collective-permute-start | bytes 884744 | tf_op jit(solution)/shard_map/ppermute | solution.py:413
  45.7 12.3 %collective-permute-start.10 = (bf16[384,384]{1,0:T(8,128)(2,1)S(1)}, bf16[384,384]{1,0:T(8,128)(2,1)S(1)}, u32[]{:S(2)}, u32[]{:S(2)}) collective-permute-start(bf16[384,384]{1,0:T(8,128)(2,1)S(1)} %collective-permute-done.8.refs_2_), channel_id=1, source_target_pairs={{0,4},{6,2},{8,12},{14,10},{1,5},{7,3},{9,13},{15,11},{16,20},{22,... | collective-permute-start | bytes 884744 | tf_op jit(solution)/shard_map/ppermute | solution.py:413
  51.0 10.2 %collective-permute-start.12 = (bf16[384,384]{1,0:T(8,128)(2,1)S(1)}, bf16[384,384]{1,0:T(8,128)(2,1)S(1)}, u32[]{:S(2)}, u32[]{:S(2)}) collective-permute-start(bf16[384,384]{1,0:T(8,128)(2,1)S(1)} %collective-permute-done.11), channel_id=1, source_target_pairs={{0,2},{6,4},{8,10},{14,12},{1,3},{7,5},{9,11},{15,13},{16,18},{22,... | collective-permute-start | bytes 884744 | tf_op jit(solution)/shard_map/ppermute | solution.py:413
  52.7 13.7 %collective-permute-start.1 = (bf16[384,384]{1,0:T(8,128)(2,1)S(1)}, bf16[384,384]{1,0:T(8,128)(2,1)S(1)}, u32[]{:S(2)}, u32[]{:S(2)}) collective-permute-start(bf16[384,384]{1,0:T(8,128)(2,1)S(1)} %get-tuple-element.31.refs_1_), channel_id=1, source_target_pairs={{0,2},{2,0},{4,6},{6,4},{8,10},{10,8},{12,14},{14,12},{1,3},{3,1},... | collective-permute-start | bytes 884744 | tf_op jit(solution)/shard_map/ppermute | solution.py:406
  53.3 14.5 %collective-permute-start.2 = (bf16[384,384]{1,0:T(8,128)(2,1)S(1)}, bf16[384,384]{1,0:T(8,128)(2,1)S(1)}, u32[]{:S(2)}, u32[]{:S(2)}) collective-permute-start(bf16[384,384]{1,0:T(8,128)(2,1)S(1)} %collective-permute-done.refs_2_), channel_id=1, source_target_pairs={{0,4},{6,2},{8,12},{14,10},{1,5},{7,3},{9,13},{15,11},{16,20},{22,... | collective-permute-start | bytes 884744 | tf_op jit(solution)/shard_map/ppermute | solution.py:413
  56.7 16.0 %collective-permute-start.4 = (bf16[384,384]{1,0:T(8,128)(2,1)}, bf16[384,384]{1,0:T(8,128)(2,1)S(1)}, u32[]{:S(2)}, u32[]{:S(2)}) collective-permute-start(bf16[384,384]{1,0:T(8,128)(2,1)} %collective-permute-done.3), channel_id=1, source_target_pairs={{0,2},{6,4},{8,10},{14,12},{1,3},{7,5},{9,11},{15,13},{16,18},{22,... | collective-permute-start | bytes 884744 | tf_op jit(solution)/shard_map/ppermute | solution.py:413
  58.1 21.0 %collective-permute-start.19 = (bf16[96,1536]{1,0:T(8,128)(2,1)}, bf16[96,1536]{1,0:T(8,128)(2,1)}, u32[]{:S(2)}, u32[]{:S(2)}) collective-permute-start(bf16[96,1536]{1,0:T(8,128)(2,1)} %constant_dynamic-slice_fusion), channel_id=1, source_target_pairs={{0,2},{2,0},{4,6},{6,4},{8,10},{10,8},{12,14},{14,12},{1,3},{3,1},... | collective-permute-start | bytes 884744 | tf_op jit(solution)/shard_map/ppermute | solution.py:406
  61.2 21.2 %collective-permute-start.18 = (bf16[96,1536]{1,0:T(8,128)(2,1)}, bf16[96,1536]{1,0:T(8,128)(2,1)}, u32[]{:S(2)}, u32[]{:S(2)}) collective-permute-start(bf16[96,1536]{1,0:T(8,128)(2,1)} %constant_dynamic-slice_fusion), channel_id=1, source_target_pairs={{0,4},{2,6},{4,0},{6,2},{8,12},{10,14},{12,8},{14,10},{1,5},{3,7},... | collective-permute-start | bytes 884744 | tf_op jit(solution)/shard_map/ppermute | solution.py:406
  66.3 16.0 %collective-permute-start.27 = (bf16[96,1536]{1,0:T(8,128)(2,1)}, bf16[96,1536]{1,0:T(8,128)(2,1)S(1)}, u32[]{:S(2)}, u32[]{:S(2)}) collective-permute-start(bf16[96,1536]{1,0:T(8,128)(2,1)} %copy-done.6), channel_id=1, source_target_pairs={{0,16},{16,0},{1,17},{17,1},{2,18},{18,2},{3,19},{19,3},{4,20},{20... | collective-permute-start | bytes 884744 | tf_op jit(solution)/shard_map/ppermute | solution.py:409
  67.8 18.2 %collective-permute-start.23 = (bf16[96,1536]{1,0:T(8,128)(2,1)}, bf16[96,1536]{1,0:T(8,128)(2,1)S(1)}, u32[]{:S(2)}, u32[]{:S(2)}) collective-permute-start(bf16[96,1536]{1,0:T(8,128)(2,1)} %copy-done.6), channel_id=1, source_target_pairs={{0,2},{2,0},{4,6},{6,4},{8,10},{10,8},{12,14},{14,12},{1,3},{3,1},... | collective-permute-start | bytes 884744 | tf_op jit(solution)/shard_map/ppermute | solution.py:406
  72.8 14.7 %collective-permute-start.22 = (bf16[96,1536]{1,0:T(8,128)(2,1)}, bf16[96,1536]{1,0:T(8,128)(2,1)}, u32[]{:S(2)}, u32[]{:S(2)}) collective-permute-start(bf16[96,1536]{1,0:T(8,128)(2,1)} %copy-done.6), channel_id=1, source_target_pairs={{0,4},{2,6},{4,0},{6,2},{8,12},{10,14},{12,8},{14,10},{1,5},{3,7},... | collective-permute-start | bytes 884744 | tf_op jit(solution)/shard_map/ppermute | solution.py:406
  79.1 30.2 %collective-permute-start.14 = (bf16[384,384]{1,0:T(8,128)(2,1)S(1)}, bf16[384,384]{1,0:T(8,128)(2,1)S(1)}, u32[]{:S(2)}, u32[]{:S(2)}) collective-permute-start(bf16[384,384]{1,0:T(8,128)(2,1)S(1)} %get-tuple-element.25), channel_id=1, source_target_pairs={{0,8},{2,10},{4,12},{6,14},{8,0},{10,2},{12,4},{14,6},{1,9},{3,11}... | collective-permute-start | bytes 884744 | tf_op jit(solution)/shard_map/ppermute | solution.py:406
  82.4 28.3 %collective-permute-start.6 = (bf16[384,384]{1,0:T(8,128)(2,1)S(1)}, bf16[384,384]{1,0:T(8,128)(2,1)S(1)}, u32[]{:S(2)}, u32[]{:S(2)}) collective-permute-start(bf16[384,384]{1,0:T(8,128)(2,1)S(1)} %get-tuple-element.20), channel_id=1, source_target_pairs={{0,8},{2,10},{4,12},{6,14},{8,0},{10,2},{12,4},{14,6},{1,9},{3,11}... | collective-permute-start | bytes 884744 | tf_op jit(solution)/shard_map/ppermute | solution.py:406
  83.1 23.9 %collective-permute-start.15 = (f32[8,384]{1,0:T(8,128)S(1)}, f32[8,384]{1,0:T(8,128)S(1)}, u32[]{:S(2)}, u32[]{:S(2)}) collective-permute-start(f32[8,384]{1,0:T(8,128)S(1)} %get-tuple-element.26), channel_id=1, source_target_pairs={{0,8},{2,10},{4,12},{6,14},{8,0},{10,2},{12,4},{14,6},{1,9},{3,11}... | collective-permute-start | bytes 36872 | tf_op jit(solution)/shard_map/ppermute | solution.py:406
  86.0 22.5 %collective-permute-start.7 = (f32[8,384]{1,0:T(8,128)S(1)}, f32[8,384]{1,0:T(8,128)S(1)}, u32[]{:S(2)}, u32[]{:S(2)}) collective-permute-start(f32[8,384]{1,0:T(8,128)S(1)} %get-tuple-element.21), channel_id=1, source_target_pairs={{0,8},{2,10},{4,12},{6,14},{8,0},{10,2},{12,4},{14,6},{1,9},{3,11}... | collective-permute-start | bytes 36872 | tf_op jit(solution)/shard_map/ppermute | solution.py:406
  87.5 29.8 %collective-permute-start.26 = (bf16[96,1536]{1,0:T(8,128)(2,1)}, bf16[96,1536]{1,0:T(8,128)(2,1)S(1)}, u32[]{:S(2)}, u32[]{:S(2)}) collective-permute-start(bf16[96,1536]{1,0:T(8,128)(2,1)} %collective-permute-done.19.rest_2_), channel_id=1, source_target_pairs={{0,16},{16,0},{1,17},{17,1},{2,18},{18,2},{3,19},{19,3},{4,20},{20... | collective-permute-start | bytes 884744 | tf_op jit(solution)/shard_map/ppermute | solution.py:409
  107.1 12.4 %collective-permute-start.25 = (bf16[96,1536]{1,0:T(8,128)(2,1)}, bf16[96,1536]{1,0:T(8,128)(2,1)}, u32[]{:S(2)}, u32[]{:S(2)}) collective-permute-start(bf16[96,1536]{1,0:T(8,128)(2,1)} %collective-permute-done.18.rest_1_), channel_id=1, source_target_pairs={{0,16},{16,0},{1,17},{17,1},{2,18},{18,2},{3,19},{19,3},{4,20},{20... | collective-permute-start | bytes 884744 | tf_op jit(solution)/shard_map/ppermute | solution.py:409
  108.6 11.6 %collective-permute-start.20 = (bf16[96,1536]{1,0:T(8,128)(2,1)}, bf16[96,1536]{1,0:T(8,128)(2,1)S(1)}, u32[]{:S(2)}, u32[]{:S(2)}) collective-permute-start(bf16[96,1536]{1,0:T(8,128)(2,1)} %collective-permute-done.19.rest_2_), channel_id=1, source_target_pairs={{0,4},{2,6},{4,0},{6,2},{8,12},{10,14},{12,8},{14,10},{1,5},{3,7},... | collective-permute-start | bytes 884744 | tf_op jit(solution)/shard_map/ppermute | solution.py:406
  109.2 11.6 %collective-permute-start.24 = (bf16[96,1536]{1,0:T(8,128)(2,1)}, bf16[96,1536]{1,0:T(8,128)(2,1)}, u32[]{:S(2)}, u32[]{:S(2)}) collective-permute-start(bf16[96,1536]{1,0:T(8,128)(2,1)} %collective-permute-done.22.rest_5_), channel_id=1, source_target_pairs={{0,2},{2,0},{4,6},{6,4},{8,10},{10,8},{12,14},{14,12},{1,3},{3,1},... | collective-permute-start | bytes 884744 | tf_op jit(solution)/shard_map/ppermute | solution.py:406
  110.6 11.5 %collective-permute-start.29 = (bf16[96,1536]{1,0:T(8,128)(2,1)S(1)}, bf16[96,1536]{1,0:T(8,128)(2,1)S(1)}, u32[]{:S(2)}, u32[]{:S(2)}) collective-permute-start(bf16[96,1536]{1,0:T(8,128)(2,1)S(1)} %collective-permute-done.23.rest_6_), channel_id=1, source_target_pairs={{0,16},{16,0},{1,17},{17,1},{2,18},{18,2},{3,19},{19,3},{4,20},{20... | collective-permute-start | bytes 884744 | tf_op jit(solution)/shard_map/ppermute | solution.py:409
  118.0 10.5 %collective-permute-start.28 = (bf16[96,1536]{1,0:T(8,128)(2,1)}, bf16[96,1536]{1,0:T(8,128)(2,1)S(1)}, u32[]{:S(2)}, u32[]{:S(2)}) collective-permute-start(bf16[96,1536]{1,0:T(8,128)(2,1)} %collective-permute-done.22.rest_5_), channel_id=1, source_target_pairs={{0,16},{16,0},{1,17},{17,1},{2,18},{18,2},{3,19},{19,3},{4,20},{20... | collective-permute-start | bytes 884744 | tf_op jit(solution)/shard_map/ppermute | solution.py:409
  119.5 15.2 %collective-permute-start.30 = (bf16[96,1536]{1,0:T(8,128)(2,1)}, bf16[96,1536]{1,0:T(8,128)(2,1)S(1)}, u32[]{:S(2)}, u32[]{:S(2)}) collective-permute-start(bf16[96,1536]{1,0:T(8,128)(2,1)} %collective-permute-done.25.rest_8_), channel_id=1, source_target_pairs={{0,2},{2,0},{4,6},{6,4},{8,10},{10,8},{12,14},{14,12},{1,3},{3,1},... | collective-permute-start | bytes 884744 | tf_op jit(solution)/shard_map/ppermute | solution.py:406
  120.8 13.9 %collective-permute-start.17 = (bf16[384,384]{1,0:T(8,128)(2,1)S(1)}, bf16[384,384]{1,0:T(8,128)(2,1)S(1)}, u32[]{:S(2)}, u32[]{:S(2)}) collective-permute-start(bf16[384,384]{1,0:T(8,128)(2,1)S(1)} %merge.3.a_high), channel_id=1, source_target_pairs={{0,1},{1,0},{2,3},{3,2},{4,5},{5,4},{6,7},{7,6},{8,9},{9,8},{10,11... | collective-permute-start | bytes 884744 | tf_op jit(solution)/shard_map/ppermute | solution.py:409
  120.9 13.8 %collective-permute-start.31 = (bf16[96,1536]{1,0:T(8,128)(2,1)}, bf16[96,1536]{1,0:T(8,128)(2,1)S(1)}, u32[]{:S(2)}, u32[]{:S(2)}) collective-permute-start(bf16[96,1536]{1,0:T(8,128)(2,1)} %collective-permute-done.24.rest_7_), channel_id=1, source_target_pairs={{0,16},{16,0},{1,17},{17,1},{2,18},{18,2},{3,19},{19,3},{4,20},{20... | collective-permute-start | bytes 884744 | tf_op jit(solution)/shard_map/ppermute | solution.py:409
  122.8 11.9 %collective-permute-start.16 = (bf16[384,384]{1,0:T(8,128)(2,1)S(1)}, bf16[384,384]{1,0:T(8,128)(2,1)}, u32[]{:S(2)}, u32[]{:S(2)}) collective-permute-start(bf16[384,384]{1,0:T(8,128)(2,1)S(1)} %merge.2.a_low), channel_id=1, source_target_pairs={{0,1},{1,0},{2,3},{3,2},{4,5},{5,4},{6,7},{7,6},{8,9},{9,8},{10,11... | collective-permute-start | bytes 884744 | tf_op jit(solution)/shard_map/ppermute | solution.py:409
  (26 other events, 309.5 us)
